TPU v7x, 256 devices: a whole 4x4x8 slice. The times are simulated.
256 devices in a mesh: seq: 64 (over z, y, x_lo), mp: 4 (over x_hi, core).
Axes of the slice: x: 4 (x_hi: 2, x_lo: 2; x = x_hi * 2 + x_lo), y: 4, z: 8, core: 2. Of those that a mesh axis runs over, the one named last changes fastest.
Arguments:
- inputs: bfloat16 [32, 4, 2048], replicated, may hold values from -3 to 3
- w_qkv: bfloat16 [3, 2048, 2048], P(None, None, 'mp'), may hold values from -0.125 to 0.125
- w_out: bfloat16 [2048, 2048], P('mp'), may hold values from -0.125 to 0.125
- w_gate_up: bfloat16 [2, 2048, 4096], P(None, None, 'mp'), may hold values from -0.125 to 0.125
- w_down: bfloat16 [4096, 2048], P('mp'), may hold values from -0.09375 to 0.09375
- cache_keys: bfloat16 [32, 8192, 2048], P(None, 'seq', 'mp'), may hold values from -256 to 256
- cache_values: bfloat16 [32, 8192, 2048], P(None, 'seq', 'mp'), may hold values from -6 to 6
- lengths: int32 [32], replicated, may hold values from 1 to 8192, as said below
Outputs:
- hidden: bfloat16 [32, 4, 2048], P(None, None, 'mp')
- queries: bfloat16 [32, 4, 2048], P(None, None, 'mp')
- new_keys: bfloat16 [32, 4, 2048], P(None, None, 'mp')
- new_values: bfloat16 [32, 4, 2048], P(None, None, 'mp')
Inputs may be any that keep to these rules, and one draw needn't show every extreme that they name: `lengths`: half of the 32 requests hold 1 to 512 cached positions, the others 8192 - 8192 // 8 to 8192; one request holds exactly 8192.
All inputs are finite; a program needn't handle non-finite values.
Results may differ from a plain program's by a relative error of at most 0.015.
The roundings to bfloat16 on the way count: a program that leaves them out, or rounds other values in their place, can miss the bound.
Values may be sent and summed in bfloat16 or wider, within the bound.
No kernel may reach another device: no remote copies, remote signals or barrier semaphores. Data moves between devices by JAX's collectives and lax.ppermute only.
A program may use at most 128 MiB of HBM per device.

v0:
```python
import jax
import jax.numpy as jnp
from jax import lax
from jax.sharding import PartitionSpec as P

DH = 128


neg_fill = -1e30
norm_eps = 1e-05
rope_base = 10000.0


def merged_2(part, axis, combine):
    gathered = jax.tree.map(lambda a: lax.all_gather(a, axis), part)

    def take(source):
        return jax.tree.map(lambda a: lax.dynamic_index_in_dim(a, source, 0, False), gathered)

    return lax.fori_loop(
        1, lax.axis_size(axis), lambda source, state: combine(state, take(source)), take(0)
    )


def layer_norm(values):
    average = jnp.mean(values, axis=-1, keepdims=True)
    centred = values - average
    variance = jnp.mean(centred * centred, axis=-1, keepdims=True)
    return centred * lax.rsqrt(variance + norm_eps)


def rotate(values, positions):
    head_dim = values.shape[-1]
    half_dim = head_dim // 2
    inverse = rope_base ** (-2.0 * jnp.arange(half_dim, dtype=jnp.float32) / head_dim)
    angles = positions.astype(jnp.float32)[..., None] * inverse
    angles = jnp.concatenate([angles, angles], axis=-1)[..., None, :]
    turned = jnp.concatenate([-values[..., half_dim:], values[..., :half_dim]], axis=-1)
    return values * jnp.cos(angles) + turned * jnp.sin(angles)


def project(inputs, w_qkv, lengths):
    batch_rows, step_count, model_width = inputs.shape
    normed = layer_norm(inputs.astype(jnp.float32)).astype(jnp.bfloat16)
    flat_rows = normed.reshape(batch_rows * step_count, model_width)
    triple = jnp.einsum("rd,jdk->jrk", flat_rows, w_qkv, preferred_element_type=jnp.float32)
    triple = triple.reshape(3, batch_rows, step_count, -1, DH)
    positions = lengths[:, None] + jnp.arange(step_count, dtype=jnp.int32)[None, :]
    queries = rotate(triple[0], positions).astype(jnp.bfloat16)
    new_keys = rotate(triple[1], positions).astype(jnp.bfloat16)
    return (queries, new_keys, triple[2].astype(jnp.bfloat16))


def attend(queries, keys_in, values_in, live):
    head_dim = queries.shape[-1]
    scores = jnp.einsum(
        "bthd,bkhd->bthk", queries, keys_in, preferred_element_type=jnp.float32
    ) * head_dim ** (-0.5)
    highest = jnp.max(jnp.where(live, scores, neg_fill), axis=-1)
    weights = jnp.where(live, jnp.exp(scores - highest[..., None]), 0.0)
    totals = jnp.sum(weights, axis=-1)
    summed = jnp.einsum(
        "bthk,bkhd->bthd",
        weights.astype(jnp.bfloat16),
        values_in,
        preferred_element_type=jnp.float32,
    )
    return (highest, totals, summed.reshape(summed.shape[0], summed.shape[1], -1))


def widen(factor, head_dim):
    return jnp.repeat(factor, head_dim, axis=-1)


def join(earlier, later):
    highest = jnp.maximum(earlier[0], later[0])
    lead_scale = jnp.exp(earlier[0] - highest)
    tail_scale = jnp.exp(later[0] - highest)
    head_dim = earlier[2].shape[-1] // earlier[0].shape[-1]
    totals = earlier[1] * lead_scale + later[1] * tail_scale
    summed = earlier[2] * widen(lead_scale, head_dim) + later[2] * widen(tail_scale, head_dim)
    return (highest, totals, summed)


def per_device(inputs, w_qkv, w_out, w_gate_up, w_down, cache_keys, cache_values, lengths):
    batch_rows, step_count, model_width = inputs.shape
    block_len = cache_keys.shape[1]
    seq_index = lax.axis_index("seq")
    col_count = model_width // lax.axis_size("mp")
    col_first = lax.axis_index("mp") * col_count
    queries, new_keys, new_values = project(inputs, w_qkv, lengths)
    head_count = queries.shape[2]
    held_keys = cache_keys.reshape(batch_rows, block_len, head_count, DH)
    held_values = cache_values.reshape(batch_rows, block_len, head_count, DH)
    places = seq_index * block_len + jnp.arange(block_len, dtype=jnp.int32)
    cache_live = (places[None, :] < lengths[:, None])[:, None, None, :]
    new_places = jnp.arange(step_count, dtype=jnp.int32)
    local_terms = attend(queries, held_keys, held_values, cache_live)
    step_ids = jnp.arange(step_count, dtype=jnp.int32)
    fresh_live = (new_places[None, :] <= step_ids[:, None])[None, :, None, :]
    fresh_terms = attend(queries, new_keys, new_values, fresh_live)
    combined = merged_2((local_terms[0], local_terms[1], local_terms[2]), "seq", join)
    merged = join(combined, fresh_terms)
    context = (merged[2] / widen(merged[1], DH)).astype(jnp.bfloat16)
    row_count = context.shape[0] * context.shape[1]
    flat_ctx = context.reshape(row_count, -1)
    attn_part = lax.psum(jnp.dot(flat_ctx, w_out, preferred_element_type=jnp.float32), "mp")
    middle = inputs.reshape(row_count, model_width).astype(jnp.float32) + attn_part
    normed = layer_norm(middle).astype(jnp.bfloat16)
    gate_up = jnp.einsum("rd,jdf->jrf", normed, w_gate_up, preferred_element_type=jnp.float32)
    active = (jax.nn.silu(gate_up[0]) * gate_up[1]).astype(jnp.bfloat16)
    down_part = jnp.dot(active, w_down, preferred_element_type=jnp.float32)
    middle_cols = lax.dynamic_slice_in_dim(middle, col_first, col_count, 1)
    down_cols = lax.dynamic_slice_in_dim(lax.psum(down_part, "mp"), col_first, col_count, 1)
    hidden = (
        (middle_cols + down_cols)
        .astype(jnp.bfloat16)
        .reshape(context.shape[0], context.shape[1], col_count)
    )
    head_width = head_count * DH
    return (
        hidden,
        queries.reshape(batch_rows, step_count, head_width),
        new_keys.reshape(batch_rows, step_count, head_width),
        new_values.reshape(batch_rows, step_count, head_width),
    )


def solution(mesh):
    placed = (
        P(),
        P(None, None, "mp"),
        P("mp", None),
        P(None, None, "mp"),
        P("mp", None),
        P(None, "seq", "mp"),
        P(None, "seq", "mp"),
        P(),
    )
    return jax.shard_map(
        per_device,
        mesh=mesh,
        in_specs=placed,
        out_specs=(
            P(None, None, "mp"),
            P(None, None, "mp"),
            P(None, None, "mp"),
            P(None, None, "mp"),
        ),
        check_vma=False,
    )
```

profile of v0, /device:TPU:4, one launch (start us, length us, event | category | flops | bytes accessed | tf_op | source)
XLA Modules:
  0.0 895.9 jit_solution(14104249272061127603)
XLA Ops:
  8.9 1.3 convert_reduce_fusion
  10.2 1.5 multiply_reduce_fusion.1
  12.4 1.4 multiply_convert_fusion.1
  14.8 4.0 convolution_bitcast_fusion.1
  19.4 1.1 squeeze.62
  21.4 1.2 copy.117
  22.6 1.0 slice_negate_fusion
  24.4 1.2 add_convert_fusion.2
  25.6 2.4 select_reduce_fusion
  28.7 1.2 fusion.16
  30.7 1.7 all_gather_reshape.3
  32.6 1.1 copy.121
  34.4 1.4 fusion.40
  37.1 1.4 fusion.38
  38.7 263.2 %all-gather.1 = f32[2048,4,4]{2,1,0:T(4,128)S(1)} all-gather(f32[32,4,4]{2,1,0:T(4,128)S(1)} %copy.122), channel_id=3, replica_groups=mesh['seq'=64,'mp'=4] {'seq'}, dimensions={0}, use_global_device_ids=true | all-gather | bytes 133120 | tf_op jit(solution)/shard_map/all_gather | solution.py:15
  302.0 1.9 copy-done.1
  304.0 4.7 copy.131
  308.7 246.8 %all-gather = f32[2048,4,4]{2,1,0:T(4,128)S(1)} all-gather(f32[32,4,4]{2,1,0:T(4,128)S(1)} %copy.121), channel_id=2, replica_groups=mesh['seq'=64,'mp'=4] {'seq'}, dimensions={0}, use_global_device_ids=true | all-gather | bytes 133120 | tf_op jit(solution)/shard_map/all_gather | solution.py:15
  555.5 1.9 copy-done.2
  557.5 4.7 copy.130
  562.3 22.0 %all-gather.4.cloned.1.call-done = f32[64,32,4,512]{3,1,2,0:T(8,128)} async-done(((f32[1,32,4,512]{3,1,2,0:T(8,128)}), f32[64,32,4,512]{3,1,2,0:T(8,128)}) %all-gather.4.cloned.1.call-update) | async-done | bytes 16777232 | tf_op jit(solution)/shard_map/all_gather | solution.py:15
  585.5 189.8 %while.19 = (s32[]{:T(128)}, f32[32,4,4]{0,2,1:T(4,128)S(1)}, f32[32,4,4]{0,2,1:T(4,128)S(1)}, f32[32,4,512]{2,1,0:T(4,128)S(1)}, f32[64,32,4,4]{1,3,2,0:T(4,128...) while((s32[]{:T(128)}, f32[32,4,4]{0,2,1:T(4,128)S(1)}, ...), condition=%wide.region_5.6_spmd, body=%wide.region_4.5_spmd.sunk | while | flops 199685 | bytes 3436687 | solution.py:20
  587.2 1.0 constant_dynamic-slice_fusion.2
  590.2 1.0 constant_dynamic-slice_fusion.2
  593.2 1.0 constant_dynamic-slice_fusion.2
  596.2 1.0 constant_dynamic-slice_fusion.2
  599.2 1.0 constant_dynamic-slice_fusion.2
  602.3 1.0 constant_dynamic-slice_fusion.2
  605.3 1.0 constant_dynamic-slice_fusion.2
  608.3 1.0 constant_dynamic-slice_fusion.2
  614.3 1.0 constant_dynamic-slice_fusion.2
  617.3 1.0 constant_dynamic-slice_fusion.2
  620.3 1.0 constant_dynamic-slice_fusion.2
  626.4 1.0 constant_dynamic-slice_fusion.2
  629.4 1.0 constant_dynamic-slice_fusion.2
  632.4 1.0 constant_dynamic-slice_fusion.2
  638.4 1.0 constant_dynamic-slice_fusion.2
  641.4 1.0 constant_dynamic-slice_fusion.2
  644.4 1.0 constant_dynamic-slice_fusion.2
  647.4 1.0 constant_dynamic-slice_fusion.2
  650.5 1.0 constant_dynamic-slice_fusion.2
  656.5 1.0 constant_dynamic-slice_fusion.2
  659.5 1.0 constant_dynamic-slice_fusion.2
  662.5 1.0 constant_dynamic-slice_fusion.2
  665.5 1.0 constant_dynamic-slice_fusion.2
  668.5 1.0 constant_dynamic-slice_fusion.2
  671.5 1.0 constant_dynamic-slice_fusion.2
  674.6 1.0 constant_dynamic-slice_fusion.2
  677.6 1.0 constant_dynamic-slice_fusion.2
  680.6 1.0 constant_dynamic-slice_fusion.2
  683.6 1.0 constant_dynamic-slice_fusion.2
  689.6 1.0 constant_dynamic-slice_fusion.2
  777.7 1.4 fusion.23
  779.1 1.5 fusion.63
  780.8 1.1 reshape.201
  782.0 46.7 %all-reduce.3.cloned.1.call-done = f32[128,2048]{1,0:T(8,128)} async-done(((f32[128,2048]{1,0:T(8,128)}), f32[128,2048]{1,0:T(8,128)}) %all-reduce.3.cloned.1.call-update) | async-done | bytes 1048592 | tf_op jit(solution)/shard_map/psum | solution.py:107
  828.7 1.7 fusion.59
  830.7 4.8 convolution_bitcast_fusion
  835.6 1.8 fusion.34
  838.1 1.7 squeeze.66
  839.8 1.7 squeeze.65
  841.5 2.4 fusion.33
  843.9 43.8 %all-reduce.5.cloned.1.call-done = f32[128,2048]{1,0:T(8,128)} async-done(((f32[128,2048]{1,0:T(8,128)}), f32[128,2048]{1,0:T(8,128)}) %all-reduce.5.cloned.1.call-update) | async-done | bytes 1048592 | tf_op jit(solution)/shard_map/psum | solution.py:114
  887.7 1.0 add_convert_fusion
  (616 shorter events, 172.5 us)
Async XLA Ops:
  7.2 772.0 %copy-start = (bf16[512,2048]{1,0:T(8,128)(2,1)S(1)}, bf16[512,2048]{1,0:T(8,128)(2,1)}, u32[]{:S(2)}) copy-start(bf16[512,2048]{1,0:T(8,128)(2,1)} %param.12) | copy-start | bytes 6291460
  7.2 577.1 %all-gather.4.cloned.1.call-start = ((), (), s32[]{:S(2)}) async-start(), calls=%async_computation | async-start | bytes 17039360 | tf_op jit(solution)/shard_map/all_gather | solution.py:15
  12.4 11.3 %copy-start.9 = (f32[32,4,128]{2,1,0:T(4,128)}, f32[32,4,128]{2,1,0:T(4,128)S(1)}, u32[]{:S(2)}) copy-start(f32[32,4,128]{2,1,0:T(4,128)S(1)} %get-tuple-element.244) | copy-start | bytes 196612
  12.4 11.3 %copy-start.10 = (f32[32,4,128]{2,1,0:T(4,128)}, f32[32,4,128]{2,1,0:T(4,128)S(1)}, u32[]{:S(2)}) copy-start(f32[32,4,128]{2,1,0:T(4,128)S(1)} %get-tuple-element.245) | copy-start | bytes 196612
  19.4 3.1 copy-start.6
  21.4 4.3 copy-start.14
  22.5 6.1 copy-start.15
  23.6 0.7 copy-start.7
  23.6 0.8 copy-start.8
  23.6 10.7 %copy-start.4 = (f32[32,4,4,64]{3,1,2,0:T(4,128)}, f32[32,4,4,64]{3,1,2,0:T(4,128)S(1)}, u32[]{:S(2)}) copy-start(f32[32,4,4,64]{3,1,2,0:T(4,128)S(1)} %get-tuple-element.238) | copy-start | bytes 393220
  25.6 4.3 copy-start.11
  28.0 0.6 copy-start.12
  28.0 1.9 copy-start.13
  32.5 796.2 %all-reduce.3.cloned.1.call-start = ((), (), s32[]{:S(2)}) async-start(), calls=%async_computation.1 | async-start | bytes 2097152 | tf_op jit(solution)/shard_map/psum | solution.py:107
  302.0 1.9 copy-start.1
  555.5 1.9 copy-start.2
  776.8 4.0 copy-start.3
  780.6 107.1 %all-reduce.5.cloned.1.call-start = ((), (), s32[]{:S(2)}) async-start(), calls=%async_computation.2 | async-start | bytes 2097152 | tf_op jit(solution)/shard_map/psum | solution.py:114
  830.7 4.9 copy-start.16
  835.5 6.0 copy-start.5
Sparse Core Ops, SparseCore 0:
  32.6 551.6 all-gather.3
  780.7 47.9 all-reduce.2
  837.5 50.1 all-reduce.4
where the time goes:
time: 906 us; the launch traced here: 896 us
  blocking collectives  510 us (56%)
  local copies, waits for them, and re-layouts  155 us (17%)
  waiting for transfers between devices  113 us (12%)
  other arithmetic  82.2 us (9%)
  matrix products  18.5 us (2%)
  between operations  14 us (2%)
    all_gather x2, blocking collectives, merged_2(): gathered = jax.tree.map(lambda a: lax.all_gather(a, axis), part)  510 us
    dynamic_slice x65, local copies, waits for them, and re-layouts, take(): lax.dynamic_index_in_dim(a, source, 0, False)  61.4 us
    add x64, other arithmetic, join(): totals = earlier[1] * lead_scale + later[1] * tail_scale  47.1 us
    psum x1, waiting for transfers between devices, per_device(): lax.psum(jnp.dot(flat_ctx, w_out, preferred_element_type=jnp.float32), 'mp')  46.7 us
    psum x1, waiting for transfers between devices, per_device(): lax.psum(down_part, 'mp')  43.8 us
    broadcast_in_dim x128, local copies, waits for them, and re-layouts, widen(): return jnp.repeat(factor, head_dim, axis=-1)  25.3 us
    all_gather x1, waiting for transfers between devices, merged_2(): gathered = jax.tree.map(lambda a: lax.all_gather(a, axis), part)  22 us
    reshape x128, local copies, waits for them, and re-layouts, widen(): return jnp.repeat(factor, head_dim, axis=-1)  20.7 us
  transfers between devices with their start and end apart: 3, of which 3 were waited for; matrix products, arithmetic and copies ran while one was open for 3% of the time, Pallas kernels for 0%

commit v1 on v0

v1 whole, which is shorter than its diff:
```python
import functools

import jax
import jax.numpy as jnp
import numpy as np
from jax import lax
from jax.experimental import pallas as pl
from jax.experimental.pallas import tpu as pltpu
from jax.sharding import PartitionSpec as P

DH = 128
NEG = -1e30
EPS = 1e-05
SCALE = DH ** (-0.5)
F32 = jnp.float32
BF16 = jnp.bfloat16


def norm_rows(x):
    centred = x - jnp.mean(x, axis=-1, keepdims=True)
    variance = jnp.mean(centred * centred, axis=-1, keepdims=True)
    return centred * lax.rsqrt(variance + EPS)


def split3(v):
    a = v.astype(BF16).astype(F32)
    rest = v - a
    b = rest.astype(BF16).astype(F32)
    return a, b, rest - b


def local_kernel(
    reqs, steps, block, width,
    len_ref, x_hbm, w_hbm, ck_hbm, cv_hbm, freq_ref,
    q_out, k_out, v_out, part_out, fresh_out,
    x_v, w_v, ck_v, cv_v, xs, q16, k16, v16, flat, sem_x, sem_w, sem_c,
):
    heads = width // DH
    rows = reqs * steps
    seq = lax.axis_index("seq")
    copy_x = pltpu.make_async_copy(x_hbm, x_v, sem_x)
    copy_x.start()
    copies_w = [pltpu.make_async_copy(w_hbm.at[j], w_v.at[j], sem_w.at[j]) for j in range(3)]
    copies_k = [
        pltpu.make_async_copy(ck_hbm.at[pl.ds(g, reqs // 2)], ck_v.at[pl.ds(g, reqs // 2)], sem_c.at[i])
        for i, g in enumerate((0, reqs // 2))
    ]
    copies_v = [
        pltpu.make_async_copy(cv_hbm.at[pl.ds(g, reqs // 2)], cv_v.at[pl.ds(g, reqs // 2)], sem_c.at[2 + i])
        for i, g in enumerate((0, reqs // 2))
    ]
    copies_w[0].start()
    copies_k[0].start()
    copies_v[0].start()
    copies_k[1].start()
    copies_v[1].start()
    copies_w[1].start()
    copies_w[2].start()

    row_ids = lax.broadcasted_iota(jnp.int32, (rows, DH), 0)
    for r in range(reqs):
        flat[pl.ds(r * steps, steps), :] = jnp.full((steps, DH), len_ref[r], jnp.int32).astype(F32)
    angles = (flat[...] + (row_ids % steps).astype(F32)) * freq_ref[0:1, :]
    lane = lax.broadcasted_iota(jnp.int32, (rows, DH), 1)
    cosine = jnp.cos(angles)
    sine = jnp.sin(angles)
    sine = jnp.where(lane < DH // 2, -sine, sine)

    copy_x.wait()
    for r in range(reqs):
        xs[pl.ds(r * steps, steps), :] = x_v[r].astype(F32)
    normed = norm_rows(xs[...]).astype(BF16)

    def turned(part, head):
        v = part[:, head * DH : (head + 1) * DH]
        return (v * cosine + pltpu.roll(v, DH // 2, 1) * sine).astype(BF16).astype(F32)

    def emit(j, rotated, out, store):
        copies_w[j].wait()
        part = jnp.dot(normed, w_v[j], preferred_element_type=F32)
        for h in range(heads):
            v = turned(part, h) if rotated else part[:, h * DH : (h + 1) * DH].astype(BF16).astype(F32)
            store[pl.ds(h, rows, stride=heads), :] = v
            flat[...] = v
            for r in range(reqs):
                out[r, :, h * DH : (h + 1) * DH] = flat[pl.ds(r * steps, steps), :].astype(BF16)

    emit(0, True, q_out, q16)

    tall = steps * heads
    row_head = lax.broadcasted_iota(jnp.int32, (tall, DH), 0) % heads
    lane16 = lax.broadcasted_iota(jnp.int32, (tall, DH), 1)
    for r in range(reqs):
        if r % (reqs // 2) == 0:
            copies_k[r // (reqs // 2)].wait()
            copies_v[r // (reqs // 2)].wait()
        q = q16[r * tall : (r + 1) * tall, :]
        spread = jnp.concatenate([jnp.where(row_head == h, q, 0.0).astype(BF16) for h in range(heads)], axis=1)
        scores = lax.dot_general(spread, ck_v[r], (((1,), (1,)), ((), ())), preferred_element_type=F32) * SCALE
        live = lane16 < len_ref[r] - seq * block
        highest = jnp.max(jnp.where(live, scores, NEG), axis=-1, keepdims=True)
        weights = jnp.where(live, jnp.exp(scores - highest), 0.0)
        total = jnp.sum(weights, axis=-1, keepdims=True)
        wide = jnp.dot(weights.astype(BF16), cv_v[r], preferred_element_type=F32)
        o = wide[:, 0:DH]
        for h in range(1, heads):
            o = jnp.where(row_head == h, wide[:, h * DH : (h + 1) * DH], o)
        pieces = split3(jnp.broadcast_to(highest, o.shape)) + split3(jnp.broadcast_to(total, o.shape))
        stats = pieces[5]
        for i in range(4, -1, -1):
            stats = jnp.where(lane16 == i, pieces[i], stats)
        half = tall // 2
        for i in range(2):
            part_out[2 * r + i, 0:half, :] = o[i * half : (i + 1) * half].astype(BF16)
            part_out[2 * r + i, half : 2 * half, :] = stats[i * half : (i + 1) * half].astype(BF16)

    emit(1, True, k_out, k16)
    emit(2, False, v_out, v16)

    half = tall // 2
    q = q16[pl.ds(seq * half, half), :]
    step = (seq % 2) * 2 + lax.broadcasted_iota(jnp.int32, (half, 1), 0) // heads
    base = (seq // 2) * tall
    scores = []
    values = []
    for s in range(steps):
        key = k16[pl.ds(base + s * heads, heads), :]
        value = v16[pl.ds(base + s * heads, heads), :]
        key = jnp.concatenate([key, key], axis=0)
        values.append(jnp.concatenate([value, value], axis=0))
        scores.append(jnp.sum(q * key, axis=-1, keepdims=True) * SCALE)
    highest = scores[0]
    for s in range(1, steps):
        highest = jnp.maximum(highest, jnp.where(s <= step, scores[s], NEG))
    total = jnp.zeros_like(highest)
    o = jnp.zeros((half, DH), F32)
    for s in range(steps):
        weight = jnp.where(s <= step, jnp.exp(scores[s] - highest), 0.0)
        total = total + weight
        o = o + weight.astype(BF16).astype(F32) * values[s]
    fresh_out[0] = o
    fresh_out[1] = jnp.broadcast_to(highest, o.shape)
    fresh_out[2] = jnp.broadcast_to(total, o.shape)


def merge_kernel(got_ref, fresh_ref, w_ref, out_ref, ctx_s):
    half = fresh_ref.shape[1]
    heads = half // 2
    stats = got_ref[:, half : 2 * half, :].astype(F32)
    highest = (stats[:, :, 0:1] + stats[:, :, 1:2]) + stats[:, :, 2:3]
    total = (stats[:, :, 3:4] + stats[:, :, 4:5]) + stats[:, :, 5:6]
    fresh_high = fresh_ref[1][:, 0:1]
    top = jnp.maximum(jnp.max(highest, axis=0), fresh_high)
    factor = jnp.exp(highest - top[None])
    fresh_factor = jnp.exp(fresh_high - top)
    whole = jnp.sum(factor * total, axis=0) + fresh_factor * fresh_ref[2][:, 0:1]
    o = jnp.sum(factor * got_ref[:, 0:half, :].astype(F32), axis=0) + fresh_factor * fresh_ref[0]
    ctx_s[...] = o / whole
    ctx = jnp.concatenate([ctx_s[pl.ds(h, 2, stride=heads), :] for h in range(heads)], axis=1)
    out_ref[...] = jnp.dot(ctx.astype(BF16), w_ref[...], preferred_element_type=F32)


def mlp_kernel(x_ref, a_ref, b_ref, c_ref, d_ref, gu_ref, wd_ref, o0, o1, o2, o3, mid_s, down_s):
    seq = lax.axis_index("seq")
    me = lax.axis_index("mp")
    parts = down_s.shape[0]
    cols = down_s.shape[2]
    x = x_ref[seq // 2].astype(F32)
    x = jnp.where(seq % 2 == 0, x[0:2], x[2:4])
    middle = x + ((a_ref[...] + b_ref[...]) + (c_ref[...] + d_ref[...]))
    normed = norm_rows(middle).astype(BF16)
    gate = jnp.dot(normed, gu_ref[0], preferred_element_type=F32)
    up = jnp.dot(normed, gu_ref[1], preferred_element_type=F32)
    active = ((gate / (1.0 + jnp.exp(-gate))) * up).astype(BF16)
    down = jnp.dot(active, wd_ref[...], preferred_element_type=F32)
    for p in range(parts):
        mid_s[p] = middle[:, p * cols : (p + 1) * cols]
        down_s[p] = down[:, p * cols : (p + 1) * cols]
    o0[...] = down_s[me] + mid_s[me]
    o1[...] = down_s[me ^ 1]
    o2[...] = down_s[me ^ 2]
    o3[...] = down_s[me ^ 3]


def to_others(values, axis):
    size = lax.axis_size(axis)
    return [
        lax.ppermute(v, axis, [(i, i ^ k) for i in range(size)]) for k, v in zip(range(1, size), values)
    ]


def per_device(inputs, w_qkv, w_out, w_gate_up, w_down, cache_keys, cache_values, lengths):
    reqs, steps, model = inputs.shape
    block = cache_keys.shape[1]
    width = cache_keys.shape[2]
    heads = width // DH
    rows = reqs * steps
    tall = steps * heads
    n_seq = lax.axis_size("seq")
    n_mp = lax.axis_size("mp")
    assert rows == 2 * n_seq and steps == 4 and n_mp == 4 and tall == 16
    half_dim = DH // 2
    freq = np.float32(10000.0) ** (np.float32(-2.0) * np.arange(half_dim, dtype=np.float32) / np.float32(DH))
    freq = np.broadcast_to(np.concatenate([freq, freq]).astype(np.float32), (8, DH))
    in_hbm = functools.partial(pltpu.with_memory_space_constraint, memory_space=pltpu.HBM)
    any_space = pl.BlockSpec(memory_space=pltpu.HBM)
    vmem = pl.BlockSpec(memory_space=pltpu.VMEM)
    smem = pl.BlockSpec(memory_space=pltpu.SMEM)
    piece = jax.ShapeDtypeStruct((reqs, steps, width), BF16)
    queries, new_keys, new_values, part, fresh = pl.pallas_call(
        functools.partial(local_kernel, reqs, steps, block, width),
        out_shape=(
            piece, piece, piece,
            jax.ShapeDtypeStruct((n_seq, tall, DH), BF16),
            jax.ShapeDtypeStruct((3, tall // 2, DH), F32),
        ),
        in_specs=[smem, any_space, any_space, any_space, any_space, vmem],
        out_specs=(vmem,) * 5,
        scratch_shapes=[
            pltpu.VMEM(inputs.shape, BF16),
            pltpu.VMEM(w_qkv.shape, BF16),
            pltpu.VMEM(cache_keys.shape, BF16),
            pltpu.VMEM(cache_values.shape, BF16),
            pltpu.VMEM((rows, model), F32),
            pltpu.VMEM((rows * heads, DH), F32),
            pltpu.VMEM((rows * heads, DH), F32),
            pltpu.VMEM((rows * heads, DH), F32),
            pltpu.VMEM((rows, DH), F32),
            pltpu.SemaphoreType.DMA,
            pltpu.SemaphoreType.DMA((3,)),
            pltpu.SemaphoreType.DMA((4,)),
        ],
        compiler_params=pltpu.CompilerParams(vmem_limit_bytes=32 << 20),
        name="local_attention",
    )(lengths, *(in_hbm(a) for a in (inputs, w_qkv, cache_keys, cache_values)), jnp.asarray(freq))

    got = lax.all_to_all(part, "seq", 0, 0)

    mine = pl.pallas_call(
        merge_kernel,
        out_shape=jax.ShapeDtypeStruct((2, model), F32),
        in_specs=[vmem, vmem, vmem],
        out_specs=vmem,
        scratch_shapes=[pltpu.VMEM((tall // 2, DH), F32)],
        compiler_params=pltpu.CompilerParams(vmem_limit_bytes=8 << 20),
        name="merge_project",
    )(got, fresh, w_out)
    others = to_others([mine] * 3, "mp")

    cols = model // n_mp
    chunk = jax.ShapeDtypeStruct((2, cols), F32)
    own, *rest = pl.pallas_call(
        mlp_kernel,
        out_shape=(chunk,) * 4,
        in_specs=[vmem] * 7,
        out_specs=(vmem,) * 4,
        scratch_shapes=[pltpu.VMEM((n_mp, 2, cols), F32)] * 2,
        compiler_params=pltpu.CompilerParams(vmem_limit_bytes=20 << 20),
        name="mlp",
    )(inputs, mine, *others, w_gate_up, w_down)
    back = to_others(rest, "mp")
    hidden = ((own + back[0]) + (back[1] + back[2])).astype(BF16)
    hidden = lax.all_to_all(jnp.broadcast_to(hidden[None], (n_seq, 2, cols)), "seq", 0, 0)
    return (hidden.reshape(reqs, steps, cols), queries, new_keys, new_values)


def solution(mesh):
    placed = (
        P(),
        P(None, None, "mp"),
        P("mp", None),
        P(None, None, "mp"),
        P("mp", None),
        P(None, "seq", "mp"),
        P(None, "seq", "mp"),
        P(),
    )
    return jax.shard_map(
        per_device,
        mesh=mesh,
        in_specs=placed,
        out_specs=(P(None, None, "mp"),) * 4,
        check_vma=False,
    )
```

time: 906 us -> 77 us (0.08); the launches traced: 896 us -> 76.6 us
  blocking collectives: 510 us -> 41.4 us
  local copies, waits for them, and re-layouts: 155 us -> 2.45 us
  waiting for transfers between devices: 113 us -> 5.56 us
  other arithmetic: 82.2 us -> 0.01 us
  Pallas kernels: 0 us -> 19.8 us
  matrix products: 18.5 us -> 0 us
  between operations: 14 us -> 0.71 us
    all_gather x2 -> x0, blocking collectives: 510 us -> none  [merged_2(): gathered = jax.tree.map(lambda a: lax.all_gather(a, axis), part)]
    psum x2 -> x0, waiting for transfers between devices: 90.5 us -> none  [the longest x1 46.7 us: per_device(): lax.psum(jnp.dot(flat_ctx, w_out, preferred_element_type=jnp.float32), 'mp')]
    add x128 -> x0, other arithmetic: 66.5 us -> none  [the longest x64 47.1 us: join(): totals = earlier[1] * lead_scale + later[1] * tail_scale]
    dynamic_slice x65 -> x0, local copies, waits for them, and re-layouts: 61.4 us -> none  [take(): lax.dynamic_index_in_dim(a, source, 0, False)]
    all_to_all x0 -> x2, blocking collectives: none -> 41.4 us  [the longest x1 25.6 us: per_device(): got = lax.all_to_all(part, 'seq', 0, 0)]
    broadcast_in_dim x128 -> x1, local copies, waits for them, and re-layouts: 25.3 us -> 0.07 us  [per_device(): jnp.broadcast_to(hidden[None], (n_seq, 2, cols))]
    all_gather x1 -> x0, waiting for transfers between devices: 22 us -> none  [merged_2(): gathered = jax.tree.map(lambda a: lax.all_gather(a, axis), part)]
    reshape x131 -> x1, local copies, waits for them, and re-layouts: 22.3 us -> 0.71 us  [per_device(): return (hidden.reshape(reqs, steps, cols), queries, new_keys, new_values)]
  transfers between devices with their start and end apart: 3 -> 6, of which waited for: 3 -> 4; matrix products, arithmetic and copies ran while one was open for 3% -> 0% of each run, Pallas kernels for 0% -> 0%
where the time goes in v1:
time: 77 us; the launch traced here: 76.6 us
  blocking collectives  41.4 us (54%)
  Pallas kernels  19.8 us (26%)
  starting transfers between devices  6.75 us (9%)
  waiting for transfers between devices  5.56 us (7%)
  local copies, waits for them, and re-layouts  2.45 us (3%)
    all_to_all x1, blocking collectives, per_device(): got = lax.all_to_all(part, 'seq', 0, 0)  25.6 us
    pallas_call x1, Pallas kernels, per_device(): pl.pallas_call(functools.partial(local_kernel, reqs, steps, block, width)...  17.1 us
    all_to_all x1, blocking collectives, per_device(): lax.all_to_all(jnp.broadcast_to(hidden[None], (n_seq, 2, cols)), 'seq', 0...  15.8 us
    ppermute x6, starting transfers between devices, to_others(): lax.ppermute(v, axis, [(i, i ^ k) for i in range(size)])  6.75 us
    ppermute x6, waiting for transfers between devices, to_others(): lax.ppermute(v, axis, [(i, i ^ k) for i in range(size)])  5.56 us
    pallas_call x1, Pallas kernels, per_device(): pl.pallas_call(mlp_kernel, out_shape=(chunk,) * 4, in_specs=[vmem] * 7, o...  1.95 us
  transfers between devices with their start and end apart: 6, of which 4 were waited for; matrix products, arithmetic and copies ran while one was open for 0% of the time, Pallas kernels for 0%

profile of v1, /device:TPU:4, one launch (start us, length us, event | category | flops | bytes accessed | tf_op | source)
XLA Modules:
  0.0 76.6 jit_solution(7301609708734430735)
XLA Ops:
  0.6 0.0 slice-start
  0.6 0.8 %jit_solution_.3.freq_ref = f32[8,128]{1,0:T(8,128)S(1)} broadcast(f32[128]{0:T(128)} %constant.2.clone), dimensions={1} | broadcast | bytes 4608 | tf_op jit(solution)
  1.5 0.0 copy-start.3
  1.5 0.8 %copy-done.3 = s32[32]{0:T(128)S(1)} copy-done((s32[32]{0:T(128)S(1)}, s32[32]{0:T(128)}, u32[]{:S(2)}) %copy-start.3) | copy-done | bytes 152
  2.3 0.0 copy-start.2
  2.3 0.0 slice-start.1
  2.3 0.0 copy-start
  2.3 0.0 copy-start.1
  2.3 17.1 %local_attention.1 = (bf16[32,4,512]{2,1,0:T(4,128)(2,1)}, bf16[32,4,512]{2,1,0:T(4,128)(2,1)}, bf16[32,4,512]{2,1,0:T(4,128)(2,1)}, bf16[64,16,128]{2,1,0:T(8,128)(2,1)S(1)}, f32[3,8,128]{2,1,0:T(8,128)S(1)}) custom-call(s32[32]{0:T(128)S(1)} %copy-done.3, bf16[32,4,2048]{2,1,0:T(4,128)(2,1)} %x_ref.1, bf16[3,2048,512]{2,1,0:T(8,128)(2,1)} %w_hbm.1, ...), custom_call_target="tpu_custom_call" | custom-call | tf_op jit(solution)/shard_map/local_attention/pallas_call | solution.py:210
  19.4 25.6 %all_to_all.10.got_ref = bf16[64,16,128]{2,1,0:T(8,128)(2,1)S(1)} all-to-all(bf16[64,16,128]{2,1,0:T(8,128)(2,1)S(1)} %get-tuple-element.13), channel_id=1, replica_groups=mesh['seq'=64,'mp'=4] {'seq'}, dimensions={0} | all-to-all | bytes 524288 | tf_op jit(solution)/shard_map/all_to_all | solution.py:237
  45.0 0.0 copy-done.2
  45.0 0.7 merge_project.1.a_ref
  45.7 0.0 collective-permute-start.2
  45.7 0.9 %collective-permute-start.1 = (f32[2,2048]{1,0:T(2,128)S(1)}, f32[2,2048]{1,0:T(2,128)S(1)}, u32[]{:S(2)}, u32[]{:S(2)}) collective-permute-start(f32[2,2048]{1,0:T(2,128)S(1)} %merge_project.1.a_ref), channel_id=1, source_target_pairs={{0,2},{1,3},{2,0},{3,1},{4,6},{5,7},{6,4},{7,5},{8,10},{9,11},{10,... | collective-permute-start | bytes 49160 | tf_op jit(solution)/shard_map/ppermute | solution.py:188
  46.6 2.5 %collective-permute-start = (f32[2,2048]{1,0:T(2,128)S(1)}, f32[2,2048]{1,0:T(2,128)S(1)}, u32[]{:S(2)}, u32[]{:S(2)}) collective-permute-start(f32[2,2048]{1,0:T(2,128)S(1)} %merge_project.1.a_ref), channel_id=1, source_target_pairs={{0,1},{1,0},{2,3},{3,2},{4,5},{5,4},{6,7},{7,6},{8,9},{9,8},{10,11... | collective-permute-start | bytes 49160 | tf_op jit(solution)/shard_map/ppermute | solution.py:188
  49.1 1.3 %collective-permute-done.2.d_ref = f32[2,2048]{1,0:T(2,128)S(1)} collective-permute-done((f32[2,2048]{1,0:T(2,128)S(1)}, f32[2,2048]{1,0:T(2,128)S(1)}, u32[]{:S(2)}, u32[]{:S(2)}) %collective-permute-start.2) | collective-permute-done | bytes 16416 | tf_op jit(solution)/shard_map/ppermute | solution.py:188
  50.4 0.7 collective-permute-done.1.c_ref
  51.1 0.0 collective-permute-done.b_ref
  51.1 0.0 slice-done
  51.1 0.0 slice-done.1
  51.1 0.0 copy-done
  51.1 0.0 copy-done.1
  51.1 1.9 %mlp.1 = (f32[2,512]{1,0:T(2,128)S(1)}, f32[2,512]{1,0:T(2,128)S(1)}, f32[2,512]{1,0:T(2,128)S(1)}, f32[2,512]{1,0:T(2,128)S(1)}) custom-call(bf16[32,4,2048]{2,1,0:T(4,128)(2,1)S(1)} %copy-done.1, f32[2,2048]{1,0:T(2,128)S(1)} %merge_project.1.a_ref, f32[2,2048]{1,0:T(2,128)S(1)} %collective-permute-done.b_ref, f32[2,2048]{1,0:T(2,128)S(1)} %collective-permute-done.1.c_ref, ...), custom_call_target="tpu_custom_call" | custom-call | tf_op jit(solution)/shard_map/mlp/pallas_call | solution.py:252
  53.0 0.0 collective-permute-start.3
  53.1 2.4 %collective-permute-start.4 = (f32[2,512]{1,0:T(2,128)S(1)}, f32[2,512]{1,0:T(2,128)S(1)}, u32[]{:S(2)}, u32[]{:S(2)}) collective-permute-start(f32[2,512]{1,0:T(2,128)S(1)} %get-tuple-element.17), channel_id=1, source_target_pairs={{0,2},{1,3},{2,0},{3,1},{4,6},{5,7},{6,4},{7,5},{8,10},{9,11},{10,... | collective-permute-start | bytes 12296 | tf_op jit(solution)/shard_map/ppermute | solution.py:188
  55.4 1.0 %collective-permute-start.5 = (f32[2,512]{1,0:T(2,128)S(1)}, f32[2,512]{1,0:T(2,128)S(1)}, u32[]{:S(2)}, u32[]{:S(2)}) collective-permute-start(f32[2,512]{1,0:T(2,128)S(1)} %get-tuple-element.18), channel_id=1, source_target_pairs={{0,3},{1,2},{2,1},{3,0},{4,7},{5,6},{6,5},{7,4},{8,11},{9,10},{10,... | collective-permute-start | bytes 12296 | tf_op jit(solution)/shard_map/ppermute | solution.py:188
  56.4 0.0 collective-permute-done.3
  56.4 1.8 %collective-permute-done.4 = f32[2,512]{1,0:T(2,128)S(1)} collective-permute-done((f32[2,512]{1,0:T(2,128)S(1)}, f32[2,512]{1,0:T(2,128)S(1)}, u32[]{:S(2)}, u32[]{:S(2)}) %collective-permute-start.4) | collective-permute-done | bytes 4128 | tf_op jit(solution)/shard_map/ppermute | solution.py:188
  58.3 1.7 %collective-permute-done.5 = f32[2,512]{1,0:T(2,128)S(1)} collective-permute-done((f32[2,512]{1,0:T(2,128)S(1)}, f32[2,512]{1,0:T(2,128)S(1)}, u32[]{:S(2)}, u32[]{:S(2)}) %collective-permute-start.5) | collective-permute-done | bytes 4128 | tf_op jit(solution)/shard_map/ppermute | solution.py:188
  60.0 0.1 broadcast_in_dim.2
  60.1 15.8 %all_to_all.11 = bf16[64,2,512]{2,1,0:T(2,128)(2,1)S(1)} all-to-all(bf16[64,2,512]{2,1,0:T(2,128)(2,1)S(1)} %broadcast_in_dim.2), channel_id=1, replica_groups=mesh['seq'=64,'mp'=4] {'seq'}, dimensions={0} | all-to-all | bytes 262144 | tf_op jit(solution)/shard_map/all_to_all | solution.py:263
  75.9 0.7 reshape.12
  (2 shorter events, 0.0 us)
Async XLA Ops:
  0.6 50.4 %slice-start = ((s8[8388608]{0:T(1024)(128)(4,1)}), s8[4194304]{0:T(1024)(128)(4,1)S(1)}, s32[]{:S(2)}) async-start(s8[8388608]{0:T(1024)(128)(4,1)} %bitcast), calls=%async_computation.2 | async-start | bytes 8388608
  1.5 0.8 %copy-start.3 = (s32[32]{0:T(128)S(1)}, s32[32]{0:T(128)}, u32[]{:S(2)}) copy-start(s32[32]{0:T(128)} %len_ref.1) | copy-start | bytes 388
  2.3 42.7 %copy-start.2 = (bf16[512,2048]{1,0:T(8,128)(2,1)S(1)}, bf16[512,2048]{1,0:T(8,128)(2,1)}, u32[]{:S(2)}) copy-start(bf16[512,2048]{1,0:T(8,128)(2,1)} %w_ref.1) | copy-start | bytes 6291460
  2.3 48.8 %slice-start.1 = ((s8[8388608]{0:T(1024)(128)(4,1)}), s8[4194304]{0:T(1024)(128)(4,1)S(1)}, s32[]{:S(2)}) async-start(s8[8388608]{0:T(1024)(128)(4,1)} %bitcast), calls=%async_computation.3 | async-start | bytes 8388608
  2.3 48.8 %copy-start = (bf16[1024,2048]{1,0:T(8,128)(2,1)S(1)}, bf16[1024,2048]{1,0:T(8,128)(2,1)}, u32[]{:S(2)}) copy-start(bf16[1024,2048]{1,0:T(8,128)(2,1)} %wd_ref.1) | copy-start | bytes 12582916
  2.3 48.8 %copy-start.1 = (bf16[32,4,2048]{2,1,0:T(4,128)(2,1)S(1)}, bf16[32,4,2048]{2,1,0:T(4,128)(2,1)}, u32[]{:S(2)}) copy-start(bf16[32,4,2048]{2,1,0:T(4,128)(2,1)} %x_ref.1) | copy-start | bytes 1572868
  45.7 4.7 %collective-permute-start.2 = (f32[2,2048]{1,0:T(2,128)S(1)}, f32[2,2048]{1,0:T(2,128)S(1)}, u32[]{:S(2)}, u32[]{:S(2)}) collective-permute-start(f32[2,2048]{1,0:T(2,128)S(1)} %merge_project.1.a_ref), channel_id=1, source_target_pairs={{0,3},{1,2},{2,1},{3,0},{4,7},{5,6},{6,5},{7,4},{8,11},{9,10},{10,... | collective-permute-start | bytes 49160 | tf_op jit(solution)/shard_map/ppermute | solution.py:188
  45.7 5.4 %collective-permute-start.1 = (f32[2,2048]{1,0:T(2,128)S(1)}, f32[2,2048]{1,0:T(2,128)S(1)}, u32[]{:S(2)}, u32[]{:S(2)}) collective-permute-start(f32[2,2048]{1,0:T(2,128)S(1)} %merge_project.1.a_ref), channel_id=1, source_target_pairs={{0,2},{1,3},{2,0},{3,1},{4,6},{5,7},{6,4},{7,5},{8,10},{9,11},{10,... | collective-permute-start | bytes 49160 | tf_op jit(solution)/shard_map/ppermute | solution.py:188
  46.6 4.5 %collective-permute-start = (f32[2,2048]{1,0:T(2,128)S(1)}, f32[2,2048]{1,0:T(2,128)S(1)}, u32[]{:S(2)}, u32[]{:S(2)}) collective-permute-start(f32[2,2048]{1,0:T(2,128)S(1)} %merge_project.1.a_ref), channel_id=1, source_target_pairs={{0,1},{1,0},{2,3},{3,2},{4,5},{5,4},{6,7},{7,6},{8,9},{9,8},{10,11... | collective-permute-start | bytes 49160 | tf_op jit(solution)/shard_map/ppermute | solution.py:188
  53.0 3.4 %collective-permute-start.3 = (f32[2,512]{1,0:T(2,128)S(1)}, f32[2,512]{1,0:T(2,128)S(1)}, u32[]{:S(2)}, u32[]{:S(2)}) collective-permute-start(f32[2,512]{1,0:T(2,128)S(1)} %get-tuple-element.16), channel_id=1, source_target_pairs={{0,1},{1,0},{2,3},{3,2},{4,5},{5,4},{6,7},{7,6},{8,9},{9,8},{10,11... | collective-permute-start | bytes 12296 | tf_op jit(solution)/shard_map/ppermute | solution.py:188
  53.1 5.2 %collective-permute-start.4 = (f32[2,512]{1,0:T(2,128)S(1)}, f32[2,512]{1,0:T(2,128)S(1)}, u32[]{:S(2)}, u32[]{:S(2)}) collective-permute-start(f32[2,512]{1,0:T(2,128)S(1)} %get-tuple-element.17), channel_id=1, source_target_pairs={{0,2},{1,3},{2,0},{3,1},{4,6},{5,7},{6,4},{7,5},{8,10},{9,11},{10,... | collective-permute-start | bytes 12296 | tf_op jit(solution)/shard_map/ppermute | solution.py:188
  55.4 4.6 %collective-permute-start.5 = (f32[2,512]{1,0:T(2,128)S(1)}, f32[2,512]{1,0:T(2,128)S(1)}, u32[]{:S(2)}, u32[]{:S(2)}) collective-permute-start(f32[2,512]{1,0:T(2,128)S(1)} %get-tuple-element.18), channel_id=1, source_target_pairs={{0,3},{1,2},{2,1},{3,0},{4,7},{5,6},{6,5},{7,4},{8,11},{9,10},{10,... | collective-permute-start | bytes 12296 | tf_op jit(solution)/shard_map/ppermute | solution.py:188

commit v2 on v1

v2 whole, which is shorter than its diff:
```python
import functools

import jax
import jax.numpy as jnp
import numpy as np
from jax import lax
from jax.experimental import pallas as pl
from jax.experimental.pallas import tpu as pltpu
from jax.sharding import PartitionSpec as P

DH = 128
NEG = -1e30
EPS = 1e-05
SCALE = DH ** (-0.5)
F32 = jnp.float32
BF16 = jnp.bfloat16


def norm_rows(x):
    centred = x - jnp.mean(x, axis=-1, keepdims=True)
    variance = jnp.mean(centred * centred, axis=-1, keepdims=True)
    return centred * lax.rsqrt(variance + EPS)


def split3(v):
    a = v.astype(BF16).astype(F32)
    rest = v - a
    b = rest.astype(BF16).astype(F32)
    return a, b, rest - b


def frequencies():
    half = DH // 2
    values = np.float32(10000.0) ** (np.float32(-2.0) * np.arange(half, dtype=np.float32) / np.float32(DH))
    lane = lax.broadcasted_iota(jnp.int32, (8, DH), 1) % half
    freq = jnp.full((8, DH), float(values[0]), F32)
    for i in range(1, half):
        freq = jnp.where(lane == i, float(values[i]), freq)
    return freq


def turn(v, cosine, sine):
    return v * cosine + pltpu.roll(v, DH // 2, 1) * sine


def rounded(v):
    return v.astype(BF16).astype(F32)


def cached_kernel(
    group, reqs, steps, block, width,
    len_hbm, x_hbm, w_hbm, ck_hbm, cv_hbm,
    part_out, q_rows, q_own, normed_out, cos_out, sin_out,
    len_s, x_v, w_v, ck_v, cv_v, xs, q16, sem_l, sem_x, sem_w, sem_k, sem_v,
):
    heads = width // DH
    rows = reqs * steps
    seq = lax.axis_index("seq")
    copy_l = pltpu.make_async_copy(len_hbm, len_s, sem_l)
    copy_l.start()
    copy_x = pltpu.make_async_copy(x_hbm, x_v, sem_x)
    copy_x.start()
    copy_w = pltpu.make_async_copy(w_hbm.at[0], w_v, sem_w)
    copy_w.start()
    count = reqs // group
    copies = []
    for g in range(count):
        span = pl.ds(g * group, group)
        copies.append((
            pltpu.make_async_copy(ck_hbm.at[span], ck_v.at[span], sem_k.at[g]),
            pltpu.make_async_copy(cv_hbm.at[span], cv_v.at[span], sem_v.at[g]),
        ))
        copies[g][0].start()
        copies[g][1].start()

    copy_l.wait()
    freq = frequencies()
    step_of = (lax.broadcasted_iota(jnp.int32, (8, DH), 0) % steps).astype(F32)
    lane8 = lax.broadcasted_iota(jnp.int32, (8, DH), 1)
    upper = lax.broadcasted_iota(jnp.int32, (8, DH), 0) >= steps
    for r in range(0, reqs, 2):
        place = jnp.where(upper, len_s[r + 1], len_s[r]).astype(F32) + step_of
        angles = place * freq
        cos_out[r * steps : (r + 2) * steps, :] = jnp.cos(angles)
        sine = jnp.sin(angles)
        sin_out[r * steps : (r + 2) * steps, :] = jnp.where(lane8 < DH // 2, -sine, sine)

    copy_x.wait()
    for r in range(reqs):
        xs[pl.ds(r * steps, steps), :] = x_v[r].astype(F32)
    normed_out[...] = norm_rows(xs[...]).astype(BF16)

    copy_w.wait()
    part = jnp.dot(normed_out[...], w_v[...], preferred_element_type=F32)
    for h in range(heads):
        q = turn(part[:, h * DH : (h + 1) * DH], cos_out[...], sin_out[...]).astype(BF16)
        q_rows[:, h * DH : (h + 1) * DH] = q
        q16[pl.ds(h, rows, stride=heads), :] = q.astype(F32)

    tall = steps * heads
    half = tall // 2
    q_own[...] = q16[pl.ds(seq * half, half), :]
    lane = lax.broadcasted_iota(jnp.int32, (tall, DH), 1)
    many_head = lax.broadcasted_iota(jnp.int32, (group * tall, DH), 0) % heads
    many_lane = lax.broadcasted_iota(jnp.int32, (group * tall, DH), 1)
    for g in range(count):
        q = q16[g * group * tall : (g + 1) * group * tall, :]
        spread = jnp.concatenate([jnp.where(many_head == h, q, 0.0).astype(BF16) for h in range(heads)], axis=1)
        copies[g][0].wait()
        scores = []
        for i in range(group):
            r = g * group + i
            score = lax.dot_general(
                spread[i * tall : (i + 1) * tall], ck_v[r], (((1,), (1,)), ((), ())), preferred_element_type=F32
            )
            scores.append(jnp.where(lane < len_s[r] - seq * block, score * SCALE, NEG))
        scores = jnp.concatenate(scores, axis=0)
        highest = jnp.max(scores, axis=-1, keepdims=True)
        weights = jnp.where(scores == NEG, 0.0, jnp.exp(scores - highest))
        total = jnp.sum(weights, axis=-1, keepdims=True)
        weights = weights.astype(BF16)
        copies[g][1].wait()
        pieces = split3(jnp.broadcast_to(highest, scores.shape)) + split3(jnp.broadcast_to(total, scores.shape))
        stats = pieces[5]
        for i in range(4, -1, -1):
            stats = jnp.where(many_lane == i, pieces[i], stats)
        stats = stats.astype(BF16)
        for i in range(group):
            r = g * group + i
            wide = jnp.dot(weights[i * tall : (i + 1) * tall], cv_v[r], preferred_element_type=F32)
            o = wide[:, 0:DH]
            for h in range(1, heads):
                o = jnp.where(many_head[0:tall] == h, wide[:, h * DH : (h + 1) * DH], o)
            for j in range(2):
                part_out[2 * r + j, 0:half, :] = o[j * half : (j + 1) * half].astype(BF16)
                part_out[2 * r + j, half : 2 * half, :] = stats[i * tall + j * half : i * tall + (j + 1) * half]


def fresh_kernel(
    reqs, steps, width,
    w_hbm, proj_hbm, q_rows, q_own, normed, cosine, sine,
    q_out, k_out, v_out, fresh_out, proj_out,
    w_v, k16, v16, sem_w, sem_p,
):
    heads = width // DH
    rows = reqs * steps
    tall = steps * heads
    half = tall // 2
    seq = lax.axis_index("seq")
    copies = [pltpu.make_async_copy(w_hbm.at[1 + j], w_v.at[j], sem_w.at[j]) for j in range(2)]
    for c in copies:
        c.start()
    copy_p = pltpu.make_async_copy(proj_hbm, proj_out, sem_p)
    copy_p.start()

    def emit(store, out):
        for h in range(heads):
            v = store[pl.ds(h, rows, stride=heads), :]
            out[:, :, h * DH : (h + 1) * DH] = v.reshape(reqs, steps, DH).astype(BF16)

    q_out[...] = q_rows[...].reshape(q_out.shape)
    for j, store, out in ((0, k16, k_out), (1, v16, v_out)):
        copies[j].wait()
        part = jnp.dot(normed[...], w_v[j], preferred_element_type=F32)
        for h in range(heads):
            v = part[:, h * DH : (h + 1) * DH]
            v = turn(v, cosine[...], sine[...]) if j == 0 else v
            store[pl.ds(h, rows, stride=heads), :] = rounded(v)
        emit(store, out)

    q = q_own[...]
    step = (seq % 2) * 2 + lax.broadcasted_iota(jnp.int32, (half, 1), 0) // heads
    base = (seq // 2) * tall
    scores = []
    values = []
    for s in range(steps):
        key = k16[pl.ds(base + s * heads, heads), :]
        value = v16[pl.ds(base + s * heads, heads), :]
        key = jnp.concatenate([key, key], axis=0)
        values.append(jnp.concatenate([value, value], axis=0))
        scores.append(jnp.sum(q * key, axis=-1, keepdims=True) * SCALE)
    highest = scores[0]
    for s in range(1, steps):
        highest = jnp.maximum(highest, jnp.where(s <= step, scores[s], NEG))
    total = jnp.zeros_like(highest)
    o = jnp.zeros((half, DH), F32)
    for s in range(steps):
        weight = jnp.where(s <= step, jnp.exp(scores[s] - highest), 0.0)
        total = total + weight
        o = o + rounded(weight) * values[s]
    fresh_out[0] = o
    fresh_out[1] = jnp.broadcast_to(highest, o.shape)
    fresh_out[2] = jnp.broadcast_to(total, o.shape)
    copy_p.wait()


def merge_kernel(got_ref, fresh_ref, w_ref, out_ref, ctx_s):
    half = fresh_ref.shape[1]
    heads = half // 2
    stats = got_ref[:, half : 2 * half, :].astype(F32)
    highest = (stats[:, :, 0:1] + stats[:, :, 1:2]) + stats[:, :, 2:3]
    total = (stats[:, :, 3:4] + stats[:, :, 4:5]) + stats[:, :, 5:6]
    fresh_high = fresh_ref[1][:, 0:1]
    top = jnp.maximum(jnp.max(highest, axis=0), fresh_high)
    factor = jnp.exp(highest - top[None])
    fresh_factor = jnp.exp(fresh_high - top)
    whole = jnp.sum(factor * total, axis=0) + fresh_factor * fresh_ref[2][:, 0:1]
    o = jnp.sum(factor * got_ref[:, 0:half, :].astype(F32), axis=0) + fresh_factor * fresh_ref[0]
    ctx_s[...] = o / whole
    ctx = jnp.concatenate([ctx_s[pl.ds(h, 2, stride=heads), :] for h in range(heads)], axis=1)
    out_ref[...] = jnp.dot(ctx.astype(BF16), w_ref[...], preferred_element_type=F32)


def mlp_kernel(
    x_hbm, gu_hbm, wd_hbm, a_ref, b_ref, c_ref, d_ref,
    o0, o1, o2, o3,
    x_v, gu_v, wd_v, mid_s, down_s, sem_x, sem_g, sem_d,
):
    seq = lax.axis_index("seq")
    me = lax.axis_index("mp")
    parts = down_s.shape[0]
    cols = down_s.shape[2]
    model = gu_v.shape[1]
    inner = wd_v.shape[0]
    pieces = sem_g.shape[1]
    copy_x = pltpu.make_async_copy(x_hbm.at[seq // 2], x_v, sem_x)
    copy_x.start()
    copies_g = []
    for p in range(pieces):
        span = pl.ds(p * (model // pieces), model // pieces)
        for j in range(2):
            copies_g.append(pltpu.make_async_copy(gu_hbm.at[j, span], gu_v.at[j, span], sem_g.at[j, p]))
            copies_g[-1].start()
    copies_d = []
    for p in range(pieces):
        span = pl.ds(p * (inner // pieces), inner // pieces)
        copies_d.append(pltpu.make_async_copy(wd_hbm.at[span], wd_v.at[span], sem_d.at[p]))
        copies_d[-1].start()
    others = (a_ref[...] + b_ref[...]) + (c_ref[...] + d_ref[...])
    copy_x.wait()
    x = x_v[...].astype(F32)
    middle = jnp.where(seq % 2 == 0, x[0:2], x[2:4]) + others
    normed = norm_rows(middle).astype(BF16)
    gate_up = [None, None]
    for p in range(pieces):
        lo, hi = p * (model // pieces), (p + 1) * (model // pieces)
        for j in range(2):
            copies_g[2 * p + j].wait()
            term = jnp.dot(normed[:, lo:hi], gu_v[j, lo:hi, :], preferred_element_type=F32)
            gate_up[j] = term if p == 0 else gate_up[j] + term
    gate, up = gate_up
    active = ((gate / (1.0 + jnp.exp(-gate))) * up).astype(BF16)
    down = None
    for p in range(pieces):
        lo, hi = p * (inner // pieces), (p + 1) * (inner // pieces)
        copies_d[p].wait()
        term = jnp.dot(active[:, lo:hi], wd_v[lo:hi, :], preferred_element_type=F32)
        down = term if p == 0 else down + term
    for p in range(parts):
        mid_s[p] = middle[:, p * cols : (p + 1) * cols]
        down_s[p] = down[:, p * cols : (p + 1) * cols]
    o0[...] = down_s[me] + mid_s[me]
    o1[...] = down_s[me ^ 1]
    o2[...] = down_s[me ^ 2]
    o3[...] = down_s[me ^ 3]


def to_others(values, axis):
    size = lax.axis_size(axis)
    return [
        lax.ppermute(v, axis, [(i, i ^ k) for i in range(size)]) for k, v in zip(range(1, size), values)
    ]


def per_device(inputs, w_qkv, w_out, w_gate_up, w_down, cache_keys, cache_values, lengths):
    reqs, steps, model = inputs.shape
    block = cache_keys.shape[1]
    width = cache_keys.shape[2]
    heads = width // DH
    rows = reqs * steps
    tall = steps * heads
    n_seq = lax.axis_size("seq")
    n_mp = lax.axis_size("mp")
    assert rows == 2 * n_seq and steps == 4 and n_mp == 4 and tall == 16
    group = min(8, reqs)
    in_hbm = functools.partial(pltpu.with_memory_space_constraint, memory_space=pltpu.HBM)
    any_space = pl.BlockSpec(memory_space=pltpu.HBM)
    vmem = pl.BlockSpec(memory_space=pltpu.VMEM)
    w_qkv_hbm = in_hbm(w_qkv)
    part, q_rows, q_own, normed, cosine, sine = pl.pallas_call(
        functools.partial(cached_kernel, group, reqs, steps, block, width),
        out_shape=(
            jax.ShapeDtypeStruct((n_seq, tall, DH), BF16),
            jax.ShapeDtypeStruct((rows, width), BF16),
            jax.ShapeDtypeStruct((tall // 2, DH), F32),
            jax.ShapeDtypeStruct((rows, model), BF16),
            jax.ShapeDtypeStruct((rows, DH), F32),
            jax.ShapeDtypeStruct((rows, DH), F32),
        ),
        in_specs=[any_space] * 5,
        out_specs=(vmem,) * 6,
        scratch_shapes=[
            pltpu.SMEM((reqs,), jnp.int32),
            pltpu.VMEM(inputs.shape, BF16),
            pltpu.VMEM((model, width), BF16),
            pltpu.VMEM(cache_keys.shape, BF16),
            pltpu.VMEM(cache_values.shape, BF16),
            pltpu.VMEM((rows, model), F32),
            pltpu.VMEM((rows * heads, DH), F32),
            pltpu.SemaphoreType.DMA,
            pltpu.SemaphoreType.DMA,
            pltpu.SemaphoreType.DMA,
            pltpu.SemaphoreType.DMA((reqs // group,)),
            pltpu.SemaphoreType.DMA((reqs // group,)),
        ],
        compiler_params=pltpu.CompilerParams(vmem_limit_bytes=48 << 20),
        name="cached_attention",
    )(in_hbm(lengths), in_hbm(inputs), w_qkv_hbm, in_hbm(cache_keys), in_hbm(cache_values))

    piece = jax.ShapeDtypeStruct((reqs, steps, width), BF16)
    queries, new_keys, new_values, fresh, w_proj = pl.pallas_call(
        functools.partial(fresh_kernel, reqs, steps, width),
        out_shape=(
            piece, piece, piece,
            jax.ShapeDtypeStruct((3, tall // 2, DH), F32),
            jax.ShapeDtypeStruct(w_out.shape, BF16),
        ),
        in_specs=[any_space] * 2 + [vmem] * 5,
        out_specs=(vmem,) * 5,
        scratch_shapes=[
            pltpu.VMEM((2, model, width), BF16),
            pltpu.VMEM((rows * heads, DH), F32),
            pltpu.VMEM((rows * heads, DH), F32),
            pltpu.SemaphoreType.DMA((2,)),
            pltpu.SemaphoreType.DMA,
        ],
        compiler_params=pltpu.CompilerParams(vmem_limit_bytes=16 << 20),
        name="new_tokens",
    )(w_qkv_hbm, in_hbm(w_out), q_rows, q_own, normed, cosine, sine)

    got = lax.all_to_all(part, "seq", 0, 0)

    mine = pl.pallas_call(
        merge_kernel,
        out_shape=jax.ShapeDtypeStruct((2, model), F32),
        in_specs=[vmem, vmem, vmem],
        out_specs=vmem,
        scratch_shapes=[pltpu.VMEM((tall // 2, DH), F32)],
        compiler_params=pltpu.CompilerParams(vmem_limit_bytes=8 << 20),
        name="merge_project",
    )(got, fresh, w_proj)
    others = to_others([mine] * 3, "mp")

    cols = model // n_mp
    chunk = jax.ShapeDtypeStruct((2, cols), F32)
    own, *rest = pl.pallas_call(
        mlp_kernel,
        out_shape=(chunk,) * 4,
        in_specs=[any_space] * 3 + [vmem] * 4,
        out_specs=(vmem,) * 4,
        scratch_shapes=[
            pltpu.VMEM((steps, model), BF16),
            pltpu.VMEM(w_gate_up.shape, BF16),
            pltpu.VMEM(w_down.shape, BF16),
            pltpu.VMEM((n_mp, 2, cols), F32),
            pltpu.VMEM((n_mp, 2, cols), F32),
            pltpu.SemaphoreType.DMA,
            pltpu.SemaphoreType.DMA((2, 4)),
            pltpu.SemaphoreType.DMA((4,)),
        ],
        compiler_params=pltpu.CompilerParams(vmem_limit_bytes=20 << 20),
        name="mlp",
    )(in_hbm(inputs), in_hbm(w_gate_up), in_hbm(w_down), mine, *others)
    back = to_others(rest, "mp")
    hidden = ((own + back[0]) + (back[1] + back[2])).astype(BF16)
    hidden = lax.all_to_all(jnp.broadcast_to(hidden[None], (n_seq, 2, cols)), "seq", 0, 0)
    return (hidden.reshape(reqs, steps, cols), queries, new_keys, new_values)


def solution(mesh):
    placed = (
        P(),
        P(None, None, "mp"),
        P("mp", None),
        P(None, None, "mp"),
        P("mp", None),
        P(None, "seq", "mp"),
        P(None, "seq", "mp"),
        P(),
    )
    return jax.shard_map(
        per_device,
        mesh=mesh,
        in_specs=placed,
        out_specs=(P(None, None, "mp"),) * 4,
        check_vma=False,
    )
```

time: 77 us -> 71.9 us (0.934)
  blocking collectives: 41.4 us -> 15.9 us
  starting transfers between devices: 6.75 us -> 19.6 us
  waiting for transfers between devices: 5.56 us -> 15 us
  local copies, waits for them, and re-layouts: 2.45 us -> 0.78 us
    all_to_all x1 -> x0, blocking collectives: 25.6 us -> none  [per_device(): got = lax.all_to_all(part, 'seq', 0, 0)]
    all_to_all x0 -> x1, starting transfers between devices: none -> 12.7 us  [per_device(): got = lax.all_to_all(part, 'seq', 0, 0)]
    all_to_all x0 -> x1, waiting for transfers between devices: none -> 9.4 us  [per_device(): got = lax.all_to_all(part, 'seq', 0, 0)]
    unnamed x12 -> x0, local copies, waits for them, and re-layouts: 0.85 us -> none
    another operation x1 -> x0, local copies, waits for them, and re-layouts: 0.81 us -> none
    pallas_call x2 -> x3, Pallas kernels: 19 us -> 18.8 us  [the longest x1 8.25 us: per_device(): pl.pallas_call(functools.partial(cached_kernel, group, reqs, steps, block...]
  transfers between devices with their start and end apart: 6 -> 7, of which waited for: 4 -> 5; matrix products, arithmetic and copies ran while one was open for 0% -> 0% of each run, Pallas kernels for 0% -> 5%
where the time goes in v2:
time: 71.9 us; the launch traced here: 71.4 us
  starting transfers between devices  19.6 us (27%)
  Pallas kernels  19.5 us (27%)
  blocking collectives  15.9 us (22%)
  waiting for transfers between devices  15 us (21%)
  local copies, waits for them, and re-layouts  0.78 us (1%)
    all_to_all x1, blocking collectives, per_device(): lax.all_to_all(jnp.broadcast_to(hidden[None], (n_seq, 2, cols)), 'seq', 0...  15.9 us
    all_to_all x1, starting transfers between devices, per_device(): got = lax.all_to_all(part, 'seq', 0, 0)  12.7 us
    all_to_all x1, waiting for transfers between devices, per_device(): got = lax.all_to_all(part, 'seq', 0, 0)  9.4 us
    pallas_call x1, Pallas kernels, per_device(): pl.pallas_call(functools.partial(cached_kernel, group, reqs, steps, block...  8.25 us
    pallas_call x1, Pallas kernels, per_device(): pl.pallas_call(mlp_kernel, out_shape=(chunk,) * 4, in_specs=[any_space] *...  6.92 us
    ppermute x6, starting transfers between devices, to_others(): lax.ppermute(v, axis, [(i, i ^ k) for i in range(size)])  6.83 us
    ppermute x6, waiting for transfers between devices, to_others(): lax.ppermute(v, axis, [(i, i ^ k) for i in range(size)])  5.57 us
    pallas_call x1, Pallas kernels, per_device(): pl.pallas_call(functools.partial(fresh_kernel, reqs, steps, width), out_s...  3.63 us
  transfers between devices with their start and end apart: 7, of which 5 were waited for; matrix products, arithmetic and copies ran while one was open for 0% of the time, Pallas kernels for 5%

profile of v2, /device:TPU:4, one launch (start us, length us, event | category | flops | bytes accessed | tf_op | source)
XLA Modules:
  0.0 71.4 jit_solution(9004720601314448847)
XLA Ops:
  0.6 8.2 %cached_attention.1 = (bf16[64,16,128]{2,1,0:T(8,128)(2,1)}, bf16[128,512]{1,0:T(8,128)(2,1)S(1)}, f32[8,128]{1,0:T(8,128)S(1)}, bf16[128,2048]{1,0:T(8,128)(2,1...) custom-call(s32[32]{0:T(128)} %len_hbm.1, bf16[32,4,2048]{2,1,0:T(4,128)(2,1)} %x_hbm.3, ...), custom_call_target="tpu_custom_call" | custom-call | tf_op jit(solution)/shard_map/cached_attention/pallas_call | solution.py:290
  8.9 12.7 %all-to-all-start = ((bf16[64,16,128]{2,1,0:T(8,128)(2,1)}), bf16[64,16,128]{2,1,0:T(8,128)(2,1)S(1)}, u32[]{:S(2)}, u32[]{:S(2)}) async-start(bf16[64,16,128]{2,1,0:T(8,128)(2,1)} %get-tuple-element.19), calls=%async_computation | async-start | bytes 524288 | tf_op jit(solution)/shard_map/all_to_all | solution.py:341
  21.6 3.6 %new_tokens.1 = (bf16[32,4,512]{2,1,0:T(4,128)(2,1)}, bf16[32,4,512]{2,1,0:T(4,128)(2,1)}, bf16[32,4,512]{2,1,0:T(4,128)(2,1)}, f32[3,8,128]{2,1,0:T(8,128)S(1)}, bf16[512,2048]{1,0:T(8,128)(2,1)S(1)}) custom-call(bf16[3,2048,512]{2,1,0:T(8,128)(2,1)} %w_hbm.3, bf16[512,2048]{1,0:T(8,128)(2,1)} %proj_hbm.1, bf16[128,512]{1,0:T(8,128)(2,1)S(1)} %get-tuple-element.20.q_rows, ...), custom_call_target="tpu_custom_call" | custom-call | tf_op jit(solution)/shard_map/new_tokens/pallas_call | solution.py:321
  25.3 9.4 %all-to-all-done.got_ref = bf16[64,16,128]{2,1,0:T(8,128)(2,1)S(1)} async-done(((bf16[64,16,128]{2,1,0:T(8,128)(2,1)}), bf16[64,16,128]{2,1,0:T(8,128)(2,1)S(1)}, u32[]{:S(2)}, u32[]{:S(2)}) %all-to-all-start) | async-done | bytes 262176 | tf_op jit(solution)/shard_map/all_to_all | solution.py:341
  34.7 0.7 merge_project.1.a_ref
  35.4 0.0 collective-permute-start.2
  35.4 0.9 %collective-permute-start.1 = (f32[2,2048]{1,0:T(2,128)S(1)}, f32[2,2048]{1,0:T(2,128)S(1)}, u32[]{:S(2)}, u32[]{:S(2)}) collective-permute-start(f32[2,2048]{1,0:T(2,128)S(1)} %merge_project.1.a_ref), channel_id=1, source_target_pairs={{0,2},{1,3},{2,0},{3,1},{4,6},{5,7},{6,4},{7,5},{8,10},{9,11},{10,... | collective-permute-start | bytes 49160 | tf_op jit(solution)/shard_map/ppermute | solution.py:271
  36.3 2.5 %collective-permute-start = (f32[2,2048]{1,0:T(2,128)S(1)}, f32[2,2048]{1,0:T(2,128)S(1)}, u32[]{:S(2)}, u32[]{:S(2)}) collective-permute-start(f32[2,2048]{1,0:T(2,128)S(1)} %merge_project.1.a_ref), channel_id=1, source_target_pairs={{0,1},{1,0},{2,3},{3,2},{4,5},{5,4},{6,7},{7,6},{8,9},{9,8},{10,11... | collective-permute-start | bytes 49160 | tf_op jit(solution)/shard_map/ppermute | solution.py:271
  38.8 1.3 %collective-permute-done.2.d_ref = f32[2,2048]{1,0:T(2,128)S(1)} collective-permute-done((f32[2,2048]{1,0:T(2,128)S(1)}, f32[2,2048]{1,0:T(2,128)S(1)}, u32[]{:S(2)}, u32[]{:S(2)}) %collective-permute-start.2) | collective-permute-done | bytes 16416 | tf_op jit(solution)/shard_map/ppermute | solution.py:271
  40.1 0.7 collective-permute-done.1.c_ref
  40.8 0.0 collective-permute-done.b_ref
  40.8 6.9 %mlp.1 = (f32[2,512]{1,0:T(2,128)S(1)}, f32[2,512]{1,0:T(2,128)S(1)}, f32[2,512]{1,0:T(2,128)S(1)}, f32[2,512]{1,0:T(2,128)S(1)}) custom-call(bf16[32,4,2048]{2,1,0:T(4,128)(2,1)} %x_hbm.3, bf16[2,2048,1024]{2,1,0:T(8,128)(2,1)} %gu_hbm.1, bf16[1024,2048]{1,0:T(8,128)(2,1)} %wd_hbm.1, f32[2,2048]{1,0:T(2,128)S(1)} %merge_project.1.a_ref, ...), custom_call_target="tpu_custom_call" | custom-call | tf_op jit(solution)/shard_map/mlp/pallas_call | solution.py:356
  47.7 0.1 collective-permute-start.3
  47.8 2.4 %collective-permute-start.4 = (f32[2,512]{1,0:T(2,128)S(1)}, f32[2,512]{1,0:T(2,128)S(1)}, u32[]{:S(2)}, u32[]{:S(2)}) collective-permute-start(f32[2,512]{1,0:T(2,128)S(1)} %get-tuple-element.29), channel_id=1, source_target_pairs={{0,2},{1,3},{2,0},{3,1},{4,6},{5,7},{6,4},{7,5},{8,10},{9,11},{10,... | collective-permute-start | bytes 12296 | tf_op jit(solution)/shard_map/ppermute | solution.py:271
  50.2 1.0 %collective-permute-start.5 = (f32[2,512]{1,0:T(2,128)S(1)}, f32[2,512]{1,0:T(2,128)S(1)}, u32[]{:S(2)}, u32[]{:S(2)}) collective-permute-start(f32[2,512]{1,0:T(2,128)S(1)} %get-tuple-element.30), channel_id=1, source_target_pairs={{0,3},{1,2},{2,1},{3,0},{4,7},{5,6},{6,5},{7,4},{8,11},{9,10},{10,... | collective-permute-start | bytes 12296 | tf_op jit(solution)/shard_map/ppermute | solution.py:271
  51.2 0.0 collective-permute-done.3
  51.2 1.8 %collective-permute-done.4 = f32[2,512]{1,0:T(2,128)S(1)} collective-permute-done((f32[2,512]{1,0:T(2,128)S(1)}, f32[2,512]{1,0:T(2,128)S(1)}, u32[]{:S(2)}, u32[]{:S(2)}) %collective-permute-start.4) | collective-permute-done | bytes 4128 | tf_op jit(solution)/shard_map/ppermute | solution.py:271
  53.0 1.7 %collective-permute-done.5 = f32[2,512]{1,0:T(2,128)S(1)} collective-permute-done((f32[2,512]{1,0:T(2,128)S(1)}, f32[2,512]{1,0:T(2,128)S(1)}, u32[]{:S(2)}, u32[]{:S(2)}) %collective-permute-start.5) | collective-permute-done | bytes 4128 | tf_op jit(solution)/shard_map/ppermute | solution.py:271
  54.7 0.1 broadcast_in_dim.2
  54.8 15.9 %all_to_all.10 = bf16[64,2,512]{2,1,0:T(2,128)(2,1)S(1)} all-to-all(bf16[64,2,512]{2,1,0:T(2,128)(2,1)S(1)} %broadcast_in_dim.2), channel_id=1, replica_groups=mesh['seq'=64,'mp'=4] {'seq'}, dimensions={0} | all-to-all | bytes 262144 | tf_op jit(solution)/shard_map/all_to_all | solution.py:376
  70.7 0.7 reshape.12
  (1 shorter events, 0.0 us)
Async XLA Ops:
  8.9 25.8 %all-to-all-start = ((bf16[64,16,128]{2,1,0:T(8,128)(2,1)}), bf16[64,16,128]{2,1,0:T(8,128)(2,1)S(1)}, u32[]{:S(2)}, u32[]{:S(2)}) async-start(bf16[64,16,128]{2,1,0:T(8,128)(2,1)} %get-tuple-element.19), calls=%async_computation | async-start | bytes 524288 | tf_op jit(solution)/shard_map/all_to_all | solution.py:341
  35.4 4.7 %collective-permute-start.2 = (f32[2,2048]{1,0:T(2,128)S(1)}, f32[2,2048]{1,0:T(2,128)S(1)}, u32[]{:S(2)}, u32[]{:S(2)}) collective-permute-start(f32[2,2048]{1,0:T(2,128)S(1)} %merge_project.1.a_ref), channel_id=1, source_target_pairs={{0,3},{1,2},{2,1},{3,0},{4,7},{5,6},{6,5},{7,4},{8,11},{9,10},{10,... | collective-permute-start | bytes 49160 | tf_op jit(solution)/shard_map/ppermute | solution.py:271
  35.4 5.4 %collective-permute-start.1 = (f32[2,2048]{1,0:T(2,128)S(1)}, f32[2,2048]{1,0:T(2,128)S(1)}, u32[]{:S(2)}, u32[]{:S(2)}) collective-permute-start(f32[2,2048]{1,0:T(2,128)S(1)} %merge_project.1.a_ref), channel_id=1, source_target_pairs={{0,2},{1,3},{2,0},{3,1},{4,6},{5,7},{6,4},{7,5},{8,10},{9,11},{10,... | collective-permute-start | bytes 49160 | tf_op jit(solution)/shard_map/ppermute | solution.py:271
  36.3 4.5 %collective-permute-start = (f32[2,2048]{1,0:T(2,128)S(1)}, f32[2,2048]{1,0:T(2,128)S(1)}, u32[]{:S(2)}, u32[]{:S(2)}) collective-permute-start(f32[2,2048]{1,0:T(2,128)S(1)} %merge_project.1.a_ref), channel_id=1, source_target_pairs={{0,1},{1,0},{2,3},{3,2},{4,5},{5,4},{6,7},{7,6},{8,9},{9,8},{10,11... | collective-permute-start | bytes 49160 | tf_op jit(solution)/shard_map/ppermute | solution.py:271
  47.7 3.5 %collective-permute-start.3 = (f32[2,512]{1,0:T(2,128)S(1)}, f32[2,512]{1,0:T(2,128)S(1)}, u32[]{:S(2)}, u32[]{:S(2)}) collective-permute-start(f32[2,512]{1,0:T(2,128)S(1)} %get-tuple-element.28), channel_id=1, source_target_pairs={{0,1},{1,0},{2,3},{3,2},{4,5},{5,4},{6,7},{7,6},{8,9},{9,8},{10,11... | collective-permute-start | bytes 12296 | tf_op jit(solution)/shard_map/ppermute | solution.py:271
  47.8 5.2 %collective-permute-start.4 = (f32[2,512]{1,0:T(2,128)S(1)}, f32[2,512]{1,0:T(2,128)S(1)}, u32[]{:S(2)}, u32[]{:S(2)}) collective-permute-start(f32[2,512]{1,0:T(2,128)S(1)} %get-tuple-element.29), channel_id=1, source_target_pairs={{0,2},{1,3},{2,0},{3,1},{4,6},{5,7},{6,4},{7,5},{8,10},{9,11},{10,... | collective-permute-start | bytes 12296 | tf_op jit(solution)/shard_map/ppermute | solution.py:271
  50.2 4.6 %collective-permute-start.5 = (f32[2,512]{1,0:T(2,128)S(1)}, f32[2,512]{1,0:T(2,128)S(1)}, u32[]{:S(2)}, u32[]{:S(2)}) collective-permute-start(f32[2,512]{1,0:T(2,128)S(1)} %get-tuple-element.30), channel_id=1, source_target_pairs={{0,3},{1,2},{2,1},{3,0},{4,7},{5,6},{6,5},{7,4},{8,11},{9,10},{10,... | collective-permute-start | bytes 12296 | tf_op jit(solution)/shard_map/ppermute | solution.py:271

commit v3 on v2

v3 whole, which is shorter than its diff:
```python
import functools

import jax
import jax.numpy as jnp
import numpy as np
from jax import lax
from jax.experimental import pallas as pl
from jax.experimental.pallas import tpu as pltpu
from jax.sharding import PartitionSpec as P

DH = 128
NEG = -1e30
EPS = 1e-05
SCALE = DH ** (-0.5)
F32 = jnp.float32
BF16 = jnp.bfloat16
FIRST = 2
LIMIT = 48


def norm_rows(x):
    centred = x - jnp.mean(x, axis=-1, keepdims=True)
    variance = jnp.mean(centred * centred, axis=-1, keepdims=True)
    return centred * lax.rsqrt(variance + EPS)


def split3(v):
    a = v.astype(BF16).astype(F32)
    rest = v - a
    b = rest.astype(BF16).astype(F32)
    return a, b, rest - b


def frequencies():
    half = DH // 2
    values = np.float32(10000.0) ** (np.float32(-2.0) * np.arange(half, dtype=np.float32) / np.float32(DH))
    lane = lax.broadcasted_iota(jnp.int32, (8, DH), 1) % half
    freq = jnp.full((8, DH), float(values[0]), F32)
    for i in range(1, half):
        freq = jnp.where(lane == i, float(values[i]), freq)
    return freq


def turn(v, cosine, sine):
    return v * cosine + pltpu.roll(v, DH // 2, 1) * sine


def rounded(v):
    return v.astype(BF16).astype(F32)


def cached_kernel(
    group, reqs, steps, block, width,
    len_hbm, x_hbm, w_hbm, ck_hbm, cv_hbm,
    part_out, q_rows, q_own, normed_out, cos_out, sin_out,
    len_s, x_v, w_v, ck_v, cv_v, xs, q16, sem_l, sem_x, sem_w, sem_k, sem_v,
):
    heads = width // DH
    rows = reqs * steps
    seq = lax.axis_index("seq")
    copy_l = pltpu.make_async_copy(len_hbm, len_s, sem_l)
    copy_l.start()
    copy_x = pltpu.make_async_copy(x_hbm, x_v, sem_x)
    copy_x.start()
    copy_w = pltpu.make_async_copy(w_hbm.at[0], w_v, sem_w)
    copy_w.start()
    count = reqs // group
    copies = []
    for g in range(count):
        span = pl.ds(g * group, group)
        copies.append(pltpu.make_async_copy(ck_hbm.at[span], ck_v.at[span], sem_k.at[g]))
        copies.append(pltpu.make_async_copy(cv_hbm.at[span], cv_v.at[span], sem_v.at[g]))
    for c in copies[:FIRST]:
        c.start()
    waiting = copies[FIRST:]

    def fetch(number):
        for _ in range(min(number, len(waiting))):
            waiting.pop(0).start()

    copy_l.wait()
    freq = frequencies()
    step_of = (lax.broadcasted_iota(jnp.int32, (8, DH), 0) % steps).astype(F32)
    lane8 = lax.broadcasted_iota(jnp.int32, (8, DH), 1)
    upper = lax.broadcasted_iota(jnp.int32, (8, DH), 0) >= steps
    for r in range(0, reqs, 2):
        place = jnp.where(upper, len_s[r + 1], len_s[r]).astype(F32) + step_of
        angles = place * freq
        cos_out[r * steps : (r + 2) * steps, :] = jnp.cos(angles)
        sine = jnp.sin(angles)
        sin_out[r * steps : (r + 2) * steps, :] = jnp.where(lane8 < DH // 2, -sine, sine)

    copy_x.wait()
    fetch(1)
    for r in range(reqs):
        xs[pl.ds(r * steps, steps), :] = x_v[r].astype(F32)
    normed_out[...] = norm_rows(xs[...]).astype(BF16)

    copy_w.wait()
    fetch(2)
    part = jnp.dot(normed_out[...], w_v[...], preferred_element_type=F32)
    for h in range(heads):
        q = turn(part[:, h * DH : (h + 1) * DH], cos_out[...], sin_out[...]).astype(BF16)
        q_rows[:, h * DH : (h + 1) * DH] = q
        q16[pl.ds(h, rows, stride=heads), :] = q.astype(F32)

    tall = steps * heads
    half = tall // 2
    q_own[...] = q16[pl.ds(seq * half, half), :]
    lane = lax.broadcasted_iota(jnp.int32, (tall, DH), 1)
    many_head = lax.broadcasted_iota(jnp.int32, (group * tall, DH), 0) % heads
    many_lane = lax.broadcasted_iota(jnp.int32, (group * tall, DH), 1)
    for g in range(count):
        q = q16[g * group * tall : (g + 1) * group * tall, :]
        spread = jnp.concatenate([jnp.where(many_head == h, q, 0.0).astype(BF16) for h in range(heads)], axis=1)
        copies[2 * g].wait()
        fetch(1)
        scores = []
        for i in range(group):
            r = g * group + i
            score = lax.dot_general(
                spread[i * tall : (i + 1) * tall], ck_v[r], (((1,), (1,)), ((), ())), preferred_element_type=F32
            )
            scores.append(jnp.where(lane < len_s[r] - seq * block, score * SCALE, NEG))
        scores = jnp.concatenate(scores, axis=0)
        highest = jnp.max(scores, axis=-1, keepdims=True)
        weights = jnp.where(scores == NEG, 0.0, jnp.exp(scores - highest))
        total = jnp.sum(weights, axis=-1, keepdims=True)
        weights = weights.astype(BF16)
        copies[2 * g + 1].wait()
        fetch(1)
        pieces = split3(jnp.broadcast_to(highest, scores.shape)) + split3(jnp.broadcast_to(total, scores.shape))
        stats = pieces[5]
        for i in range(4, -1, -1):
            stats = jnp.where(many_lane == i, pieces[i], stats)
        stats = stats.astype(BF16)
        for i in range(group):
            r = g * group + i
            wide = jnp.dot(weights[i * tall : (i + 1) * tall], cv_v[r], preferred_element_type=F32)
            o = wide[:, 0:DH]
            for h in range(1, heads):
                o = jnp.where(many_head[0:tall] == h, wide[:, h * DH : (h + 1) * DH], o)
            for j in range(2):
                part_out[2 * r + j, 0:half, :] = o[j * half : (j + 1) * half].astype(BF16)
                part_out[2 * r + j, half : 2 * half, :] = stats[i * tall + j * half : i * tall + (j + 1) * half]


def merge_kernel(
    steps,
    got_ref, q_own, normed, cosine, sine, w_qkv, w_ref,
    out_ref,
    k16, v16, ctx_s,
):
    half = q_own.shape[0]
    heads = half // 2
    tall = 2 * half
    seq = lax.axis_index("seq")

    block = pl.multiple_of((seq // 4) * 8, 8)
    rows = normed[pl.ds(block, 8), :]
    keys = jnp.dot(rows, w_qkv[1], preferred_element_type=F32)
    values = jnp.dot(rows, w_qkv[2], preferred_element_type=F32)
    turns = (cosine[pl.ds(block, 8), :], sine[pl.ds(block, 8), :])
    for h in range(heads):
        span = slice(h * DH, (h + 1) * DH)
        k16[pl.ds(h, 8, stride=heads), :] = rounded(turn(keys[:, span], *turns))
        v16[pl.ds(h, 8, stride=heads), :] = rounded(values[:, span])
    q = q_own[...]
    step = (seq % 2) * 2 + lax.broadcasted_iota(jnp.int32, (half, 1), 0) // heads
    base = pl.multiple_of(((seq // 2) % 2) * tall, tall)
    scores = []
    values = []
    for s in range(steps):
        key = k16[pl.ds(base + s * heads, heads), :]
        value = v16[pl.ds(base + s * heads, heads), :]
        key = jnp.concatenate([key, key], axis=0)
        values.append(jnp.concatenate([value, value], axis=0))
        scores.append(jnp.sum(q * key, axis=-1, keepdims=True) * SCALE)
    fresh_high = scores[0]
    for s in range(1, steps):
        fresh_high = jnp.maximum(fresh_high, jnp.where(s <= step, scores[s], NEG))
    fresh_total = jnp.zeros_like(fresh_high)
    fresh = jnp.zeros((half, DH), F32)
    for s in range(steps):
        weight = jnp.where(s <= step, jnp.exp(scores[s] - fresh_high), 0.0)
        fresh_total = fresh_total + weight
        fresh = fresh + rounded(weight) * values[s]

    stats = got_ref[:, half : 2 * half, :].astype(F32)
    highest = (stats[:, :, 0:1] + stats[:, :, 1:2]) + stats[:, :, 2:3]
    total = (stats[:, :, 3:4] + stats[:, :, 4:5]) + stats[:, :, 5:6]
    top = jnp.maximum(jnp.max(highest, axis=0), fresh_high)
    factor = jnp.exp(highest - top[None])
    fresh_factor = jnp.exp(fresh_high - top)
    whole = jnp.sum(factor * total, axis=0) + fresh_factor * fresh_total
    o = jnp.sum(factor * got_ref[:, 0:half, :].astype(F32), axis=0) + fresh_factor * fresh
    ctx_s[...] = o / whole
    ctx = jnp.concatenate([ctx_s[pl.ds(h, 2, stride=heads), :] for h in range(heads)], axis=1)
    out_ref[...] = jnp.dot(ctx.astype(BF16), w_ref[...], preferred_element_type=F32)


def outputs_kernel(
    after_hbm, w_hbm, q_rows, normed, cosine, sine,
    q_out, k_out, v_out,
    w_v, sem_w,
):
    reqs, steps, width = q_out.shape
    copies = [pltpu.make_async_copy(w_hbm.at[1 + j], w_v.at[j], sem_w.at[j]) for j in range(2)]
    for c in copies:
        c.start()
    q_out[...] = q_rows[...].reshape(q_out.shape)
    for j, out in enumerate((k_out, v_out)):
        copies[j].wait()
        part = jnp.dot(normed[...], w_v[j], preferred_element_type=F32)
        for h in range(width // DH):
            v = part[:, h * DH : (h + 1) * DH]
            v = turn(v, cosine[...], sine[...]) if j == 0 else v
            out[:, :, h * DH : (h + 1) * DH] = v.reshape(reqs, steps, DH).astype(BF16)


def mlp_kernel(x_ref, gu_ref, wd_ref, a_ref, b_ref, c_ref, d_ref, o0, o1, o2, o3, mid_s, down_s):
    seq = lax.axis_index("seq")
    me = lax.axis_index("mp")
    parts = down_s.shape[0]
    cols = down_s.shape[2]
    x = x_ref[seq // 2].astype(F32)
    x = jnp.where(seq % 2 == 0, x[0:2], x[2:4])
    middle = x + ((a_ref[...] + b_ref[...]) + (c_ref[...] + d_ref[...]))
    normed = norm_rows(middle).astype(BF16)
    gate = jnp.dot(normed, gu_ref[0], preferred_element_type=F32)
    up = jnp.dot(normed, gu_ref[1], preferred_element_type=F32)
    active = ((gate / (1.0 + jnp.exp(-gate))) * up).astype(BF16)
    down = jnp.dot(active, wd_ref[...], preferred_element_type=F32)
    for p in range(parts):
        mid_s[p] = middle[:, p * cols : (p + 1) * cols]
        down_s[p] = down[:, p * cols : (p + 1) * cols]
    o0[...] = down_s[me] + mid_s[me]
    o1[...] = down_s[me ^ 1]
    o2[...] = down_s[me ^ 2]
    o3[...] = down_s[me ^ 3]


def to_others(values, axis):
    size = lax.axis_size(axis)
    got = [None] * (size - 1)
    for k in range(size - 1, 0, -1):
        got[k - 1] = lax.ppermute(values[k - 1], axis, [(i, i ^ k) for i in range(size)])
    return got


def per_device(inputs, w_qkv, w_out, w_gate_up, w_down, cache_keys, cache_values, lengths):
    reqs, steps, model = inputs.shape
    block = cache_keys.shape[1]
    width = cache_keys.shape[2]
    heads = width // DH
    rows = reqs * steps
    tall = steps * heads
    n_seq = lax.axis_size("seq")
    n_mp = lax.axis_size("mp")
    assert rows == 2 * n_seq and steps == 4 and n_mp == 4 and tall == 16
    group = min(16, reqs)
    in_hbm = functools.partial(pltpu.with_memory_space_constraint, memory_space=pltpu.HBM)
    any_space = pl.BlockSpec(memory_space=pltpu.HBM)
    vmem = pl.BlockSpec(memory_space=pltpu.VMEM)
    part, q_rows, q_own, normed, cosine, sine = pl.pallas_call(
        functools.partial(cached_kernel, group, reqs, steps, block, width),
        out_shape=(
            jax.ShapeDtypeStruct((n_seq, tall, DH), BF16),
            jax.ShapeDtypeStruct((rows, width), BF16),
            jax.ShapeDtypeStruct((tall // 2, DH), F32),
            jax.ShapeDtypeStruct((rows, model), BF16),
            jax.ShapeDtypeStruct((rows, DH), F32),
            jax.ShapeDtypeStruct((rows, DH), F32),
        ),
        in_specs=[any_space] * 5,
        out_specs=(vmem,) * 6,
        scratch_shapes=[
            pltpu.SMEM((reqs,), jnp.int32),
            pltpu.VMEM(inputs.shape, BF16),
            pltpu.VMEM((model, width), BF16),
            pltpu.VMEM(cache_keys.shape, BF16),
            pltpu.VMEM(cache_values.shape, BF16),
            pltpu.VMEM((rows, model), F32),
            pltpu.VMEM((rows * heads, DH), F32),
            pltpu.SemaphoreType.DMA,
            pltpu.SemaphoreType.DMA,
            pltpu.SemaphoreType.DMA,
            pltpu.SemaphoreType.DMA((reqs // group,)),
            pltpu.SemaphoreType.DMA((reqs // group,)),
        ],
        compiler_params=pltpu.CompilerParams(vmem_limit_bytes=LIMIT << 20),
        name="cached_attention",
    )(in_hbm(lengths), in_hbm(inputs), in_hbm(w_qkv), in_hbm(cache_keys), in_hbm(cache_values))

    got = lax.all_to_all(part, "seq", 0, 0)

    mine = pl.pallas_call(
        functools.partial(merge_kernel, steps),
        out_shape=jax.ShapeDtypeStruct((2, model), F32),
        in_specs=[vmem] * 7,
        out_specs=vmem,
        scratch_shapes=[
            pltpu.VMEM((8 * heads, DH), F32),
            pltpu.VMEM((8 * heads, DH), F32),
            pltpu.VMEM((tall // 2, DH), F32),
        ],
        compiler_params=pltpu.CompilerParams(vmem_limit_bytes=8 << 20),
        name="merge_project",
    )(got, q_own, normed, cosine, sine, w_qkv, w_out)
    others = to_others([mine] * 3, "mp")

    piece = jax.ShapeDtypeStruct((reqs, steps, width), BF16)
    queries, new_keys, new_values = pl.pallas_call(
        outputs_kernel,
        out_shape=(piece,) * 3,
        in_specs=[any_space] * 2 + [vmem] * 4,
        out_specs=(vmem,) * 3,
        scratch_shapes=[pltpu.VMEM((2, model, width), BF16), pltpu.SemaphoreType.DMA((2,))],
        compiler_params=pltpu.CompilerParams(vmem_limit_bytes=12 << 20),
        name="projections",
    )(mine, in_hbm(w_qkv), q_rows, normed, cosine, sine)

    cols = model // n_mp
    chunk = jax.ShapeDtypeStruct((2, cols), F32)
    own, *rest = pl.pallas_call(
        mlp_kernel,
        out_shape=(chunk,) * 4,
        in_specs=[vmem] * 7,
        out_specs=(vmem,) * 4,
        scratch_shapes=[pltpu.VMEM((n_mp, 2, cols), F32)] * 2,
        compiler_params=pltpu.CompilerParams(vmem_limit_bytes=8 << 20),
        name="mlp",
    )(inputs, w_gate_up, w_down, mine, *others)
    back = to_others(rest, "mp")
    hidden = ((own + back[0]) + (back[1] + back[2])).astype(BF16)
    hidden = lax.all_to_all(jnp.broadcast_to(hidden[None], (n_seq, 2, cols)), "seq", 0, 0)
    return (hidden.reshape(reqs, steps, cols), queries, new_keys, new_values)


def solution(mesh):
    placed = (
        P(),
        P(None, None, "mp"),
        P("mp", None),
        P(None, None, "mp"),
        P("mp", None),
        P(None, "seq", "mp"),
        P(None, "seq", "mp"),
        P(),
    )
    return jax.shard_map(
        per_device,
        mesh=mesh,
        in_specs=placed,
        out_specs=(P(None, None, "mp"),) * 4,
        check_vma=False,
    )
```

time: 71.9 us -> 65.2 us (0.907)
  blocking collectives: 15.9 us -> 25.8 us
  starting transfers between devices: 19.6 us -> 11.6 us
  Pallas kernels: 19.5 us -> 11.7 us
  waiting for transfers between devices: 15 us -> 13.4 us
    all_to_all x1, blocking collectives: 15.9 us -> 25.8 us  [per_device(): got = lax.all_to_all(part, 'seq', 0, 0)]
    all_to_all x1, starting transfers between devices: 12.7 us -> 4.87 us  [per_device(): lax.all_to_all(jnp.broadcast_to(hidden[None], (n_seq, 2, cols)), 'seq', 0...]
    pallas_call x3, Pallas kernels: 11.3 us -> 6.44 us  [the longest x1 3.35 us: per_device(): pl.pallas_call(outputs_kernel, out_shape=(piece,) * 3, in_specs=[any_spac...]
    pallas_call x1, Pallas kernels: 8.25 us -> 5.26 us  [per_device(): pl.pallas_call(functools.partial(cached_kernel, group, reqs, steps, block...]
    all_to_all x1, waiting for transfers between devices: 9.4 us -> 7.86 us  [per_device(): lax.all_to_all(jnp.broadcast_to(hidden[None], (n_seq, 2, cols)), 'seq', 0...]
where the time goes in v3:
time: 65.2 us; the launch traced here: 64.8 us
  blocking collectives  25.8 us (40%)
  waiting for transfers between devices  13.4 us (21%)
  Pallas kernels  11.7 us (18%)
  starting transfers between devices  11.6 us (18%)
  local copies, waits for them, and re-layouts  1.46 us (2%)
  between operations  0.72 us (1%)
    all_to_all x1, blocking collectives, per_device(): got = lax.all_to_all(part, 'seq', 0, 0)  25.8 us
    all_to_all x1, waiting for transfers between devices, per_device(): lax.all_to_all(jnp.broadcast_to(hidden[None], (n_seq, 2, cols)), 'seq', 0...  7.86 us
    ppermute x6, starting transfers between devices, to_others(): lax.ppermute(values[k - 1], axis, [(i, i ^ k) for i in range(size)])  6.75 us
    ppermute x6, waiting for transfers between devices, to_others(): lax.ppermute(values[k - 1], axis, [(i, i ^ k) for i in range(size)])  5.56 us
    pallas_call x1, Pallas kernels, per_device(): pl.pallas_call(functools.partial(cached_kernel, group, reqs, steps, block...  5.26 us
    all_to_all x1, starting transfers between devices, per_device(): lax.all_to_all(jnp.broadcast_to(hidden[None], (n_seq, 2, cols)), 'seq', 0...  4.87 us
    pallas_call x1, Pallas kernels, per_device(): pl.pallas_call(outputs_kernel, out_shape=(piece,) * 3, in_specs=[any_spac...  3.35 us
    pallas_call x1, Pallas kernels, per_device(): pl.pallas_call(mlp_kernel, out_shape=(chunk,) * 4, in_specs=[vmem] * 7, o...  1.95 us
  transfers between devices with their start and end apart: 7, of which 5 were waited for; matrix products, arithmetic and copies ran while one was open for 0% of the time, Pallas kernels for 5%

profile of v3, /device:TPU:4, one launch (start us, length us, event | category | flops | bytes accessed | tf_op | source)
XLA Modules:
  0.0 64.8 jit_solution(14373299340298771915)
XLA Ops:
  0.6 0.0 copy-start
  0.6 0.0 copy-start.4
  0.7 0.0 copy-start.2
  0.7 5.3 %cached_attention.1 = (bf16[64,16,128]{2,1,0:T(8,128)(2,1)S(1)}, bf16[128,512]{1,0:T(8,128)(2,1)S(1)}, f32[8,128]{1,0:T(8,128)S(1)}, bf16[128,2048]{1,0:T(8,128)...) custom-call(s32[32]{0:T(128)} %len_hbm.1, bf16[32,4,2048]{2,1,0:T(4,128)(2,1)} %x_ref.1, ...), custom_call_target="tpu_custom_call" | custom-call | tf_op jit(solution)/shard_map/cached_attention/pallas_call | solution.py:265
  5.9 25.8 %all_to_all.10.got_ref = bf16[64,16,128]{2,1,0:T(8,128)(2,1)S(1)} all-to-all(bf16[64,16,128]{2,1,0:T(8,128)(2,1)S(1)} %get-tuple-element.17), channel_id=1, replica_groups=mesh['seq'=64,'mp'=4] {'seq'}, dimensions={0} | all-to-all | bytes 524288 | tf_op jit(solution)/shard_map/all_to_all | solution.py:295
  31.8 0.0 copy-done
  31.8 0.0 copy-done.4
  31.8 0.0 copy-start.1
  31.8 0.0 copy-start.3
  31.8 1.1 %merge_project.1.a_ref.after_hbm = f32[2,2048]{1,0:T(2,128)S(1)} custom-call(bf16[64,16,128]{2,1,0:T(8,128)(2,1)S(1)} %all_to_all.10.got_ref, f32[8,128]{1,0:T(8,128)S(1)} %get-tuple-element.18.q_own, bf16[128,2048]{1,0:T(8,128)(2,1)S(1)} %get-tuple-element.19.normed, f32[128,128]{1,0:T(8,128)S(1)} %get-tuple-element.20.cosine, ...), custom_call_target="tpu_custom_call" | custom-call | tf_op jit(solution)/shard_map/merge_project/pallas_call | solution.py:297
  32.9 0.0 collective-permute-start.2
  33.0 0.9 %collective-permute-start.1 = (f32[2,2048]{1,0:T(2,128)S(1)}, f32[2,2048]{1,0:T(2,128)S(1)}, u32[]{:S(2)}, u32[]{:S(2)}) collective-permute-start(f32[2,2048]{1,0:T(2,128)S(1)} %merge_project.1.a_ref.after_hbm), channel_id=1, source_target_pairs={{0,2},{1,3},{2,0},{3,1},{4,6},{5,7},{6,4},{7,5},{8,10},{9,11},{10,... | collective-permute-start | bytes 49160 | tf_op jit(solution)/shard_map/ppermute | solution.py:247
  33.8 2.5 %collective-permute-start = (f32[2,2048]{1,0:T(2,128)S(1)}, f32[2,2048]{1,0:T(2,128)S(1)}, u32[]{:S(2)}, u32[]{:S(2)}) collective-permute-start(f32[2,2048]{1,0:T(2,128)S(1)} %merge_project.1.a_ref.after_hbm), channel_id=1, source_target_pairs={{0,1},{1,0},{2,3},{3,2},{4,5},{5,4},{6,7},{7,6},{8,9},{9,8},{10,11... | collective-permute-start | bytes 49160 | tf_op jit(solution)/shard_map/ppermute | solution.py:247
  36.3 1.3 %collective-permute-done.2.d_ref = f32[2,2048]{1,0:T(2,128)S(1)} collective-permute-done((f32[2,2048]{1,0:T(2,128)S(1)}, f32[2,2048]{1,0:T(2,128)S(1)}, u32[]{:S(2)}, u32[]{:S(2)}) %collective-permute-start.2) | collective-permute-done | bytes 16416 | tf_op jit(solution)/shard_map/ppermute | solution.py:247
  37.6 0.7 %collective-permute-done.1.c_ref = f32[2,2048]{1,0:T(2,128)S(1)} collective-permute-done((f32[2,2048]{1,0:T(2,128)S(1)}, f32[2,2048]{1,0:T(2,128)S(1)}, u32[]{:S(2)}, u32[]{:S(2)}) %collective-permute-start.1) | collective-permute-done | bytes 16416 | tf_op jit(solution)/shard_map/ppermute | solution.py:247
  38.3 0.0 collective-permute-done.b_ref
  38.3 0.0 copy-done.2
  38.3 0.0 copy-done.1
  38.3 0.0 copy-done.3
  38.3 1.9 %mlp.1 = (f32[2,512]{1,0:T(2,128)S(1)}, f32[2,512]{1,0:T(2,128)S(1)}, f32[2,512]{1,0:T(2,128)S(1)}, f32[2,512]{1,0:T(2,128)S(1)}) custom-call(bf16[32,4,2048]{2,1,0:T(4,128)(2,1)S(1)} %copy-done.3, bf16[2,2048,1024]{2,1,0:T(8,128)(2,1)S(1)} %copy-done.1, bf16[1024,2048]{1,0:T(8,128)(2,1)S(1)} %copy-done.2, f32[2,2048]{1,0:T(2,128)S(1)} %merge_project.1.a_ref.after_hbm, ...), custom_call_target="tpu_custom_call" | custom-call | tf_op jit(solution)/shard_map/mlp/pallas_call | solution.py:325
  40.3 0.0 collective-permute-start.3
  40.3 2.4 %collective-permute-start.4 = (f32[2,512]{1,0:T(2,128)S(1)}, f32[2,512]{1,0:T(2,128)S(1)}, u32[]{:S(2)}, u32[]{:S(2)}) collective-permute-start(f32[2,512]{1,0:T(2,128)S(1)} %get-tuple-element.24), channel_id=1, source_target_pairs={{0,2},{1,3},{2,0},{3,1},{4,6},{5,7},{6,4},{7,5},{8,10},{9,11},{10,... | collective-permute-start | bytes 12296 | tf_op jit(solution)/shard_map/ppermute | solution.py:247
  42.7 1.0 %collective-permute-start.5 = (f32[2,512]{1,0:T(2,128)S(1)}, f32[2,512]{1,0:T(2,128)S(1)}, u32[]{:S(2)}, u32[]{:S(2)}) collective-permute-start(f32[2,512]{1,0:T(2,128)S(1)} %get-tuple-element.25), channel_id=1, source_target_pairs={{0,3},{1,2},{2,1},{3,0},{4,7},{5,6},{6,5},{7,4},{8,11},{9,10},{10,... | collective-permute-start | bytes 12296 | tf_op jit(solution)/shard_map/ppermute | solution.py:247
  43.7 0.0 collective-permute-done.3
  43.7 1.8 %collective-permute-done.4 = f32[2,512]{1,0:T(2,128)S(1)} collective-permute-done((f32[2,512]{1,0:T(2,128)S(1)}, f32[2,512]{1,0:T(2,128)S(1)}, u32[]{:S(2)}, u32[]{:S(2)}) %collective-permute-start.4) | collective-permute-done | bytes 4128 | tf_op jit(solution)/shard_map/ppermute | solution.py:247
  45.5 1.7 %collective-permute-done.5 = f32[2,512]{1,0:T(2,128)S(1)} collective-permute-done((f32[2,512]{1,0:T(2,128)S(1)}, f32[2,512]{1,0:T(2,128)S(1)}, u32[]{:S(2)}, u32[]{:S(2)}) %collective-permute-start.5) | collective-permute-done | bytes 4128 | tf_op jit(solution)/shard_map/ppermute | solution.py:247
  47.2 0.7 %broadcast_in_dim.2 = bf16[64,2,512]{2,1,0:T(2,128)(2,1)} broadcast(bf16[2,512]{1,0:T(2,128)(2,1)S(1)} %add_convert_fusion), dimensions={1,2} | broadcast | bytes 133120 | tf_op jit(solution)/shard_map/broadcast_in_dim | solution.py:336
  48.0 4.9 %all-to-all-start.1 = ((bf16[64,2,512]{2,1,0:T(2,128)(2,1)}), bf16[64,2,512]{2,1,0:T(2,128)(2,1)S(1)}, u32[]{:S(2)}, u32[]{:S(2)}) async-start(bf16[64,2,512]{2,1,0:T(2,128)(2,1)} %broadcast_in_dim.2), calls=%async_computation.1 | async-start | bytes 262144 | tf_op jit(solution)/shard_map/all_to_all | solution.py:336
  52.8 3.4 %projections.1 = (bf16[32,4,512]{2,1,0:T(4,128)(2,1)}, bf16[32,4,512]{2,1,0:T(4,128)(2,1)}, bf16[32,4,512]{2,1,0:T(4,128)(2,1)}) custom-call(f32[2,2048]{1,0:T(2,128)S(1)} %merge_project.1.a_ref.after_hbm, bf16[3,2048,512]{2,1,0:T(8,128)(2,1)} %w_hbm.3, bf16[128,512]{1,0:T(8,128)(2,1)S(1)} %get-tuple-element.26.q_rows, ...), custom_call_target="tpu_custom_call" | custom-call | tf_op jit(solution)/shard_map/projections/pallas_call | solution.py:313
  56.2 7.9 %all-to-all-done.1 = bf16[64,2,512]{2,1,0:T(2,128)(2,1)S(1)} async-done(((bf16[64,2,512]{2,1,0:T(2,128)(2,1)}), bf16[64,2,512]{2,1,0:T(2,128)(2,1)S(1)}, u32[]{:S(2)}, u32[]{:S(2)}) %all-to-all-start.1) | async-done | bytes 131104 | tf_op jit(solution)/shard_map/all_to_all | solution.py:336
  64.1 0.7 %reshape.12 = bf16[32,4,512]{2,1,0:T(4,128)(2,1)} reshape(bf16[64,2,512]{2,1,0:T(2,128)(2,1)S(1)} %all-to-all-done.1) | data formatting | bytes 262144 | tf_op jit(solution)/shard_map/reshape | solution.py:337
  (1 shorter events, 0.0 us)
Async XLA Ops:
  0.6 31.1 %copy-start = (bf16[3,2048,512]{2,1,0:T(8,128)(2,1)S(1)}, bf16[3,2048,512]{2,1,0:T(8,128)(2,1)}, u32[]{:S(2)}) copy-start(bf16[3,2048,512]{2,1,0:T(8,128)(2,1)} %w_hbm.3) | copy-start | bytes 18874372
  0.6 31.1 %copy-start.4 = (bf16[512,2048]{1,0:T(8,128)(2,1)S(1)}, bf16[512,2048]{1,0:T(8,128)(2,1)}, u32[]{:S(2)}) copy-start(bf16[512,2048]{1,0:T(8,128)(2,1)} %w_ref.1) | copy-start | bytes 6291460
  0.7 37.7 %copy-start.2 = (bf16[1024,2048]{1,0:T(8,128)(2,1)S(1)}, bf16[1024,2048]{1,0:T(8,128)(2,1)}, u32[]{:S(2)}) copy-start(bf16[1024,2048]{1,0:T(8,128)(2,1)} %wd_ref.1) | copy-start | bytes 12582916
  31.8 6.5 %copy-start.1 = (bf16[2,2048,1024]{2,1,0:T(8,128)(2,1)S(1)}, bf16[2,2048,1024]{2,1,0:T(8,128)(2,1)}, u32[]{:S(2)}) copy-start(bf16[2,2048,1024]{2,1,0:T(8,128)(2,1)} %gu_ref.1) | copy-start | bytes 25165828
  31.8 6.5 %copy-start.3 = (bf16[32,4,2048]{2,1,0:T(4,128)(2,1)S(1)}, bf16[32,4,2048]{2,1,0:T(4,128)(2,1)}, u32[]{:S(2)}) copy-start(bf16[32,4,2048]{2,1,0:T(4,128)(2,1)} %x_ref.1) | copy-start | bytes 1572868
  32.9 4.7 %collective-permute-start.2 = (f32[2,2048]{1,0:T(2,128)S(1)}, f32[2,2048]{1,0:T(2,128)S(1)}, u32[]{:S(2)}, u32[]{:S(2)}) collective-permute-start(f32[2,2048]{1,0:T(2,128)S(1)} %merge_project.1.a_ref.after_hbm), channel_id=1, source_target_pairs={{0,3},{1,2},{2,1},{3,0},{4,7},{5,6},{6,5},{7,4},{8,11},{9,10},{10,... | collective-permute-start | bytes 49160 | tf_op jit(solution)/shard_map/ppermute | solution.py:247
  33.0 5.4 %collective-permute-start.1 = (f32[2,2048]{1,0:T(2,128)S(1)}, f32[2,2048]{1,0:T(2,128)S(1)}, u32[]{:S(2)}, u32[]{:S(2)}) collective-permute-start(f32[2,2048]{1,0:T(2,128)S(1)} %merge_project.1.a_ref.after_hbm), channel_id=1, source_target_pairs={{0,2},{1,3},{2,0},{3,1},{4,6},{5,7},{6,4},{7,5},{8,10},{9,11},{10,... | collective-permute-start | bytes 49160 | tf_op jit(solution)/shard_map/ppermute | solution.py:247
  33.8 4.5 %collective-permute-start = (f32[2,2048]{1,0:T(2,128)S(1)}, f32[2,2048]{1,0:T(2,128)S(1)}, u32[]{:S(2)}, u32[]{:S(2)}) collective-permute-start(f32[2,2048]{1,0:T(2,128)S(1)} %merge_project.1.a_ref.after_hbm), channel_id=1, source_target_pairs={{0,1},{1,0},{2,3},{3,2},{4,5},{5,4},{6,7},{7,6},{8,9},{9,8},{10,11... | collective-permute-start | bytes 49160 | tf_op jit(solution)/shard_map/ppermute | solution.py:247
  40.3 3.4 %collective-permute-start.3 = (f32[2,512]{1,0:T(2,128)S(1)}, f32[2,512]{1,0:T(2,128)S(1)}, u32[]{:S(2)}, u32[]{:S(2)}) collective-permute-start(f32[2,512]{1,0:T(2,128)S(1)} %get-tuple-element.23), channel_id=1, source_target_pairs={{0,1},{1,0},{2,3},{3,2},{4,5},{5,4},{6,7},{7,6},{8,9},{9,8},{10,11... | collective-permute-start | bytes 12296 | tf_op jit(solution)/shard_map/ppermute | solution.py:247
  40.3 5.2 %collective-permute-start.4 = (f32[2,512]{1,0:T(2,128)S(1)}, f32[2,512]{1,0:T(2,128)S(1)}, u32[]{:S(2)}, u32[]{:S(2)}) collective-permute-start(f32[2,512]{1,0:T(2,128)S(1)} %get-tuple-element.24), channel_id=1, source_target_pairs={{0,2},{1,3},{2,0},{3,1},{4,6},{5,7},{6,4},{7,5},{8,10},{9,11},{10,... | collective-permute-start | bytes 12296 | tf_op jit(solution)/shard_map/ppermute | solution.py:247
  42.7 4.6 %collective-permute-start.5 = (f32[2,512]{1,0:T(2,128)S(1)}, f32[2,512]{1,0:T(2,128)S(1)}, u32[]{:S(2)}, u32[]{:S(2)}) collective-permute-start(f32[2,512]{1,0:T(2,128)S(1)} %get-tuple-element.25), channel_id=1, source_target_pairs={{0,3},{1,2},{2,1},{3,0},{4,7},{5,6},{6,5},{7,4},{8,11},{9,10},{10,... | collective-permute-start | bytes 12296 | tf_op jit(solution)/shard_map/ppermute | solution.py:247
  48.0 16.1 %all-to-all-start.1 = ((bf16[64,2,512]{2,1,0:T(2,128)(2,1)}), bf16[64,2,512]{2,1,0:T(2,128)(2,1)S(1)}, u32[]{:S(2)}, u32[]{:S(2)}) async-start(bf16[64,2,512]{2,1,0:T(2,128)(2,1)} %broadcast_in_dim.2), calls=%async_computation.1 | async-start | bytes 262144 | tf_op jit(solution)/shard_map/all_to_all | solution.py:336

commit v4 on v3

--- a/solution.py
+++ b/solution.py
@@ -218,26 +218,25 @@
             out[:, :, h * DH : (h + 1) * DH] = v.reshape(reqs, steps, DH).astype(BF16)
 
 
-def mlp_kernel(x_ref, gu_ref, wd_ref, a_ref, b_ref, c_ref, d_ref, o0, o1, o2, o3, mid_s, down_s):
+def mlp_kernel(x_ref, gu_ref, wd_ref, a_ref, b_ref, c_ref, d_ref, middle_out, down_out):
     seq = lax.axis_index("seq")
-    me = lax.axis_index("mp")
-    parts = down_s.shape[0]
-    cols = down_s.shape[2]
     x = x_ref[seq // 2].astype(F32)
     x = jnp.where(seq % 2 == 0, x[0:2], x[2:4])
     middle = x + ((a_ref[...] + b_ref[...]) + (c_ref[...] + d_ref[...]))
+    middle_out[...] = middle
     normed = norm_rows(middle).astype(BF16)
     gate = jnp.dot(normed, gu_ref[0], preferred_element_type=F32)
     up = jnp.dot(normed, gu_ref[1], preferred_element_type=F32)
     active = ((gate / (1.0 + jnp.exp(-gate))) * up).astype(BF16)
-    down = jnp.dot(active, wd_ref[...], preferred_element_type=F32)
-    for p in range(parts):
-        mid_s[p] = middle[:, p * cols : (p + 1) * cols]
-        down_s[p] = down[:, p * cols : (p + 1) * cols]
-    o0[...] = down_s[me] + mid_s[me]
-    o1[...] = down_s[me ^ 1]
-    o2[...] = down_s[me ^ 2]
-    o3[...] = down_s[me ^ 3]
+    down_out[...] = jnp.dot(active, wd_ref[...], preferred_element_type=F32)
+
+
+def last_kernel(middle_ref, a_ref, b_ref, c_ref, d_ref, out_ref):
+    cols = out_ref.shape[2]
+    span = pl.ds(pl.multiple_of(lax.axis_index("mp") * cols, cols), cols)
+    down = (a_ref[:, span] + b_ref[:, span]) + (c_ref[:, span] + d_ref[:, span])
+    hidden = (middle_ref[:, span] + down).astype(BF16)
+    out_ref[...] = jnp.broadcast_to(hidden[None], out_ref.shape)
 
 
 def to_others(values, axis):
@@ -321,19 +320,24 @@
     )(mine, in_hbm(w_qkv), q_rows, normed, cosine, sine)
 
     cols = model // n_mp
-    chunk = jax.ShapeDtypeStruct((2, cols), F32)
-    own, *rest = pl.pallas_call(
+    rows2 = jax.ShapeDtypeStruct((2, model), F32)
+    middle, down = pl.pallas_call(
         mlp_kernel,
-        out_shape=(chunk,) * 4,
+        out_shape=(rows2,) * 2,
         in_specs=[vmem] * 7,
-        out_specs=(vmem,) * 4,
-        scratch_shapes=[pltpu.VMEM((n_mp, 2, cols), F32)] * 2,
+        out_specs=(vmem,) * 2,
         compiler_params=pltpu.CompilerParams(vmem_limit_bytes=8 << 20),
         name="mlp",
     )(inputs, w_gate_up, w_down, mine, *others)
-    back = to_others(rest, "mp")
-    hidden = ((own + back[0]) + (back[1] + back[2])).astype(BF16)
-    hidden = lax.all_to_all(jnp.broadcast_to(hidden[None], (n_seq, 2, cols)), "seq", 0, 0)
+    hidden = pl.pallas_call(
+        last_kernel,
+        out_shape=jax.ShapeDtypeStruct((n_seq, 2, cols), BF16),
+        in_specs=[vmem] * 5,
+        out_specs=vmem,
+        compiler_params=pltpu.CompilerParams(vmem_limit_bytes=4 << 20),
+        name="last_sum",
+    )(middle, down, *to_others([down] * 3, "mp"))
+    hidden = lax.all_to_all(hidden, "seq", 0, 0)
     return (hidden.reshape(reqs, steps, cols), queries, new_keys, new_values)
 
 

time: 65.2 us -> 65 us (level)
  local copies, waits for them, and re-layouts: 1.46 us -> 0.73 us
  Pallas kernels: 11.7 us -> 12.4 us
    broadcast_in_dim x1 -> x0, local copies, waits for them, and re-layouts: 0.73 us -> none  [per_device(): jnp.broadcast_to(hidden[None], (n_seq, 2, cols))]
    pallas_call x1 -> x2, Pallas kernels: 1.95 us -> 2.65 us  [the longest x1 1.94 us: per_device(): pl.pallas_call(mlp_kernel, out_shape=(rows2,) * 2, in_specs=[vmem] * 7, o...]
where the time goes in v4:
time: 65 us; the launch traced here: 64.8 us
  blocking collectives  25.8 us (40%)
  waiting for transfers between devices  13.5 us (21%)
  Pallas kernels  12.4 us (19%)
  starting transfers between devices  11.6 us (18%)
  local copies, waits for them, and re-layouts  0.73 us (1%)
  between operations  0.72 us (1%)
    all_to_all x1, blocking collectives, per_device(): got = lax.all_to_all(part, 'seq', 0, 0)  25.8 us
    all_to_all x1, waiting for transfers between devices, per_device(): hidden = lax.all_to_all(hidden, 'seq', 0, 0)  7.67 us
    ppermute x6, starting transfers between devices, to_others(): lax.ppermute(values[k - 1], axis, [(i, i ^ k) for i in range(size)])  6.74 us
    ppermute x6, waiting for transfers between devices, to_others(): lax.ppermute(values[k - 1], axis, [(i, i ^ k) for i in range(size)])  5.86 us
    pallas_call x1, Pallas kernels, per_device(): pl.pallas_call(functools.partial(cached_kernel, group, reqs, steps, block...  5.26 us
    all_to_all x1, starting transfers between devices, per_device(): hidden = lax.all_to_all(hidden, 'seq', 0, 0)  4.87 us
    pallas_call x1, Pallas kernels, per_device(): pl.pallas_call(outputs_kernel, out_shape=(piece,) * 3, in_specs=[any_spac...  3.35 us
    pallas_call x1, Pallas kernels, per_device(): pl.pallas_call(mlp_kernel, out_shape=(rows2,) * 2, in_specs=[vmem] * 7, o...  1.94 us
  transfers between devices with their start and end apart: 7, of which 5 were waited for; matrix products, arithmetic and copies ran while one was open for 0% of the time, Pallas kernels for 5%

profile of v4, /device:TPU:4, one launch (start us, length us, event | category | flops | bytes accessed | tf_op | source)
XLA Modules:
  0.0 64.8 jit_solution(1001444744127662786)
XLA Ops:
  0.6 0.0 copy-start
  0.6 0.0 copy-start.4
  0.7 0.0 copy-start.2
  0.7 5.3 %cached_attention.1 = (bf16[64,16,128]{2,1,0:T(8,128)(2,1)S(1)}, bf16[128,512]{1,0:T(8,128)(2,1)S(1)}, f32[8,128]{1,0:T(8,128)S(1)}, bf16[128,2048]{1,0:T(8,128)...) custom-call(s32[32]{0:T(128)} %len_hbm.1, bf16[32,4,2048]{2,1,0:T(4,128)(2,1)} %x_ref.1, ...), custom_call_target="tpu_custom_call" | custom-call | tf_op jit(solution)/shard_map/cached_attention/pallas_call | solution.py:264
  5.9 25.8 %all_to_all.10.got_ref = bf16[64,16,128]{2,1,0:T(8,128)(2,1)S(1)} all-to-all(bf16[64,16,128]{2,1,0:T(8,128)(2,1)S(1)} %get-tuple-element.15), channel_id=1, replica_groups=mesh['seq'=64,'mp'=4] {'seq'}, dimensions={0} | all-to-all | bytes 524288 | tf_op jit(solution)/shard_map/all_to_all | solution.py:294
  31.8 0.0 copy-done
  31.8 0.0 copy-done.4
  31.8 0.0 copy-start.1
  31.8 0.0 copy-start.3
  31.8 1.1 %merge_project.1.a_ref.after_hbm = f32[2,2048]{1,0:T(2,128)S(1)} custom-call(bf16[64,16,128]{2,1,0:T(8,128)(2,1)S(1)} %all_to_all.10.got_ref, f32[8,128]{1,0:T(8,128)S(1)} %get-tuple-element.16.q_own, bf16[128,2048]{1,0:T(8,128)(2,1)S(1)} %get-tuple-element.17.normed, f32[128,128]{1,0:T(8,128)S(1)} %get-tuple-element.18.cosine, ...), custom_call_target="tpu_custom_call" | custom-call | tf_op jit(solution)/shard_map/merge_project/pallas_call | solution.py:296
  32.9 0.0 collective-permute-start.2
  33.0 0.9 %collective-permute-start.1 = (f32[2,2048]{1,0:T(2,128)S(1)}, f32[2,2048]{1,0:T(2,128)S(1)}, u32[]{:S(2)}, u32[]{:S(2)}) collective-permute-start(f32[2,2048]{1,0:T(2,128)S(1)} %merge_project.1.a_ref.after_hbm), channel_id=1, source_target_pairs={{0,2},{1,3},{2,0},{3,1},{4,6},{5,7},{6,4},{7,5},{8,10},{9,11},{10,... | collective-permute-start | bytes 49160 | tf_op jit(solution)/shard_map/ppermute | solution.py:246
  33.8 2.5 %collective-permute-start = (f32[2,2048]{1,0:T(2,128)S(1)}, f32[2,2048]{1,0:T(2,128)S(1)}, u32[]{:S(2)}, u32[]{:S(2)}) collective-permute-start(f32[2,2048]{1,0:T(2,128)S(1)} %merge_project.1.a_ref.after_hbm), channel_id=1, source_target_pairs={{0,1},{1,0},{2,3},{3,2},{4,5},{5,4},{6,7},{7,6},{8,9},{9,8},{10,11... | collective-permute-start | bytes 49160 | tf_op jit(solution)/shard_map/ppermute | solution.py:246
  36.3 1.3 %collective-permute-done.2.d_ref = f32[2,2048]{1,0:T(2,128)S(1)} collective-permute-done((f32[2,2048]{1,0:T(2,128)S(1)}, f32[2,2048]{1,0:T(2,128)S(1)}, u32[]{:S(2)}, u32[]{:S(2)}) %collective-permute-start.2) | collective-permute-done | bytes 16416 | tf_op jit(solution)/shard_map/ppermute | solution.py:246
  37.6 0.7 %collective-permute-done.1.c_ref = f32[2,2048]{1,0:T(2,128)S(1)} collective-permute-done((f32[2,2048]{1,0:T(2,128)S(1)}, f32[2,2048]{1,0:T(2,128)S(1)}, u32[]{:S(2)}, u32[]{:S(2)}) %collective-permute-start.1) | collective-permute-done | bytes 16416 | tf_op jit(solution)/shard_map/ppermute | solution.py:246
  38.3 0.0 collective-permute-done.b_ref
  38.3 0.0 copy-done.2
  38.3 0.0 copy-done.1
  38.3 0.0 copy-done.3
  38.3 1.9 %mlp.1 = (f32[2,2048]{1,0:T(2,128)S(1)}, f32[2,2048]{1,0:T(2,128)S(1)}) custom-call(bf16[32,4,2048]{2,1,0:T(4,128)(2,1)S(1)} %copy-done.3, bf16[2,2048,1024]{2,1,0:T(8,128)(2,1)S(1)} %copy-done.1, bf16[1024,2048]{1,0:T(8,128)(2,1)S(1)} %copy-done.2, f32[2,2048]{1,0:T(2,128)S(1)} %merge_project.1.a_ref.after_hbm, f32[2,2048]{1,0:T(2,128)S(1)} %collective-permute-done.b_ref, ...), custom_call_target="tpu_custom_call" | custom-call | tf_op jit(solution)/shard_map/mlp/pallas_call | solution.py:324
  40.3 2.0 %collective-permute-start.5 = (f32[2,2048]{1,0:T(2,128)S(1)}, f32[2,2048]{1,0:T(2,128)S(1)}, u32[]{:S(2)}, u32[]{:S(2)}) collective-permute-start(f32[2,2048]{1,0:T(2,128)S(1)} %get-tuple-element.21.a_ref), channel_id=1, source_target_pairs={{0,3},{1,2},{2,1},{3,0},{4,7},{5,6},{6,5},{7,4},{8,11},{9,10},{10,... | collective-permute-start | bytes 49160 | tf_op jit(solution)/shard_map/ppermute | solution.py:246
  42.3 1.1 %collective-permute-start.4 = (f32[2,2048]{1,0:T(2,128)S(1)}, f32[2,2048]{1,0:T(2,128)S(1)}, u32[]{:S(2)}, u32[]{:S(2)}) collective-permute-start(f32[2,2048]{1,0:T(2,128)S(1)} %get-tuple-element.21.a_ref), channel_id=1, source_target_pairs={{0,2},{1,3},{2,0},{3,1},{4,6},{5,7},{6,4},{7,5},{8,10},{9,11},{10,... | collective-permute-start | bytes 49160 | tf_op jit(solution)/shard_map/ppermute | solution.py:246
  43.4 0.3 collective-permute-start.3
  43.6 1.3 %collective-permute-done.5.d_ref = f32[2,2048]{1,0:T(2,128)S(1)} collective-permute-done((f32[2,2048]{1,0:T(2,128)S(1)}, f32[2,2048]{1,0:T(2,128)S(1)}, u32[]{:S(2)}, u32[]{:S(2)}) %collective-permute-start.5) | collective-permute-done | bytes 16416 | tf_op jit(solution)/shard_map/ppermute | solution.py:246
  45.0 2.5 %collective-permute-done.4.c_ref = f32[2,2048]{1,0:T(2,128)S(1)} collective-permute-done((f32[2,2048]{1,0:T(2,128)S(1)}, f32[2,2048]{1,0:T(2,128)S(1)}, u32[]{:S(2)}, u32[]{:S(2)}) %collective-permute-start.4) | collective-permute-done | bytes 16416 | tf_op jit(solution)/shard_map/ppermute | solution.py:246
  47.5 0.0 collective-permute-done.3.b_ref
  47.5 0.7 %last_sum.1 = bf16[64,2,512]{2,1,0:T(2,128)(2,1)} custom-call(f32[2,2048]{1,0:T(2,128)S(1)} %get-tuple-element.20.middle_ref, f32[2,2048]{1,0:T(2,128)S(1)} %get-tuple-element.21.a_ref, f32[2,2048]{1,0:T(2,128)S(1)} %collective-permute-done.3.b_ref, f32[2,2048]{1,0:T(2,128)S(1)} %collective-permute-done.4.c_ref, f32[2,2048]{1,0:T(2,128)S(1)} %collective-permute-done.5.d_ref), custom_call_target="tpu_custom_call" | custom-call | tf_op jit(solution)/shard_map/last_sum/pallas_call | solution.py:332
  48.2 4.9 %all-to-all-start.1 = ((bf16[64,2,512]{2,1,0:T(2,128)(2,1)}), bf16[64,2,512]{2,1,0:T(2,128)(2,1)S(1)}, u32[]{:S(2)}, u32[]{:S(2)}) async-start(bf16[64,2,512]{2,1,0:T(2,128)(2,1)} %last_sum.1), calls=%async_computation.1 | async-start | bytes 262144 | tf_op jit(solution)/shard_map/all_to_all | solution.py:340
  53.1 3.4 %projections.1 = (bf16[32,4,512]{2,1,0:T(4,128)(2,1)}, bf16[32,4,512]{2,1,0:T(4,128)(2,1)}, bf16[32,4,512]{2,1,0:T(4,128)(2,1)}) custom-call(f32[2,2048]{1,0:T(2,128)S(1)} %merge_project.1.a_ref.after_hbm, bf16[3,2048,512]{2,1,0:T(8,128)(2,1)} %w_hbm.3, bf16[128,512]{1,0:T(8,128)(2,1)S(1)} %get-tuple-element.22.q_rows, ...), custom_call_target="tpu_custom_call" | custom-call | tf_op jit(solution)/shard_map/projections/pallas_call | solution.py:312
  56.4 7.7 %all-to-all-done.1 = bf16[64,2,512]{2,1,0:T(2,128)(2,1)S(1)} async-done(((bf16[64,2,512]{2,1,0:T(2,128)(2,1)}), bf16[64,2,512]{2,1,0:T(2,128)(2,1)S(1)}, u32[]{:S(2)}, u32[]{:S(2)}) %all-to-all-start.1) | async-done | bytes 131104 | tf_op jit(solution)/shard_map/all_to_all | solution.py:340
  64.1 0.7 %reshape.11 = bf16[32,4,512]{2,1,0:T(4,128)(2,1)} reshape(bf16[64,2,512]{2,1,0:T(2,128)(2,1)S(1)} %all-to-all-done.1) | data formatting | bytes 262144 | tf_op jit(solution)/shard_map/reshape | solution.py:341
Async XLA Ops:
  0.6 31.1 %copy-start = (bf16[3,2048,512]{2,1,0:T(8,128)(2,1)S(1)}, bf16[3,2048,512]{2,1,0:T(8,128)(2,1)}, u32[]{:S(2)}) copy-start(bf16[3,2048,512]{2,1,0:T(8,128)(2,1)} %w_hbm.3) | copy-start | bytes 18874372
  0.6 31.1 %copy-start.4 = (bf16[512,2048]{1,0:T(8,128)(2,1)S(1)}, bf16[512,2048]{1,0:T(8,128)(2,1)}, u32[]{:S(2)}) copy-start(bf16[512,2048]{1,0:T(8,128)(2,1)} %w_ref.1) | copy-start | bytes 6291460
  0.7 37.7 %copy-start.2 = (bf16[1024,2048]{1,0:T(8,128)(2,1)S(1)}, bf16[1024,2048]{1,0:T(8,128)(2,1)}, u32[]{:S(2)}) copy-start(bf16[1024,2048]{1,0:T(8,128)(2,1)} %wd_ref.1) | copy-start | bytes 12582916
  31.8 6.5 %copy-start.1 = (bf16[2,2048,1024]{2,1,0:T(8,128)(2,1)S(1)}, bf16[2,2048,1024]{2,1,0:T(8,128)(2,1)}, u32[]{:S(2)}) copy-start(bf16[2,2048,1024]{2,1,0:T(8,128)(2,1)} %gu_ref.1) | copy-start | bytes 25165828
  31.8 6.5 %copy-start.3 = (bf16[32,4,2048]{2,1,0:T(4,128)(2,1)S(1)}, bf16[32,4,2048]{2,1,0:T(4,128)(2,1)}, u32[]{:S(2)}) copy-start(bf16[32,4,2048]{2,1,0:T(4,128)(2,1)} %x_ref.1) | copy-start | bytes 1572868
  32.9 4.7 %collective-permute-start.2 = (f32[2,2048]{1,0:T(2,128)S(1)}, f32[2,2048]{1,0:T(2,128)S(1)}, u32[]{:S(2)}, u32[]{:S(2)}) collective-permute-start(f32[2,2048]{1,0:T(2,128)S(1)} %merge_project.1.a_ref.after_hbm), channel_id=1, source_target_pairs={{0,3},{1,2},{2,1},{3,0},{4,7},{5,6},{6,5},{7,4},{8,11},{9,10},{10,... | collective-permute-start | bytes 49160 | tf_op jit(solution)/shard_map/ppermute | solution.py:246
  33.0 5.4 %collective-permute-start.1 = (f32[2,2048]{1,0:T(2,128)S(1)}, f32[2,2048]{1,0:T(2,128)S(1)}, u32[]{:S(2)}, u32[]{:S(2)}) collective-permute-start(f32[2,2048]{1,0:T(2,128)S(1)} %merge_project.1.a_ref.after_hbm), channel_id=1, source_target_pairs={{0,2},{1,3},{2,0},{3,1},{4,6},{5,7},{6,4},{7,5},{8,10},{9,11},{10,... | collective-permute-start | bytes 49160 | tf_op jit(solution)/shard_map/ppermute | solution.py:246
  33.8 4.5 %collective-permute-start = (f32[2,2048]{1,0:T(2,128)S(1)}, f32[2,2048]{1,0:T(2,128)S(1)}, u32[]{:S(2)}, u32[]{:S(2)}) collective-permute-start(f32[2,2048]{1,0:T(2,128)S(1)} %merge_project.1.a_ref.after_hbm), channel_id=1, source_target_pairs={{0,1},{1,0},{2,3},{3,2},{4,5},{5,4},{6,7},{7,6},{8,9},{9,8},{10,11... | collective-permute-start | bytes 49160 | tf_op jit(solution)/shard_map/ppermute | solution.py:246
  40.3 4.7 %collective-permute-start.5 = (f32[2,2048]{1,0:T(2,128)S(1)}, f32[2,2048]{1,0:T(2,128)S(1)}, u32[]{:S(2)}, u32[]{:S(2)}) collective-permute-start(f32[2,2048]{1,0:T(2,128)S(1)} %get-tuple-element.21.a_ref), channel_id=1, source_target_pairs={{0,3},{1,2},{2,1},{3,0},{4,7},{5,6},{6,5},{7,4},{8,11},{9,10},{10,... | collective-permute-start | bytes 49160 | tf_op jit(solution)/shard_map/ppermute | solution.py:246
  42.3 5.2 %collective-permute-start.4 = (f32[2,2048]{1,0:T(2,128)S(1)}, f32[2,2048]{1,0:T(2,128)S(1)}, u32[]{:S(2)}, u32[]{:S(2)}) collective-permute-start(f32[2,2048]{1,0:T(2,128)S(1)} %get-tuple-element.21.a_ref), channel_id=1, source_target_pairs={{0,2},{1,3},{2,0},{3,1},{4,6},{5,7},{6,4},{7,5},{8,10},{9,11},{10,... | collective-permute-start | bytes 49160 | tf_op jit(solution)/shard_map/ppermute | solution.py:246
  43.4 4.1 %collective-permute-start.3 = (f32[2,2048]{1,0:T(2,128)S(1)}, f32[2,2048]{1,0:T(2,128)S(1)}, u32[]{:S(2)}, u32[]{:S(2)}) collective-permute-start(f32[2,2048]{1,0:T(2,128)S(1)} %get-tuple-element.21.a_ref), channel_id=1, source_target_pairs={{0,1},{1,0},{2,3},{3,2},{4,5},{5,4},{6,7},{7,6},{8,9},{9,8},{10,11... | collective-permute-start | bytes 49160 | tf_op jit(solution)/shard_map/ppermute | solution.py:246
  48.2 15.9 %all-to-all-start.1 = ((bf16[64,2,512]{2,1,0:T(2,128)(2,1)}), bf16[64,2,512]{2,1,0:T(2,128)(2,1)S(1)}, u32[]{:S(2)}, u32[]{:S(2)}) async-start(bf16[64,2,512]{2,1,0:T(2,128)(2,1)} %last_sum.1), calls=%async_computation.1 | async-start | bytes 262144 | tf_op jit(solution)/shard_map/all_to_all | solution.py:340

commit v5 on v4

--- a/solution.py
+++ b/solution.py
@@ -14,8 +14,6 @@
 SCALE = DH ** (-0.5)
 F32 = jnp.float32
 BF16 = jnp.bfloat16
-FIRST = 2
-LIMIT = 48
 
 
 def norm_rows(x):
@@ -53,32 +51,43 @@
     group, reqs, steps, block, width,
     len_hbm, x_hbm, w_hbm, ck_hbm, cv_hbm,
     part_out, q_rows, q_own, normed_out, cos_out, sin_out,
-    len_s, x_v, w_v, ck_v, cv_v, xs, q16, sem_l, sem_x, sem_w, sem_k, sem_v,
+    len_s, order_s, x_v, w_v, ck_v, cv_v, xs, q16, sem_l, sem_x, sem_w, sem_k, sem_v,
 ):
     heads = width // DH
     rows = reqs * steps
+    tall = steps * heads
+    half = tall // 2
     seq = lax.axis_index("seq")
+    first = seq * block
     copy_l = pltpu.make_async_copy(len_hbm, len_s, sem_l)
     copy_l.start()
     copy_x = pltpu.make_async_copy(x_hbm, x_v, sem_x)
     copy_x.start()
     copy_w = pltpu.make_async_copy(w_hbm.at[0], w_v, sem_w)
     copy_w.start()
-    count = reqs // group
-    copies = []
-    for g in range(count):
-        span = pl.ds(g * group, group)
-        copies.append(pltpu.make_async_copy(ck_hbm.at[span], ck_v.at[span], sem_k.at[g]))
-        copies.append(pltpu.make_async_copy(cv_hbm.at[span], cv_v.at[span], sem_v.at[g]))
-    for c in copies[:FIRST]:
-        c.start()
-    waiting = copies[FIRST:]
-
-    def fetch(number):
-        for _ in range(min(number, len(waiting))):
-            waiting.pop(0).start()
 
     copy_l.wait()
+    count = jnp.int32(0)
+    for r in range(reqs):
+        live = len_s[r] > first
+        order_s[jnp.where(live, count, reqs - 1 - r + count)] = r
+        count = count + live.astype(jnp.int32)
+
+    def copies(cache, held, sems, lo):
+        return [
+            pltpu.make_async_copy(cache.at[order_s[i]], held.at[i], sems.at[i]) for i in range(lo, lo + group)
+        ]
+
+    def fetch(*args):
+        for c in copies(*args):
+            c.start()
+
+    def arrive(*args):
+        for c in copies(*args):
+            c.wait()
+
+    fetch(ck_hbm, ck_v, sem_k, 0)
+
     freq = frequencies()
     step_of = (lax.broadcasted_iota(jnp.int32, (8, DH), 0) % steps).astype(F32)
     lane8 = lax.broadcasted_iota(jnp.int32, (8, DH), 1)
@@ -90,59 +99,67 @@
         sine = jnp.sin(angles)
         sin_out[r * steps : (r + 2) * steps, :] = jnp.where(lane8 < DH // 2, -sine, sine)
 
+    lane = lax.broadcasted_iota(jnp.int32, (tall, DH), 1)
+    empty = jnp.where(lane[0:half] == 0, NEG, 0.0).astype(BF16)
+    for p in range(2 * reqs):
+        part_out[p, 0:half, :] = jnp.zeros((half, DH), BF16)
+        part_out[p, half : 2 * half, :] = empty
+
     copy_x.wait()
-    fetch(1)
+    fetch(cv_hbm, cv_v, sem_v, 0)
     for r in range(reqs):
         xs[pl.ds(r * steps, steps), :] = x_v[r].astype(F32)
     normed_out[...] = norm_rows(xs[...]).astype(BF16)
 
     copy_w.wait()
-    fetch(2)
     part = jnp.dot(normed_out[...], w_v[...], preferred_element_type=F32)
     for h in range(heads):
         q = turn(part[:, h * DH : (h + 1) * DH], cos_out[...], sin_out[...]).astype(BF16)
         q_rows[:, h * DH : (h + 1) * DH] = q
         q16[pl.ds(h, rows, stride=heads), :] = q.astype(F32)
-
-    tall = steps * heads
-    half = tall // 2
     q_own[...] = q16[pl.ds(seq * half, half), :]
-    lane = lax.broadcasted_iota(jnp.int32, (tall, DH), 1)
-    many_head = lax.broadcasted_iota(jnp.int32, (group * tall, DH), 0) % heads
+
+    row_head = lax.broadcasted_iota(jnp.int32, (tall, DH), 0) % heads
     many_lane = lax.broadcasted_iota(jnp.int32, (group * tall, DH), 1)
-    for g in range(count):
-        q = q16[g * group * tall : (g + 1) * group * tall, :]
-        spread = jnp.concatenate([jnp.where(many_head == h, q, 0.0).astype(BF16) for h in range(heads)], axis=1)
-        copies[2 * g].wait()
-        fetch(1)
+
+    def attend(lo):
+        arrive(ck_hbm, ck_v, sem_k, lo)
         scores = []
-        for i in range(group):
-            r = g * group + i
-            score = lax.dot_general(
-                spread[i * tall : (i + 1) * tall], ck_v[r], (((1,), (1,)), ((), ())), preferred_element_type=F32
-            )
-            scores.append(jnp.where(lane < len_s[r] - seq * block, score * SCALE, NEG))
+        for i in range(lo, lo + group):
+            r = order_s[i]
+            q = q16[pl.ds(pl.multiple_of(r * tall, tall), tall), :]
+            spread = jnp.concatenate([jnp.where(row_head == h, q, 0.0).astype(BF16) for h in range(heads)], axis=1)
+            score = lax.dot_general(spread, ck_v[i], (((1,), (1,)), ((), ())), preferred_element_type=F32)
+            scores.append(jnp.where(lane < len_s[r] - first, score * SCALE, NEG))
         scores = jnp.concatenate(scores, axis=0)
         highest = jnp.max(scores, axis=-1, keepdims=True)
         weights = jnp.where(scores == NEG, 0.0, jnp.exp(scores - highest))
         total = jnp.sum(weights, axis=-1, keepdims=True)
         weights = weights.astype(BF16)
-        copies[2 * g + 1].wait()
-        fetch(1)
         pieces = split3(jnp.broadcast_to(highest, scores.shape)) + split3(jnp.broadcast_to(total, scores.shape))
         stats = pieces[5]
         for i in range(4, -1, -1):
             stats = jnp.where(many_lane == i, pieces[i], stats)
         stats = stats.astype(BF16)
-        for i in range(group):
-            r = g * group + i
-            wide = jnp.dot(weights[i * tall : (i + 1) * tall], cv_v[r], preferred_element_type=F32)
+        arrive(cv_hbm, cv_v, sem_v, lo)
+        for i in range(lo, lo + group):
+            r = order_s[i]
+            at = (i - lo) * tall
+            wide = jnp.dot(weights[at : at + tall], cv_v[i], preferred_element_type=F32)
             o = wide[:, 0:DH]
             for h in range(1, heads):
-                o = jnp.where(many_head[0:tall] == h, wide[:, h * DH : (h + 1) * DH], o)
+                o = jnp.where(row_head == h, wide[:, h * DH : (h + 1) * DH], o)
             for j in range(2):
                 part_out[2 * r + j, 0:half, :] = o[j * half : (j + 1) * half].astype(BF16)
-                part_out[2 * r + j, half : 2 * half, :] = stats[i * tall + j * half : i * tall + (j + 1) * half]
+                part_out[2 * r + j, half : 2 * half, :] = stats[at + j * half : at + (j + 1) * half]
+
+    attend(0)
+    for lo in range(group, reqs, group):
+        @pl.when(count > lo)
+        def _():
+            fetch(ck_hbm, ck_v, sem_k, lo)
+            fetch(cv_hbm, cv_v, sem_v, lo)
+            attend(lo)
 
 
 def merge_kernel(
@@ -257,7 +274,7 @@
     n_seq = lax.axis_size("seq")
     n_mp = lax.axis_size("mp")
     assert rows == 2 * n_seq and steps == 4 and n_mp == 4 and tall == 16
-    group = min(16, reqs)
+    group = max(reqs // 2, 1)
     in_hbm = functools.partial(pltpu.with_memory_space_constraint, memory_space=pltpu.HBM)
     any_space = pl.BlockSpec(memory_space=pltpu.HBM)
     vmem = pl.BlockSpec(memory_space=pltpu.VMEM)
@@ -275,6 +292,7 @@
         out_specs=(vmem,) * 6,
         scratch_shapes=[
             pltpu.SMEM((reqs,), jnp.int32),
+            pltpu.SMEM((reqs,), jnp.int32),
             pltpu.VMEM(inputs.shape, BF16),
             pltpu.VMEM((model, width), BF16),
             pltpu.VMEM(cache_keys.shape, BF16),
@@ -284,10 +302,10 @@
             pltpu.SemaphoreType.DMA,
             pltpu.SemaphoreType.DMA,
             pltpu.SemaphoreType.DMA,
-            pltpu.SemaphoreType.DMA((reqs // group,)),
-            pltpu.SemaphoreType.DMA((reqs // group,)),
+            pltpu.SemaphoreType.DMA((reqs,)),
+            pltpu.SemaphoreType.DMA((reqs,)),
         ],
-        compiler_params=pltpu.CompilerParams(vmem_limit_bytes=LIMIT << 20),
+        compiler_params=pltpu.CompilerParams(vmem_limit_bytes=48 << 20),
         name="cached_attention",
     )(in_hbm(lengths), in_hbm(inputs), in_hbm(w_qkv), in_hbm(cache_keys), in_hbm(cache_values))
 

time: 65 us -> 64.5 us (level)
  blocking collectives: 25.8 us -> 21.6 us
  Pallas kernels: 12.4 us -> 16.1 us
    all_to_all x1, blocking collectives: 25.8 us -> 21.6 us  [per_device(): got = lax.all_to_all(part, 'seq', 0, 0)]
    pallas_call x1, Pallas kernels: 5.26 us -> 8.98 us  [per_device(): pl.pallas_call(functools.partial(cached_kernel, group, reqs, steps, block...]
where the time goes in v5:
time: 64.5 us; the launch traced here: 64.3 us
  blocking collectives  21.6 us (33%)
  Pallas kernels  16.1 us (25%)
  waiting for transfers between devices  13.5 us (21%)
  starting transfers between devices  11.6 us (18%)
  local copies, waits for them, and re-layouts  0.73 us (1%)
  between operations  0.72 us (1%)
    all_to_all x1, blocking collectives, per_device(): got = lax.all_to_all(part, 'seq', 0, 0)  21.6 us
    pallas_call x1, Pallas kernels, per_device(): pl.pallas_call(functools.partial(cached_kernel, group, reqs, steps, block...  8.98 us
    all_to_all x1, waiting for transfers between devices, per_device(): hidden = lax.all_to_all(hidden, 'seq', 0, 0)  7.67 us
    ppermute x6, starting transfers between devices, to_others(): lax.ppermute(values[k - 1], axis, [(i, i ^ k) for i in range(size)])  6.74 us
    ppermute x6, waiting for transfers between devices, to_others(): lax.ppermute(values[k - 1], axis, [(i, i ^ k) for i in range(size)])  5.86 us
    all_to_all x1, starting transfers between devices, per_device(): hidden = lax.all_to_all(hidden, 'seq', 0, 0)  4.87 us
    pallas_call x1, Pallas kernels, per_device(): pl.pallas_call(outputs_kernel, out_shape=(piece,) * 3, in_specs=[any_spac...  3.35 us
    pallas_call x1, Pallas kernels, per_device(): pl.pallas_call(mlp_kernel, out_shape=(rows2,) * 2, in_specs=[vmem] * 7, o...  1.94 us
  transfers between devices with their start and end apart: 7, of which 5 were waited for; matrix products, arithmetic and copies ran while one was open for 0% of the time, Pallas kernels for 5%

profile of v5, /device:TPU:4, one launch (start us, length us, event | category | flops | bytes accessed | tf_op | source)
XLA Modules:
  0.0 64.3 jit_solution(16331848170096548359)
XLA Ops:
  0.6 0.0 copy-start
  0.6 0.0 copy-start.4
  0.7 0.0 copy-start.2
  0.7 9.0 %cached_attention.1 = (bf16[64,16,128]{2,1,0:T(8,128)(2,1)S(1)}, bf16[128,512]{1,0:T(8,128)(2,1)S(1)}, f32[8,128]{1,0:T(8,128)S(1)}, bf16[128,2048]{1,0:T(8,128)...) custom-call(s32[32]{0:T(128)} %len_hbm.1, bf16[32,4,2048]{2,1,0:T(4,128)(2,1)} %x_ref.1, ...), custom_call_target="tpu_custom_call" | custom-call | tf_op jit(solution)/shard_map/cached_attention/pallas_call | solution.py:281
  9.7 21.6 %all_to_all.10.got_ref = bf16[64,16,128]{2,1,0:T(8,128)(2,1)S(1)} all-to-all(bf16[64,16,128]{2,1,0:T(8,128)(2,1)S(1)} %get-tuple-element.15), channel_id=1, replica_groups=mesh['seq'=64,'mp'=4] {'seq'}, dimensions={0} | all-to-all | bytes 524288 | tf_op jit(solution)/shard_map/all_to_all | solution.py:312
  31.3 0.0 copy-done
  31.3 0.0 copy-done.4
  31.3 0.0 copy-start.1
  31.3 0.0 copy-start.3
  31.3 1.1 %merge_project.1.a_ref.after_hbm = f32[2,2048]{1,0:T(2,128)S(1)} custom-call(bf16[64,16,128]{2,1,0:T(8,128)(2,1)S(1)} %all_to_all.10.got_ref, f32[8,128]{1,0:T(8,128)S(1)} %get-tuple-element.16.q_own, bf16[128,2048]{1,0:T(8,128)(2,1)S(1)} %get-tuple-element.17.normed, f32[128,128]{1,0:T(8,128)S(1)} %get-tuple-element.18.cosine, ...), custom_call_target="tpu_custom_call" | custom-call | tf_op jit(solution)/shard_map/merge_project/pallas_call | solution.py:314
  32.4 0.0 collective-permute-start.2
  32.5 0.9 %collective-permute-start.1 = (f32[2,2048]{1,0:T(2,128)S(1)}, f32[2,2048]{1,0:T(2,128)S(1)}, u32[]{:S(2)}, u32[]{:S(2)}) collective-permute-start(f32[2,2048]{1,0:T(2,128)S(1)} %merge_project.1.a_ref.after_hbm), channel_id=1, source_target_pairs={{0,2},{1,3},{2,0},{3,1},{4,6},{5,7},{6,4},{7,5},{8,10},{9,11},{10,... | collective-permute-start | bytes 49160 | tf_op jit(solution)/shard_map/ppermute | solution.py:263
  33.4 2.5 %collective-permute-start = (f32[2,2048]{1,0:T(2,128)S(1)}, f32[2,2048]{1,0:T(2,128)S(1)}, u32[]{:S(2)}, u32[]{:S(2)}) collective-permute-start(f32[2,2048]{1,0:T(2,128)S(1)} %merge_project.1.a_ref.after_hbm), channel_id=1, source_target_pairs={{0,1},{1,0},{2,3},{3,2},{4,5},{5,4},{6,7},{7,6},{8,9},{9,8},{10,11... | collective-permute-start | bytes 49160 | tf_op jit(solution)/shard_map/ppermute | solution.py:263
  35.8 1.3 %collective-permute-done.2.d_ref = f32[2,2048]{1,0:T(2,128)S(1)} collective-permute-done((f32[2,2048]{1,0:T(2,128)S(1)}, f32[2,2048]{1,0:T(2,128)S(1)}, u32[]{:S(2)}, u32[]{:S(2)}) %collective-permute-start.2) | collective-permute-done | bytes 16416 | tf_op jit(solution)/shard_map/ppermute | solution.py:263
  37.1 0.7 %collective-permute-done.1.c_ref = f32[2,2048]{1,0:T(2,128)S(1)} collective-permute-done((f32[2,2048]{1,0:T(2,128)S(1)}, f32[2,2048]{1,0:T(2,128)S(1)}, u32[]{:S(2)}, u32[]{:S(2)}) %collective-permute-start.1) | collective-permute-done | bytes 16416 | tf_op jit(solution)/shard_map/ppermute | solution.py:263
  37.8 0.0 collective-permute-done.b_ref
  37.8 0.0 copy-done.2
  37.8 0.0 copy-done.1
  37.8 0.0 copy-done.3
  37.8 1.9 %mlp.1 = (f32[2,2048]{1,0:T(2,128)S(1)}, f32[2,2048]{1,0:T(2,128)S(1)}) custom-call(bf16[32,4,2048]{2,1,0:T(4,128)(2,1)S(1)} %copy-done.3, bf16[2,2048,1024]{2,1,0:T(8,128)(2,1)S(1)} %copy-done.1, bf16[1024,2048]{1,0:T(8,128)(2,1)S(1)} %copy-done.2, f32[2,2048]{1,0:T(2,128)S(1)} %merge_project.1.a_ref.after_hbm, f32[2,2048]{1,0:T(2,128)S(1)} %collective-permute-done.b_ref, ...), custom_call_target="tpu_custom_call" | custom-call | tf_op jit(solution)/shard_map/mlp/pallas_call | solution.py:342
  39.8 2.0 %collective-permute-start.5 = (f32[2,2048]{1,0:T(2,128)S(1)}, f32[2,2048]{1,0:T(2,128)S(1)}, u32[]{:S(2)}, u32[]{:S(2)}) collective-permute-start(f32[2,2048]{1,0:T(2,128)S(1)} %get-tuple-element.21.a_ref), channel_id=1, source_target_pairs={{0,3},{1,2},{2,1},{3,0},{4,7},{5,6},{6,5},{7,4},{8,11},{9,10},{10,... | collective-permute-start | bytes 49160 | tf_op jit(solution)/shard_map/ppermute | solution.py:263
  41.8 1.1 %collective-permute-start.4 = (f32[2,2048]{1,0:T(2,128)S(1)}, f32[2,2048]{1,0:T(2,128)S(1)}, u32[]{:S(2)}, u32[]{:S(2)}) collective-permute-start(f32[2,2048]{1,0:T(2,128)S(1)} %get-tuple-element.21.a_ref), channel_id=1, source_target_pairs={{0,2},{1,3},{2,0},{3,1},{4,6},{5,7},{6,4},{7,5},{8,10},{9,11},{10,... | collective-permute-start | bytes 49160 | tf_op jit(solution)/shard_map/ppermute | solution.py:263
  42.9 0.3 collective-permute-start.3
  43.2 1.3 %collective-permute-done.5.d_ref = f32[2,2048]{1,0:T(2,128)S(1)} collective-permute-done((f32[2,2048]{1,0:T(2,128)S(1)}, f32[2,2048]{1,0:T(2,128)S(1)}, u32[]{:S(2)}, u32[]{:S(2)}) %collective-permute-start.5) | collective-permute-done | bytes 16416 | tf_op jit(solution)/shard_map/ppermute | solution.py:263
  44.5 2.5 %collective-permute-done.4.c_ref = f32[2,2048]{1,0:T(2,128)S(1)} collective-permute-done((f32[2,2048]{1,0:T(2,128)S(1)}, f32[2,2048]{1,0:T(2,128)S(1)}, u32[]{:S(2)}, u32[]{:S(2)}) %collective-permute-start.4) | collective-permute-done | bytes 16416 | tf_op jit(solution)/shard_map/ppermute | solution.py:263
  47.0 0.0 collective-permute-done.3.b_ref
  47.0 0.7 %last_sum.1 = bf16[64,2,512]{2,1,0:T(2,128)(2,1)} custom-call(f32[2,2048]{1,0:T(2,128)S(1)} %get-tuple-element.20.middle_ref, f32[2,2048]{1,0:T(2,128)S(1)} %get-tuple-element.21.a_ref, f32[2,2048]{1,0:T(2,128)S(1)} %collective-permute-done.3.b_ref, f32[2,2048]{1,0:T(2,128)S(1)} %collective-permute-done.4.c_ref, f32[2,2048]{1,0:T(2,128)S(1)} %collective-permute-done.5.d_ref), custom_call_target="tpu_custom_call" | custom-call | tf_op jit(solution)/shard_map/last_sum/pallas_call | solution.py:350
  47.7 4.9 %all-to-all-start.1 = ((bf16[64,2,512]{2,1,0:T(2,128)(2,1)}), bf16[64,2,512]{2,1,0:T(2,128)(2,1)S(1)}, u32[]{:S(2)}, u32[]{:S(2)}) async-start(bf16[64,2,512]{2,1,0:T(2,128)(2,1)} %last_sum.1), calls=%async_computation.1 | async-start | bytes 262144 | tf_op jit(solution)/shard_map/all_to_all | solution.py:358
  52.6 3.4 %projections.1 = (bf16[32,4,512]{2,1,0:T(4,128)(2,1)}, bf16[32,4,512]{2,1,0:T(4,128)(2,1)}, bf16[32,4,512]{2,1,0:T(4,128)(2,1)}) custom-call(f32[2,2048]{1,0:T(2,128)S(1)} %merge_project.1.a_ref.after_hbm, bf16[3,2048,512]{2,1,0:T(8,128)(2,1)} %w_hbm.3, bf16[128,512]{1,0:T(8,128)(2,1)S(1)} %get-tuple-element.22.q_rows, ...), custom_call_target="tpu_custom_call" | custom-call | tf_op jit(solution)/shard_map/projections/pallas_call | solution.py:330
  56.0 7.7 %all-to-all-done.1 = bf16[64,2,512]{2,1,0:T(2,128)(2,1)S(1)} async-done(((bf16[64,2,512]{2,1,0:T(2,128)(2,1)}), bf16[64,2,512]{2,1,0:T(2,128)(2,1)S(1)}, u32[]{:S(2)}, u32[]{:S(2)}) %all-to-all-start.1) | async-done | bytes 131104 | tf_op jit(solution)/shard_map/all_to_all | solution.py:358
  63.6 0.7 %reshape.11 = bf16[32,4,512]{2,1,0:T(4,128)(2,1)} reshape(bf16[64,2,512]{2,1,0:T(2,128)(2,1)S(1)} %all-to-all-done.1) | data formatting | bytes 262144 | tf_op jit(solution)/shard_map/reshape | solution.py:359
Async XLA Ops:
  0.6 30.7 %copy-start = (bf16[3,2048,512]{2,1,0:T(8,128)(2,1)S(1)}, bf16[3,2048,512]{2,1,0:T(8,128)(2,1)}, u32[]{:S(2)}) copy-start(bf16[3,2048,512]{2,1,0:T(8,128)(2,1)} %w_hbm.3) | copy-start | bytes 18874372
  0.6 30.7 %copy-start.4 = (bf16[512,2048]{1,0:T(8,128)(2,1)S(1)}, bf16[512,2048]{1,0:T(8,128)(2,1)}, u32[]{:S(2)}) copy-start(bf16[512,2048]{1,0:T(8,128)(2,1)} %w_ref.1) | copy-start | bytes 6291460
  0.7 37.2 %copy-start.2 = (bf16[1024,2048]{1,0:T(8,128)(2,1)S(1)}, bf16[1024,2048]{1,0:T(8,128)(2,1)}, u32[]{:S(2)}) copy-start(bf16[1024,2048]{1,0:T(8,128)(2,1)} %wd_ref.1) | copy-start | bytes 12582916
  31.3 6.5 %copy-start.1 = (bf16[2,2048,1024]{2,1,0:T(8,128)(2,1)S(1)}, bf16[2,2048,1024]{2,1,0:T(8,128)(2,1)}, u32[]{:S(2)}) copy-start(bf16[2,2048,1024]{2,1,0:T(8,128)(2,1)} %gu_ref.1) | copy-start | bytes 25165828
  31.3 6.5 %copy-start.3 = (bf16[32,4,2048]{2,1,0:T(4,128)(2,1)S(1)}, bf16[32,4,2048]{2,1,0:T(4,128)(2,1)}, u32[]{:S(2)}) copy-start(bf16[32,4,2048]{2,1,0:T(4,128)(2,1)} %x_ref.1) | copy-start | bytes 1572868
  32.4 4.7 %collective-permute-start.2 = (f32[2,2048]{1,0:T(2,128)S(1)}, f32[2,2048]{1,0:T(2,128)S(1)}, u32[]{:S(2)}, u32[]{:S(2)}) collective-permute-start(f32[2,2048]{1,0:T(2,128)S(1)} %merge_project.1.a_ref.after_hbm), channel_id=1, source_target_pairs={{0,3},{1,2},{2,1},{3,0},{4,7},{5,6},{6,5},{7,4},{8,11},{9,10},{10,... | collective-permute-start | bytes 49160 | tf_op jit(solution)/shard_map/ppermute | solution.py:263
  32.5 5.4 %collective-permute-start.1 = (f32[2,2048]{1,0:T(2,128)S(1)}, f32[2,2048]{1,0:T(2,128)S(1)}, u32[]{:S(2)}, u32[]{:S(2)}) collective-permute-start(f32[2,2048]{1,0:T(2,128)S(1)} %merge_project.1.a_ref.after_hbm), channel_id=1, source_target_pairs={{0,2},{1,3},{2,0},{3,1},{4,6},{5,7},{6,4},{7,5},{8,10},{9,11},{10,... | collective-permute-start | bytes 49160 | tf_op jit(solution)/shard_map/ppermute | solution.py:263
  33.4 4.5 %collective-permute-start = (f32[2,2048]{1,0:T(2,128)S(1)}, f32[2,2048]{1,0:T(2,128)S(1)}, u32[]{:S(2)}, u32[]{:S(2)}) collective-permute-start(f32[2,2048]{1,0:T(2,128)S(1)} %merge_project.1.a_ref.after_hbm), channel_id=1, source_target_pairs={{0,1},{1,0},{2,3},{3,2},{4,5},{5,4},{6,7},{7,6},{8,9},{9,8},{10,11... | collective-permute-start | bytes 49160 | tf_op jit(solution)/shard_map/ppermute | solution.py:263
  39.8 4.7 %collective-permute-start.5 = (f32[2,2048]{1,0:T(2,128)S(1)}, f32[2,2048]{1,0:T(2,128)S(1)}, u32[]{:S(2)}, u32[]{:S(2)}) collective-permute-start(f32[2,2048]{1,0:T(2,128)S(1)} %get-tuple-element.21.a_ref), channel_id=1, source_target_pairs={{0,3},{1,2},{2,1},{3,0},{4,7},{5,6},{6,5},{7,4},{8,11},{9,10},{10,... | collective-permute-start | bytes 49160 | tf_op jit(solution)/shard_map/ppermute | solution.py:263
  41.8 5.2 %collective-permute-start.4 = (f32[2,2048]{1,0:T(2,128)S(1)}, f32[2,2048]{1,0:T(2,128)S(1)}, u32[]{:S(2)}, u32[]{:S(2)}) collective-permute-start(f32[2,2048]{1,0:T(2,128)S(1)} %get-tuple-element.21.a_ref), channel_id=1, source_target_pairs={{0,2},{1,3},{2,0},{3,1},{4,6},{5,7},{6,4},{7,5},{8,10},{9,11},{10,... | collective-permute-start | bytes 49160 | tf_op jit(solution)/shard_map/ppermute | solution.py:263
  42.9 4.1 %collective-permute-start.3 = (f32[2,2048]{1,0:T(2,128)S(1)}, f32[2,2048]{1,0:T(2,128)S(1)}, u32[]{:S(2)}, u32[]{:S(2)}) collective-permute-start(f32[2,2048]{1,0:T(2,128)S(1)} %get-tuple-element.21.a_ref), channel_id=1, source_target_pairs={{0,1},{1,0},{2,3},{3,2},{4,5},{5,4},{6,7},{7,6},{8,9},{9,8},{10,11... | collective-permute-start | bytes 49160 | tf_op jit(solution)/shard_map/ppermute | solution.py:263
  47.7 15.9 %all-to-all-start.1 = ((bf16[64,2,512]{2,1,0:T(2,128)(2,1)}), bf16[64,2,512]{2,1,0:T(2,128)(2,1)S(1)}, u32[]{:S(2)}, u32[]{:S(2)}) async-start(bf16[64,2,512]{2,1,0:T(2,128)(2,1)} %last_sum.1), calls=%async_computation.1 | async-start | bytes 262144 | tf_op jit(solution)/shard_map/all_to_all | solution.py:358

commit v6 on v5

--- a/solution.py
+++ b/solution.py
@@ -162,26 +162,30 @@
             attend(lo)
 
 
-def merge_kernel(
+def fresh_kernel(
     steps,
-    got_ref, q_own, normed, cosine, sine, w_qkv, w_ref,
-    out_ref,
-    k16, v16, ctx_s,
+    w_hbm, proj_hbm, q_own, normed, cosine, sine,
+    fresh_out, proj_out,
+    w_v, k16, v16, sem_w, sem_p,
 ):
     half = q_own.shape[0]
     heads = half // 2
     tall = 2 * half
     seq = lax.axis_index("seq")
-
+    copies = [pltpu.make_async_copy(w_hbm.at[1 + j], w_v.at[j], sem_w.at[j]) for j in range(2)]
+    for c in copies:
+        c.start()
+    copy_p = pltpu.make_async_copy(proj_hbm, proj_out, sem_p)
+    copy_p.start()
     block = pl.multiple_of((seq // 4) * 8, 8)
     rows = normed[pl.ds(block, 8), :]
-    keys = jnp.dot(rows, w_qkv[1], preferred_element_type=F32)
-    values = jnp.dot(rows, w_qkv[2], preferred_element_type=F32)
     turns = (cosine[pl.ds(block, 8), :], sine[pl.ds(block, 8), :])
-    for h in range(heads):
-        span = slice(h * DH, (h + 1) * DH)
-        k16[pl.ds(h, 8, stride=heads), :] = rounded(turn(keys[:, span], *turns))
-        v16[pl.ds(h, 8, stride=heads), :] = rounded(values[:, span])
+    for j, store in enumerate((k16, v16)):
+        copies[j].wait()
+        part = jnp.dot(rows, w_v[j], preferred_element_type=F32)
+        for h in range(heads):
+            v = part[:, h * DH : (h + 1) * DH]
+            store[pl.ds(h, 8, stride=heads), :] = rounded(turn(v, *turns) if j == 0 else v)
     q = q_own[...]
     step = (seq % 2) * 2 + lax.broadcasted_iota(jnp.int32, (half, 1), 0) // heads
     base = pl.multiple_of(((seq // 2) % 2) * tall, tall)
@@ -193,24 +197,33 @@
         key = jnp.concatenate([key, key], axis=0)
         values.append(jnp.concatenate([value, value], axis=0))
         scores.append(jnp.sum(q * key, axis=-1, keepdims=True) * SCALE)
-    fresh_high = scores[0]
+    high = scores[0]
     for s in range(1, steps):
-        fresh_high = jnp.maximum(fresh_high, jnp.where(s <= step, scores[s], NEG))
-    fresh_total = jnp.zeros_like(fresh_high)
-    fresh = jnp.zeros((half, DH), F32)
+        high = jnp.maximum(high, jnp.where(s <= step, scores[s], NEG))
+    total = jnp.zeros_like(high)
+    o = jnp.zeros((half, DH), F32)
     for s in range(steps):
-        weight = jnp.where(s <= step, jnp.exp(scores[s] - fresh_high), 0.0)
-        fresh_total = fresh_total + weight
-        fresh = fresh + rounded(weight) * values[s]
-
+        weight = jnp.where(s <= step, jnp.exp(scores[s] - high), 0.0)
+        total = total + weight
+        o = o + rounded(weight) * values[s]
+    fresh_out[0] = o
+    fresh_out[1] = jnp.broadcast_to(high, o.shape)
+    fresh_out[2] = jnp.broadcast_to(total, o.shape)
+    copy_p.wait()
+
+
+def merge_kernel(got_ref, fresh_ref, w_ref, out_ref, ctx_s):
+    half = fresh_ref.shape[1]
+    heads = half // 2
+    fresh_high = fresh_ref[1][:, 0:1]
     stats = got_ref[:, half : 2 * half, :].astype(F32)
     highest = (stats[:, :, 0:1] + stats[:, :, 1:2]) + stats[:, :, 2:3]
     total = (stats[:, :, 3:4] + stats[:, :, 4:5]) + stats[:, :, 5:6]
     top = jnp.maximum(jnp.max(highest, axis=0), fresh_high)
     factor = jnp.exp(highest - top[None])
     fresh_factor = jnp.exp(fresh_high - top)
-    whole = jnp.sum(factor * total, axis=0) + fresh_factor * fresh_total
-    o = jnp.sum(factor * got_ref[:, 0:half, :].astype(F32), axis=0) + fresh_factor * fresh
+    whole = jnp.sum(factor * total, axis=0) + fresh_factor * fresh_ref[2][:, 0:1]
+    o = jnp.sum(factor * got_ref[:, 0:half, :].astype(F32), axis=0) + fresh_factor * fresh_ref[0]
     ctx_s[...] = o / whole
     ctx = jnp.concatenate([ctx_s[pl.ds(h, 2, stride=heads), :] for h in range(heads)], axis=1)
     out_ref[...] = jnp.dot(ctx.astype(BF16), w_ref[...], preferred_element_type=F32)
@@ -311,19 +324,31 @@
 
     got = lax.all_to_all(part, "seq", 0, 0)
 
-    mine = pl.pallas_call(
-        functools.partial(merge_kernel, steps),
-        out_shape=jax.ShapeDtypeStruct((2, model), F32),
-        in_specs=[vmem] * 7,
-        out_specs=vmem,
+    fresh, w_proj = pl.pallas_call(
+        functools.partial(fresh_kernel, steps),
+        out_shape=(jax.ShapeDtypeStruct((3, tall // 2, DH), F32), jax.ShapeDtypeStruct(w_out.shape, BF16)),
+        in_specs=[any_space] * 2 + [vmem] * 4,
+        out_specs=(vmem,) * 2,
         scratch_shapes=[
+            pltpu.VMEM((2, model, width), BF16),
             pltpu.VMEM((8 * heads, DH), F32),
             pltpu.VMEM((8 * heads, DH), F32),
-            pltpu.VMEM((tall // 2, DH), F32),
+            pltpu.SemaphoreType.DMA((2,)),
+            pltpu.SemaphoreType.DMA,
         ],
-        compiler_params=pltpu.CompilerParams(vmem_limit_bytes=8 << 20),
+        compiler_params=pltpu.CompilerParams(vmem_limit_bytes=12 << 20),
+        name="new_tokens",
+    )(in_hbm(w_qkv), in_hbm(w_out), q_own, normed, cosine, sine)
+    mine = pl.pallas_call(
+        merge_kernel,
+        out_shape=jax.ShapeDtypeStruct((2, model), F32),
+        in_specs=[vmem] * 3,
+        out_specs=vmem,
+        scratch_shapes=[pltpu.VMEM((tall // 2, DH), F32)],
+        compiler_params=pltpu.CompilerParams(vmem_limit_bytes=4 << 20),
+        cost_estimate=pl.CostEstimate(flops=10**10, transcendentals=0, bytes_accessed=60 << 20),
         name="merge_project",
-    )(got, q_own, normed, cosine, sine, w_qkv, w_out)
+    )(got, fresh, w_proj)
     others = to_others([mine] * 3, "mp")
 
     piece = jax.ShapeDtypeStruct((reqs, steps, width), BF16)

time: 64.5 us -> 64.3 us (level)
  blocking collectives: 21.6 us -> 0 us
  waiting for transfers between devices: 13.5 us -> 23.7 us
  starting transfers between devices: 11.6 us -> 20.9 us
  Pallas kernels: 16.1 us -> 18 us
    all_to_all x1 -> x0, blocking collectives: 21.6 us -> none  [per_device(): got = lax.all_to_all(part, 'seq', 0, 0)]
    all_to_all x0 -> x1, waiting for transfers between devices: none -> 10.1 us  [per_device(): got = lax.all_to_all(part, 'seq', 0, 0)]
    all_to_all x0 -> x1, starting transfers between devices: none -> 9.33 us  [per_device(): got = lax.all_to_all(part, 'seq', 0, 0)]
    pallas_call x1 -> x2, Pallas kernels: 1.14 us -> 3.59 us  [the longest x1 2.89 us: per_device(): pl.pallas_call(functools.partial(fresh_kernel, steps), out_shape=(jax.Sha...]
  transfers between devices with their start and end apart: 7 -> 8, of which waited for: 5 -> 6; matrix products, arithmetic and copies ran while one was open for 0% -> 0% of each run, Pallas kernels for 5% -> 10%
where the time goes in v6:
time: 64.3 us; the launch traced here: 64 us
  waiting for transfers between devices  23.7 us (37%)
  starting transfers between devices  20.9 us (33%)
  Pallas kernels  18 us (28%)
  local copies, waits for them, and re-layouts  0.73 us (1%)
  between operations  0.72 us (1%)
    all_to_all x1, waiting for transfers between devices, per_device(): got = lax.all_to_all(part, 'seq', 0, 0)  10.1 us
    all_to_all x1, starting transfers between devices, per_device(): got = lax.all_to_all(part, 'seq', 0, 0)  9.33 us
    pallas_call x1, Pallas kernels, per_device(): pl.pallas_call(functools.partial(cached_kernel, group, reqs, steps, block...  8.4 us
    all_to_all x1, waiting for transfers between devices, per_device(): hidden = lax.all_to_all(hidden, 'seq', 0, 0)  7.66 us
    ppermute x6, starting transfers between devices, to_others(): lax.ppermute(values[k - 1], axis, [(i, i ^ k) for i in range(size)])  6.74 us
    ppermute x6, waiting for transfers between devices, to_others(): lax.ppermute(values[k - 1], axis, [(i, i ^ k) for i in range(size)])  5.86 us
    all_to_all x1, starting transfers between devices, per_device(): hidden = lax.all_to_all(hidden, 'seq', 0, 0)  4.87 us
    pallas_call x1, Pallas kernels, per_device(): pl.pallas_call(outputs_kernel, out_shape=(piece,) * 3, in_specs=[any_spac...  3.35 us
  transfers between devices with their start and end apart: 8, of which 6 were waited for; matrix products, arithmetic and copies ran while one was open for 0% of the time, Pallas kernels for 10%

profile of v6, /device:TPU:4, one launch (start us, length us, event | category | flops | bytes accessed | tf_op | source)
XLA Modules:
  0.0 64.0 jit_solution(10120715837230267409)
XLA Ops:
  0.6 8.4 %cached_attention.1 = (bf16[64,16,128]{2,1,0:T(8,128)(2,1)}, bf16[128,512]{1,0:T(8,128)(2,1)S(1)}, f32[8,128]{1,0:T(8,128)S(1)}, bf16[128,2048]{1,0:T(8,128)(2,1...) custom-call(s32[32]{0:T(128)} %len_hbm.1, bf16[32,4,2048]{2,1,0:T(4,128)(2,1)} %x_ref.1, ...), custom_call_target="tpu_custom_call" | custom-call | tf_op jit(solution)/shard_map/cached_attention/pallas_call | solution.py:294
  9.0 9.3 %all-to-all-start = ((bf16[64,16,128]{2,1,0:T(8,128)(2,1)}), bf16[64,16,128]{2,1,0:T(8,128)(2,1)S(1)}, u32[]{:S(2)}, u32[]{:S(2)}) async-start(bf16[64,16,128]{2,1,0:T(8,128)(2,1)} %get-tuple-element.17), calls=%async_computation | async-start | bytes 524288 | tf_op jit(solution)/shard_map/all_to_all | solution.py:325
  18.4 2.9 %new_tokens.1 = (f32[3,8,128]{2,1,0:T(8,128)S(1)}, bf16[512,2048]{1,0:T(8,128)(2,1)S(1)}) custom-call(bf16[3,2048,512]{2,1,0:T(8,128)(2,1)} %w_hbm.5, bf16[512,2048]{1,0:T(8,128)(2,1)} %proj_hbm.1, f32[8,128]{1,0:T(8,128)S(1)} %get-tuple-element.18.q_own, bf16[128,2048]{1,0:T(8,128)(2,1)S(1)} %get-tuple-element.19.normed, ...), custom_call_target="tpu_custom_call" | custom-call | tf_op jit(solution)/shard_map/new_tokens/pallas_call | solution.py:327
  21.3 10.1 %all-to-all-done.got_ref = bf16[64,16,128]{2,1,0:T(8,128)(2,1)S(1)} async-done(((bf16[64,16,128]{2,1,0:T(8,128)(2,1)}), bf16[64,16,128]{2,1,0:T(8,128)(2,1)S(1)}, u32[]{:S(2)}, u32[]{:S(2)}) %all-to-all-start) | async-done | bytes 262176 | tf_op jit(solution)/shard_map/all_to_all | solution.py:325
  31.4 0.0 slice-start
  31.4 0.0 slice-start.1
  31.4 0.0 copy-start
  31.4 0.0 copy-start.1
  31.4 0.7 %merge_project.1.a_ref.after_hbm = f32[2,2048]{1,0:T(2,128)S(1)} custom-call(bf16[64,16,128]{2,1,0:T(8,128)(2,1)S(1)} %all-to-all-done.got_ref, f32[3,8,128]{2,1,0:T(8,128)S(1)} %get-tuple-element.22.fresh_ref, bf16[512,2048]{1,0:T(8,128)(2,1)S(1)} %get-tuple-element.23.w_ref), custom_call_target="tpu_custom_call" | custom-call | flops 10000000000 | bytes 62914560 | tf_op jit(solution)/shard_map/merge_project/pallas_call | solution.py:342
  32.1 0.0 collective-permute-start.2
  32.2 0.9 %collective-permute-start.1 = (f32[2,2048]{1,0:T(2,128)S(1)}, f32[2,2048]{1,0:T(2,128)S(1)}, u32[]{:S(2)}, u32[]{:S(2)}) collective-permute-start(f32[2,2048]{1,0:T(2,128)S(1)} %merge_project.1.a_ref.after_hbm), channel_id=1, source_target_pairs={{0,2},{1,3},{2,0},{3,1},{4,6},{5,7},{6,4},{7,5},{8,10},{9,11},{10,... | collective-permute-start | bytes 49160 | tf_op jit(solution)/shard_map/ppermute | solution.py:276
  33.0 2.5 %collective-permute-start = (f32[2,2048]{1,0:T(2,128)S(1)}, f32[2,2048]{1,0:T(2,128)S(1)}, u32[]{:S(2)}, u32[]{:S(2)}) collective-permute-start(f32[2,2048]{1,0:T(2,128)S(1)} %merge_project.1.a_ref.after_hbm), channel_id=1, source_target_pairs={{0,1},{1,0},{2,3},{3,2},{4,5},{5,4},{6,7},{7,6},{8,9},{9,8},{10,11... | collective-permute-start | bytes 49160 | tf_op jit(solution)/shard_map/ppermute | solution.py:276
  35.5 1.3 %collective-permute-done.2.d_ref = f32[2,2048]{1,0:T(2,128)S(1)} collective-permute-done((f32[2,2048]{1,0:T(2,128)S(1)}, f32[2,2048]{1,0:T(2,128)S(1)}, u32[]{:S(2)}, u32[]{:S(2)}) %collective-permute-start.2) | collective-permute-done | bytes 16416 | tf_op jit(solution)/shard_map/ppermute | solution.py:276
  36.8 0.7 %collective-permute-done.1.c_ref = f32[2,2048]{1,0:T(2,128)S(1)} collective-permute-done((f32[2,2048]{1,0:T(2,128)S(1)}, f32[2,2048]{1,0:T(2,128)S(1)}, u32[]{:S(2)}, u32[]{:S(2)}) %collective-permute-start.1) | collective-permute-done | bytes 16416 | tf_op jit(solution)/shard_map/ppermute | solution.py:276
  37.5 0.0 collective-permute-done.b_ref
  37.5 0.0 slice-done
  37.5 0.0 slice-done.1
  37.5 0.0 copy-done
  37.5 0.0 copy-done.1
  37.5 1.9 %mlp.1 = (f32[2,2048]{1,0:T(2,128)S(1)}, f32[2,2048]{1,0:T(2,128)S(1)}) custom-call(bf16[32,4,2048]{2,1,0:T(4,128)(2,1)S(1)} %copy-done.1, bf16[2,2048,1024]{2,1,0:T(8,128)(2,1)S(1)} %bitcast.1, bf16[1024,2048]{1,0:T(8,128)(2,1)S(1)} %copy-done, f32[2,2048]{1,0:T(2,128)S(1)} %merge_project.1.a_ref.after_hbm, f32[2,2048]{1,0:T(2,128)S(1)} %collective-permute-done.b_ref, ...), custom_call_target="tpu_custom_call" | custom-call | tf_op jit(solution)/shard_map/mlp/pallas_call | solution.py:367
  39.5 2.0 %collective-permute-start.5 = (f32[2,2048]{1,0:T(2,128)S(1)}, f32[2,2048]{1,0:T(2,128)S(1)}, u32[]{:S(2)}, u32[]{:S(2)}) collective-permute-start(f32[2,2048]{1,0:T(2,128)S(1)} %get-tuple-element.25.a_ref), channel_id=1, source_target_pairs={{0,3},{1,2},{2,1},{3,0},{4,7},{5,6},{6,5},{7,4},{8,11},{9,10},{10,... | collective-permute-start | bytes 49160 | tf_op jit(solution)/shard_map/ppermute | solution.py:276
  41.5 1.1 %collective-permute-start.4 = (f32[2,2048]{1,0:T(2,128)S(1)}, f32[2,2048]{1,0:T(2,128)S(1)}, u32[]{:S(2)}, u32[]{:S(2)}) collective-permute-start(f32[2,2048]{1,0:T(2,128)S(1)} %get-tuple-element.25.a_ref), channel_id=1, source_target_pairs={{0,2},{1,3},{2,0},{3,1},{4,6},{5,7},{6,4},{7,5},{8,10},{9,11},{10,... | collective-permute-start | bytes 49160 | tf_op jit(solution)/shard_map/ppermute | solution.py:276
  42.6 0.3 collective-permute-start.3
  42.9 1.3 %collective-permute-done.5.d_ref = f32[2,2048]{1,0:T(2,128)S(1)} collective-permute-done((f32[2,2048]{1,0:T(2,128)S(1)}, f32[2,2048]{1,0:T(2,128)S(1)}, u32[]{:S(2)}, u32[]{:S(2)}) %collective-permute-start.5) | collective-permute-done | bytes 16416 | tf_op jit(solution)/shard_map/ppermute | solution.py:276
  44.2 2.5 %collective-permute-done.4.c_ref = f32[2,2048]{1,0:T(2,128)S(1)} collective-permute-done((f32[2,2048]{1,0:T(2,128)S(1)}, f32[2,2048]{1,0:T(2,128)S(1)}, u32[]{:S(2)}, u32[]{:S(2)}) %collective-permute-start.4) | collective-permute-done | bytes 16416 | tf_op jit(solution)/shard_map/ppermute | solution.py:276
  46.7 0.0 collective-permute-done.3.b_ref
  46.7 0.7 %last_sum.1 = bf16[64,2,512]{2,1,0:T(2,128)(2,1)} custom-call(f32[2,2048]{1,0:T(2,128)S(1)} %get-tuple-element.24.middle_ref, f32[2,2048]{1,0:T(2,128)S(1)} %get-tuple-element.25.a_ref, f32[2,2048]{1,0:T(2,128)S(1)} %collective-permute-done.3.b_ref, f32[2,2048]{1,0:T(2,128)S(1)} %collective-permute-done.4.c_ref, f32[2,2048]{1,0:T(2,128)S(1)} %collective-permute-done.5.d_ref), custom_call_target="tpu_custom_call" | custom-call | tf_op jit(solution)/shard_map/last_sum/pallas_call | solution.py:375
  47.4 4.9 %all-to-all-start.1 = ((bf16[64,2,512]{2,1,0:T(2,128)(2,1)}), bf16[64,2,512]{2,1,0:T(2,128)(2,1)S(1)}, u32[]{:S(2)}, u32[]{:S(2)}) async-start(bf16[64,2,512]{2,1,0:T(2,128)(2,1)} %last_sum.1), calls=%async_computation.1 | async-start | bytes 262144 | tf_op jit(solution)/shard_map/all_to_all | solution.py:383
  52.3 3.4 %projections.1 = (bf16[32,4,512]{2,1,0:T(4,128)(2,1)}, bf16[32,4,512]{2,1,0:T(4,128)(2,1)}, bf16[32,4,512]{2,1,0:T(4,128)(2,1)}) custom-call(f32[2,2048]{1,0:T(2,128)S(1)} %merge_project.1.a_ref.after_hbm, bf16[3,2048,512]{2,1,0:T(8,128)(2,1)} %w_hbm.5, bf16[128,512]{1,0:T(8,128)(2,1)S(1)} %get-tuple-element.26.q_rows, ...), custom_call_target="tpu_custom_call" | custom-call | tf_op jit(solution)/shard_map/projections/pallas_call | solution.py:355
  55.7 7.7 %all-to-all-done.1 = bf16[64,2,512]{2,1,0:T(2,128)(2,1)S(1)} async-done(((bf16[64,2,512]{2,1,0:T(2,128)(2,1)}), bf16[64,2,512]{2,1,0:T(2,128)(2,1)S(1)}, u32[]{:S(2)}, u32[]{:S(2)}) %all-to-all-start.1) | async-done | bytes 131104 | tf_op jit(solution)/shard_map/all_to_all | solution.py:383
  63.3 0.7 %reshape.11 = bf16[32,4,512]{2,1,0:T(4,128)(2,1)} reshape(bf16[64,2,512]{2,1,0:T(2,128)(2,1)S(1)} %all-to-all-done.1) | data formatting | bytes 262144 | tf_op jit(solution)/shard_map/reshape | solution.py:384
  (1 shorter events, 0.0 us)
Async XLA Ops:
  9.0 22.4 %all-to-all-start = ((bf16[64,16,128]{2,1,0:T(8,128)(2,1)}), bf16[64,16,128]{2,1,0:T(8,128)(2,1)S(1)}, u32[]{:S(2)}, u32[]{:S(2)}) async-start(bf16[64,16,128]{2,1,0:T(8,128)(2,1)} %get-tuple-element.17), calls=%async_computation | async-start | bytes 524288 | tf_op jit(solution)/shard_map/all_to_all | solution.py:325
  31.4 6.1 %slice-start = ((s8[8388608]{0:T(1024)(128)(4,1)}), s8[4194304]{0:T(1024)(128)(4,1)S(1)}, s32[]{:S(2)}) async-start(s8[8388608]{0:T(1024)(128)(4,1)} %bitcast), calls=%async_computation.2 | async-start | bytes 8388608
  31.4 6.1 %slice-start.1 = ((s8[8388608]{0:T(1024)(128)(4,1)}), s8[4194304]{0:T(1024)(128)(4,1)S(1)}, s32[]{:S(2)}) async-start(s8[8388608]{0:T(1024)(128)(4,1)} %bitcast), calls=%async_computation.3 | async-start | bytes 8388608
  31.4 6.1 %copy-start = (bf16[1024,2048]{1,0:T(8,128)(2,1)S(1)}, bf16[1024,2048]{1,0:T(8,128)(2,1)}, u32[]{:S(2)}) copy-start(bf16[1024,2048]{1,0:T(8,128)(2,1)} %wd_ref.1) | copy-start | bytes 12582916
  31.4 6.1 %copy-start.1 = (bf16[32,4,2048]{2,1,0:T(4,128)(2,1)S(1)}, bf16[32,4,2048]{2,1,0:T(4,128)(2,1)}, u32[]{:S(2)}) copy-start(bf16[32,4,2048]{2,1,0:T(4,128)(2,1)} %x_ref.1) | copy-start | bytes 1572868
  32.1 4.7 %collective-permute-start.2 = (f32[2,2048]{1,0:T(2,128)S(1)}, f32[2,2048]{1,0:T(2,128)S(1)}, u32[]{:S(2)}, u32[]{:S(2)}) collective-permute-start(f32[2,2048]{1,0:T(2,128)S(1)} %merge_project.1.a_ref.after_hbm), channel_id=1, source_target_pairs={{0,3},{1,2},{2,1},{3,0},{4,7},{5,6},{6,5},{7,4},{8,11},{9,10},{10,... | collective-permute-start | bytes 49160 | tf_op jit(solution)/shard_map/ppermute | solution.py:276
  32.2 5.4 %collective-permute-start.1 = (f32[2,2048]{1,0:T(2,128)S(1)}, f32[2,2048]{1,0:T(2,128)S(1)}, u32[]{:S(2)}, u32[]{:S(2)}) collective-permute-start(f32[2,2048]{1,0:T(2,128)S(1)} %merge_project.1.a_ref.after_hbm), channel_id=1, source_target_pairs={{0,2},{1,3},{2,0},{3,1},{4,6},{5,7},{6,4},{7,5},{8,10},{9,11},{10,... | collective-permute-start | bytes 49160 | tf_op jit(solution)/shard_map/ppermute | solution.py:276
  33.0 4.5 %collective-permute-start = (f32[2,2048]{1,0:T(2,128)S(1)}, f32[2,2048]{1,0:T(2,128)S(1)}, u32[]{:S(2)}, u32[]{:S(2)}) collective-permute-start(f32[2,2048]{1,0:T(2,128)S(1)} %merge_project.1.a_ref.after_hbm), channel_id=1, source_target_pairs={{0,1},{1,0},{2,3},{3,2},{4,5},{5,4},{6,7},{7,6},{8,9},{9,8},{10,11... | collective-permute-start | bytes 49160 | tf_op jit(solution)/shard_map/ppermute | solution.py:276
  39.5 4.7 %collective-permute-start.5 = (f32[2,2048]{1,0:T(2,128)S(1)}, f32[2,2048]{1,0:T(2,128)S(1)}, u32[]{:S(2)}, u32[]{:S(2)}) collective-permute-start(f32[2,2048]{1,0:T(2,128)S(1)} %get-tuple-element.25.a_ref), channel_id=1, source_target_pairs={{0,3},{1,2},{2,1},{3,0},{4,7},{5,6},{6,5},{7,4},{8,11},{9,10},{10,... | collective-permute-start | bytes 49160 | tf_op jit(solution)/shard_map/ppermute | solution.py:276
  41.5 5.2 %collective-permute-start.4 = (f32[2,2048]{1,0:T(2,128)S(1)}, f32[2,2048]{1,0:T(2,128)S(1)}, u32[]{:S(2)}, u32[]{:S(2)}) collective-permute-start(f32[2,2048]{1,0:T(2,128)S(1)} %get-tuple-element.25.a_ref), channel_id=1, source_target_pairs={{0,2},{1,3},{2,0},{3,1},{4,6},{5,7},{6,4},{7,5},{8,10},{9,11},{10,... | collective-permute-start | bytes 49160 | tf_op jit(solution)/shard_map/ppermute | solution.py:276
  42.6 4.1 %collective-permute-start.3 = (f32[2,2048]{1,0:T(2,128)S(1)}, f32[2,2048]{1,0:T(2,128)S(1)}, u32[]{:S(2)}, u32[]{:S(2)}) collective-permute-start(f32[2,2048]{1,0:T(2,128)S(1)} %get-tuple-element.25.a_ref), channel_id=1, source_target_pairs={{0,1},{1,0},{2,3},{3,2},{4,5},{5,4},{6,7},{7,6},{8,9},{9,8},{10,11... | collective-permute-start | bytes 49160 | tf_op jit(solution)/shard_map/ppermute | solution.py:276
  47.4 15.9 %all-to-all-start.1 = ((bf16[64,2,512]{2,1,0:T(2,128)(2,1)}), bf16[64,2,512]{2,1,0:T(2,128)(2,1)S(1)}, u32[]{:S(2)}, u32[]{:S(2)}) async-start(bf16[64,2,512]{2,1,0:T(2,128)(2,1)} %last_sum.1), calls=%async_computation.1 | async-start | bytes 262144 | tf_op jit(solution)/shard_map/all_to_all | solution.py:383

commit v7 on v6

--- a/solution.py
+++ b/solution.py
@@ -100,10 +100,11 @@
         sin_out[r * steps : (r + 2) * steps, :] = jnp.where(lane8 < DH // 2, -sine, sine)
 
     lane = lax.broadcasted_iota(jnp.int32, (tall, DH), 1)
-    empty = jnp.where(lane[0:half] == 0, NEG, 0.0).astype(BF16)
+    empty = jnp.where(lane[0:heads] % (DH // 2) == 0, NEG, 0.0).astype(BF16)
     for p in range(2 * reqs):
-        part_out[p, 0:half, :] = jnp.zeros((half, DH), BF16)
-        part_out[p, half : 2 * half, :] = empty
+        part_out[p, 0] = jnp.zeros((heads, DH), BF16)
+        part_out[p, 1] = jnp.zeros((heads, DH), BF16)
+        part_out[p, 2] = empty
 
     copy_x.wait()
     fetch(cv_hbm, cv_v, sem_v, 0)
@@ -139,8 +140,7 @@
         pieces = split3(jnp.broadcast_to(highest, scores.shape)) + split3(jnp.broadcast_to(total, scores.shape))
         stats = pieces[5]
         for i in range(4, -1, -1):
-            stats = jnp.where(many_lane == i, pieces[i], stats)
-        stats = stats.astype(BF16)
+            stats = jnp.where(many_lane % (DH // 2) == i, pieces[i], stats)
         arrive(cv_hbm, cv_v, sem_v, lo)
         for i in range(lo, lo + group):
             r = order_s[i]
@@ -150,8 +150,11 @@
             for h in range(1, heads):
                 o = jnp.where(row_head == h, wide[:, h * DH : (h + 1) * DH], o)
             for j in range(2):
-                part_out[2 * r + j, 0:half, :] = o[j * half : (j + 1) * half].astype(BF16)
-                part_out[2 * r + j, half : 2 * half, :] = stats[at + j * half : at + (j + 1) * half]
+                lo_row = 2 * j * heads
+                for k in range(2):
+                    part_out[2 * r + j, k] = o[lo_row + k * heads : lo_row + (k + 1) * heads].astype(BF16)
+                pair = [stats[at + lo_row + k * heads : at + lo_row + (k + 1) * heads] for k in range(2)]
+                part_out[2 * r + j, 2] = jnp.where(lane[0:heads] < DH // 2, pair[0], pair[1]).astype(BF16)
 
     attend(0)
     for lo in range(group, reqs, group):
@@ -213,18 +216,20 @@
 
 
 def merge_kernel(got_ref, fresh_ref, w_ref, out_ref, ctx_s):
-    half = fresh_ref.shape[1]
-    heads = half // 2
-    fresh_high = fresh_ref[1][:, 0:1]
-    stats = got_ref[:, half : 2 * half, :].astype(F32)
-    highest = (stats[:, :, 0:1] + stats[:, :, 1:2]) + stats[:, :, 2:3]
-    total = (stats[:, :, 3:4] + stats[:, :, 4:5]) + stats[:, :, 5:6]
-    top = jnp.maximum(jnp.max(highest, axis=0), fresh_high)
-    factor = jnp.exp(highest - top[None])
-    fresh_factor = jnp.exp(fresh_high - top)
-    whole = jnp.sum(factor * total, axis=0) + fresh_factor * fresh_ref[2][:, 0:1]
-    o = jnp.sum(factor * got_ref[:, 0:half, :].astype(F32), axis=0) + fresh_factor * fresh_ref[0]
-    ctx_s[...] = o / whole
+    heads = got_ref.shape[2]
+    stats = got_ref[:, 2].astype(F32)
+    for k in range(2):
+        span = slice(k * heads, (k + 1) * heads)
+        fresh, fresh_high, fresh_total = fresh_ref[0][span], fresh_ref[1][span, 0:1], fresh_ref[2][span, 0:1]
+        at = [stats[:, :, k * DH // 2 + i : k * DH // 2 + i + 1] for i in range(6)]
+        highest = (at[0] + at[1]) + at[2]
+        total = (at[3] + at[4]) + at[5]
+        top = jnp.maximum(jnp.max(highest, axis=0), fresh_high)
+        factor = jnp.exp(highest - top[None])
+        fresh_factor = jnp.exp(fresh_high - top)
+        whole = jnp.sum(factor * total, axis=0) + fresh_factor * fresh_total
+        o = jnp.sum(factor * got_ref[:, k].astype(F32), axis=0) + fresh_factor * fresh
+        ctx_s[span, :] = o / whole
     ctx = jnp.concatenate([ctx_s[pl.ds(h, 2, stride=heads), :] for h in range(heads)], axis=1)
     out_ref[...] = jnp.dot(ctx.astype(BF16), w_ref[...], preferred_element_type=F32)
 
@@ -294,7 +299,7 @@
     part, q_rows, q_own, normed, cosine, sine = pl.pallas_call(
         functools.partial(cached_kernel, group, reqs, steps, block, width),
         out_shape=(
-            jax.ShapeDtypeStruct((n_seq, tall, DH), BF16),
+            jax.ShapeDtypeStruct((n_seq, 3, heads, DH), BF16),
             jax.ShapeDtypeStruct((rows, width), BF16),
             jax.ShapeDtypeStruct((tall // 2, DH), F32),
             jax.ShapeDtypeStruct((rows, model), BF16),

time: 64.3 us -> 63 us (0.980)
  waiting for transfers between devices: 23.7 us -> 22.5 us
    all_to_all x1, waiting for transfers between devices: 10.1 us -> 8.99 us  [per_device(): got = lax.all_to_all(part, 'seq', 0, 0)]
where the time goes in v7:
time: 63 us; the launch traced here: 62.7 us
  waiting for transfers between devices  22.5 us (36%)
  starting transfers between devices  20.7 us (33%)
  Pallas kernels  18.1 us (29%)
  local copies, waits for them, and re-layouts  0.73 us (1%)
  between operations  0.72 us (1%)
    all_to_all x1, starting transfers between devices, per_device(): got = lax.all_to_all(part, 'seq', 0, 0)  9.32 us
    all_to_all x1, waiting for transfers between devices, per_device(): got = lax.all_to_all(part, 'seq', 0, 0)  8.99 us
    pallas_call x1, Pallas kernels, per_device(): pl.pallas_call(functools.partial(cached_kernel, group, reqs, steps, block...  8.39 us
    all_to_all x1, waiting for transfers between devices, per_device(): hidden = lax.all_to_all(hidden, 'seq', 0, 0)  7.67 us
    ppermute x6, starting transfers between devices, to_others(): lax.ppermute(values[k - 1], axis, [(i, i ^ k) for i in range(size)])  6.74 us
    ppermute x6, waiting for transfers between devices, to_others(): lax.ppermute(values[k - 1], axis, [(i, i ^ k) for i in range(size)])  5.86 us
    all_to_all x1, starting transfers between devices, per_device(): hidden = lax.all_to_all(hidden, 'seq', 0, 0)  4.65 us
    pallas_call x1, Pallas kernels, per_device(): pl.pallas_call(outputs_kernel, out_shape=(piece,) * 3, in_specs=[any_spac...  3.35 us
  transfers between devices with their start and end apart: 8, of which 6 were waited for; matrix products, arithmetic and copies ran while one was open for 0% of the time, Pallas kernels for 10%

profile of v7, /device:TPU:4, one launch (start us, length us, event | category | flops | bytes accessed | tf_op | source)
XLA Modules:
  0.0 62.7 jit_solution(13183005017256027331)
XLA Ops:
  0.6 8.4 %cached_attention.1 = (bf16[64,3,4,128]{3,2,1,0:T(4,128)(2,1)}, bf16[128,512]{1,0:T(8,128)(2,1)S(1)}, f32[8,128]{1,0:T(8,128)S(1)}, bf16[128,2048]{1,0:T(8,128)(...) custom-call(s32[32]{0:T(128)} %len_hbm.1, bf16[32,4,2048]{2,1,0:T(4,128)(2,1)} %x_ref.1, ...), custom_call_target="tpu_custom_call" | custom-call | tf_op jit(solution)/shard_map/cached_attention/pallas_call | solution.py:299
  9.0 9.3 %all-to-all-start = ((bf16[64,3,4,128]{3,2,1,0:T(4,128)(2,1)}), bf16[64,3,4,128]{3,2,1,0:T(4,128)(2,1)S(1)}, u32[]{:S(2)}, u32[]{:S(2)}) async-start(bf16[64,3,4,128]{3,2,1,0:T(4,128)(2,1)} %get-tuple-element.17), calls=%async_computation | async-start | bytes 393216 | tf_op jit(solution)/shard_map/all_to_all | solution.py:330
  18.4 2.9 %new_tokens.1 = (f32[3,8,128]{2,1,0:T(8,128)S(1)}, bf16[512,2048]{1,0:T(8,128)(2,1)S(1)}) custom-call(bf16[3,2048,512]{2,1,0:T(8,128)(2,1)} %w_hbm.5, bf16[512,2048]{1,0:T(8,128)(2,1)} %proj_hbm.1, f32[8,128]{1,0:T(8,128)S(1)} %get-tuple-element.18.q_own, bf16[128,2048]{1,0:T(8,128)(2,1)S(1)} %get-tuple-element.19.normed, ...), custom_call_target="tpu_custom_call" | custom-call | tf_op jit(solution)/shard_map/new_tokens/pallas_call | solution.py:332
  21.3 9.0 %all-to-all-done.got_ref = bf16[64,3,4,128]{3,2,1,0:T(4,128)(2,1)S(1)} async-done(((bf16[64,3,4,128]{3,2,1,0:T(4,128)(2,1)}), bf16[64,3,4,128]{3,2,1,0:T(4,128)(2,1)S(1)}, u32[]{:S(2)}, u32[]{:S(2)}) %all-to-all-start) | async-done | bytes 196640 | tf_op jit(solution)/shard_map/all_to_all | solution.py:330
  30.3 0.0 slice-start
  30.3 0.0 slice-start.1
  30.3 0.0 copy-start
  30.3 0.0 copy-start.1
  30.3 0.8 %merge_project.1.a_ref.after_hbm = f32[2,2048]{1,0:T(2,128)S(1)} custom-call(bf16[64,3,4,128]{3,2,1,0:T(4,128)(2,1)S(1)} %all-to-all-done.got_ref, f32[3,8,128]{2,1,0:T(8,128)S(1)} %get-tuple-element.22.fresh_ref, bf16[512,2048]{1,0:T(8,128)(2,1)S(1)} %get-tuple-element.23.w_ref), custom_call_target="tpu_custom_call" | custom-call | flops 10000000000 | bytes 62914560 | tf_op jit(solution)/shard_map/merge_project/pallas_call | solution.py:347
  31.1 0.0 collective-permute-start.2
  31.1 0.9 %collective-permute-start.1 = (f32[2,2048]{1,0:T(2,128)S(1)}, f32[2,2048]{1,0:T(2,128)S(1)}, u32[]{:S(2)}, u32[]{:S(2)}) collective-permute-start(f32[2,2048]{1,0:T(2,128)S(1)} %merge_project.1.a_ref.after_hbm), channel_id=1, source_target_pairs={{0,2},{1,3},{2,0},{3,1},{4,6},{5,7},{6,4},{7,5},{8,10},{9,11},{10,... | collective-permute-start | bytes 49160 | tf_op jit(solution)/shard_map/ppermute | solution.py:281
  32.0 2.4 %collective-permute-start = (f32[2,2048]{1,0:T(2,128)S(1)}, f32[2,2048]{1,0:T(2,128)S(1)}, u32[]{:S(2)}, u32[]{:S(2)}) collective-permute-start(f32[2,2048]{1,0:T(2,128)S(1)} %merge_project.1.a_ref.after_hbm), channel_id=1, source_target_pairs={{0,1},{1,0},{2,3},{3,2},{4,5},{5,4},{6,7},{7,6},{8,9},{9,8},{10,11... | collective-permute-start | bytes 49160 | tf_op jit(solution)/shard_map/ppermute | solution.py:281
  34.4 1.3 %collective-permute-done.2.d_ref = f32[2,2048]{1,0:T(2,128)S(1)} collective-permute-done((f32[2,2048]{1,0:T(2,128)S(1)}, f32[2,2048]{1,0:T(2,128)S(1)}, u32[]{:S(2)}, u32[]{:S(2)}) %collective-permute-start.2) | collective-permute-done | bytes 16416 | tf_op jit(solution)/shard_map/ppermute | solution.py:281
  35.7 0.7 %collective-permute-done.1.c_ref = f32[2,2048]{1,0:T(2,128)S(1)} collective-permute-done((f32[2,2048]{1,0:T(2,128)S(1)}, f32[2,2048]{1,0:T(2,128)S(1)}, u32[]{:S(2)}, u32[]{:S(2)}) %collective-permute-start.1) | collective-permute-done | bytes 16416 | tf_op jit(solution)/shard_map/ppermute | solution.py:281
  36.4 0.0 collective-permute-done.b_ref
  36.4 0.0 slice-done
  36.4 0.0 slice-done.1
  36.4 0.0 copy-done
  36.4 0.0 copy-done.1
  36.5 1.9 %mlp.1 = (f32[2,2048]{1,0:T(2,128)S(1)}, f32[2,2048]{1,0:T(2,128)S(1)}) custom-call(bf16[32,4,2048]{2,1,0:T(4,128)(2,1)S(1)} %copy-done.1, bf16[2,2048,1024]{2,1,0:T(8,128)(2,1)S(1)} %bitcast.1, bf16[1024,2048]{1,0:T(8,128)(2,1)S(1)} %copy-done, f32[2,2048]{1,0:T(2,128)S(1)} %merge_project.1.a_ref.after_hbm, f32[2,2048]{1,0:T(2,128)S(1)} %collective-permute-done.b_ref, ...), custom_call_target="tpu_custom_call" | custom-call | tf_op jit(solution)/shard_map/mlp/pallas_call | solution.py:372
  38.4 2.0 %collective-permute-start.5 = (f32[2,2048]{1,0:T(2,128)S(1)}, f32[2,2048]{1,0:T(2,128)S(1)}, u32[]{:S(2)}, u32[]{:S(2)}) collective-permute-start(f32[2,2048]{1,0:T(2,128)S(1)} %get-tuple-element.25.a_ref), channel_id=1, source_target_pairs={{0,3},{1,2},{2,1},{3,0},{4,7},{5,6},{6,5},{7,4},{8,11},{9,10},{10,... | collective-permute-start | bytes 49160 | tf_op jit(solution)/shard_map/ppermute | solution.py:281
  40.4 1.1 %collective-permute-start.4 = (f32[2,2048]{1,0:T(2,128)S(1)}, f32[2,2048]{1,0:T(2,128)S(1)}, u32[]{:S(2)}, u32[]{:S(2)}) collective-permute-start(f32[2,2048]{1,0:T(2,128)S(1)} %get-tuple-element.25.a_ref), channel_id=1, source_target_pairs={{0,2},{1,3},{2,0},{3,1},{4,6},{5,7},{6,4},{7,5},{8,10},{9,11},{10,... | collective-permute-start | bytes 49160 | tf_op jit(solution)/shard_map/ppermute | solution.py:281
  41.5 0.3 collective-permute-start.3
  41.8 1.3 %collective-permute-done.5.d_ref = f32[2,2048]{1,0:T(2,128)S(1)} collective-permute-done((f32[2,2048]{1,0:T(2,128)S(1)}, f32[2,2048]{1,0:T(2,128)S(1)}, u32[]{:S(2)}, u32[]{:S(2)}) %collective-permute-start.5) | collective-permute-done | bytes 16416 | tf_op jit(solution)/shard_map/ppermute | solution.py:281
  43.1 2.5 %collective-permute-done.4.c_ref = f32[2,2048]{1,0:T(2,128)S(1)} collective-permute-done((f32[2,2048]{1,0:T(2,128)S(1)}, f32[2,2048]{1,0:T(2,128)S(1)}, u32[]{:S(2)}, u32[]{:S(2)}) %collective-permute-start.4) | collective-permute-done | bytes 16416 | tf_op jit(solution)/shard_map/ppermute | solution.py:281
  45.6 0.0 collective-permute-done.3.b_ref
  45.6 0.7 %last_sum.1 = bf16[64,2,512]{2,1,0:T(2,128)(2,1)} custom-call(f32[2,2048]{1,0:T(2,128)S(1)} %get-tuple-element.24.middle_ref, f32[2,2048]{1,0:T(2,128)S(1)} %get-tuple-element.25.a_ref, f32[2,2048]{1,0:T(2,128)S(1)} %collective-permute-done.3.b_ref, f32[2,2048]{1,0:T(2,128)S(1)} %collective-permute-done.4.c_ref, f32[2,2048]{1,0:T(2,128)S(1)} %collective-permute-done.5.d_ref), custom_call_target="tpu_custom_call" | custom-call | tf_op jit(solution)/shard_map/last_sum/pallas_call | solution.py:380
  46.3 4.7 %all-to-all-start.1 = ((bf16[64,2,512]{2,1,0:T(2,128)(2,1)}), bf16[64,2,512]{2,1,0:T(2,128)(2,1)S(1)}, u32[]{:S(2)}, u32[]{:S(2)}) async-start(bf16[64,2,512]{2,1,0:T(2,128)(2,1)} %last_sum.1), calls=%async_computation.1 | async-start | bytes 262144 | tf_op jit(solution)/shard_map/all_to_all | solution.py:388
  51.0 3.4 %projections.1 = (bf16[32,4,512]{2,1,0:T(4,128)(2,1)}, bf16[32,4,512]{2,1,0:T(4,128)(2,1)}, bf16[32,4,512]{2,1,0:T(4,128)(2,1)}) custom-call(f32[2,2048]{1,0:T(2,128)S(1)} %merge_project.1.a_ref.after_hbm, bf16[3,2048,512]{2,1,0:T(8,128)(2,1)} %w_hbm.5, bf16[128,512]{1,0:T(8,128)(2,1)S(1)} %get-tuple-element.26.q_rows, ...), custom_call_target="tpu_custom_call" | custom-call | tf_op jit(solution)/shard_map/projections/pallas_call | solution.py:360
  54.4 7.7 %all-to-all-done.1 = bf16[64,2,512]{2,1,0:T(2,128)(2,1)S(1)} async-done(((bf16[64,2,512]{2,1,0:T(2,128)(2,1)}), bf16[64,2,512]{2,1,0:T(2,128)(2,1)S(1)}, u32[]{:S(2)}, u32[]{:S(2)}) %all-to-all-start.1) | async-done | bytes 131104 | tf_op jit(solution)/shard_map/all_to_all | solution.py:388
  62.0 0.7 %reshape.11 = bf16[32,4,512]{2,1,0:T(4,128)(2,1)} reshape(bf16[64,2,512]{2,1,0:T(2,128)(2,1)S(1)} %all-to-all-done.1) | data formatting | bytes 262144 | tf_op jit(solution)/shard_map/reshape | solution.py:389
  (1 shorter events, 0.0 us)
Async XLA Ops:
  9.0 21.2 %all-to-all-start = ((bf16[64,3,4,128]{3,2,1,0:T(4,128)(2,1)}), bf16[64,3,4,128]{3,2,1,0:T(4,128)(2,1)S(1)}, u32[]{:S(2)}, u32[]{:S(2)}) async-start(bf16[64,3,4,128]{3,2,1,0:T(4,128)(2,1)} %get-tuple-element.17), calls=%async_computation | async-start | bytes 393216 | tf_op jit(solution)/shard_map/all_to_all | solution.py:330
  30.3 6.2 %slice-start = ((s8[8388608]{0:T(1024)(128)(4,1)}), s8[4194304]{0:T(1024)(128)(4,1)S(1)}, s32[]{:S(2)}) async-start(s8[8388608]{0:T(1024)(128)(4,1)} %bitcast), calls=%async_computation.2 | async-start | bytes 8388608
  30.3 6.2 %slice-start.1 = ((s8[8388608]{0:T(1024)(128)(4,1)}), s8[4194304]{0:T(1024)(128)(4,1)S(1)}, s32[]{:S(2)}) async-start(s8[8388608]{0:T(1024)(128)(4,1)} %bitcast), calls=%async_computation.3 | async-start | bytes 8388608
  30.3 6.2 %copy-start = (bf16[1024,2048]{1,0:T(8,128)(2,1)S(1)}, bf16[1024,2048]{1,0:T(8,128)(2,1)}, u32[]{:S(2)}) copy-start(bf16[1024,2048]{1,0:T(8,128)(2,1)} %wd_ref.1) | copy-start | bytes 12582916
  30.3 6.2 %copy-start.1 = (bf16[32,4,2048]{2,1,0:T(4,128)(2,1)S(1)}, bf16[32,4,2048]{2,1,0:T(4,128)(2,1)}, u32[]{:S(2)}) copy-start(bf16[32,4,2048]{2,1,0:T(4,128)(2,1)} %x_ref.1) | copy-start | bytes 1572868
  31.1 4.7 %collective-permute-start.2 = (f32[2,2048]{1,0:T(2,128)S(1)}, f32[2,2048]{1,0:T(2,128)S(1)}, u32[]{:S(2)}, u32[]{:S(2)}) collective-permute-start(f32[2,2048]{1,0:T(2,128)S(1)} %merge_project.1.a_ref.after_hbm), channel_id=1, source_target_pairs={{0,3},{1,2},{2,1},{3,0},{4,7},{5,6},{6,5},{7,4},{8,11},{9,10},{10,... | collective-permute-start | bytes 49160 | tf_op jit(solution)/shard_map/ppermute | solution.py:281
  31.1 5.4 %collective-permute-start.1 = (f32[2,2048]{1,0:T(2,128)S(1)}, f32[2,2048]{1,0:T(2,128)S(1)}, u32[]{:S(2)}, u32[]{:S(2)}) collective-permute-start(f32[2,2048]{1,0:T(2,128)S(1)} %merge_project.1.a_ref.after_hbm), channel_id=1, source_target_pairs={{0,2},{1,3},{2,0},{3,1},{4,6},{5,7},{6,4},{7,5},{8,10},{9,11},{10,... | collective-permute-start | bytes 49160 | tf_op jit(solution)/shard_map/ppermute | solution.py:281
  32.0 4.4 %collective-permute-start = (f32[2,2048]{1,0:T(2,128)S(1)}, f32[2,2048]{1,0:T(2,128)S(1)}, u32[]{:S(2)}, u32[]{:S(2)}) collective-permute-start(f32[2,2048]{1,0:T(2,128)S(1)} %merge_project.1.a_ref.after_hbm), channel_id=1, source_target_pairs={{0,1},{1,0},{2,3},{3,2},{4,5},{5,4},{6,7},{7,6},{8,9},{9,8},{10,11... | collective-permute-start | bytes 49160 | tf_op jit(solution)/shard_map/ppermute | solution.py:281
  38.4 4.7 %collective-permute-start.5 = (f32[2,2048]{1,0:T(2,128)S(1)}, f32[2,2048]{1,0:T(2,128)S(1)}, u32[]{:S(2)}, u32[]{:S(2)}) collective-permute-start(f32[2,2048]{1,0:T(2,128)S(1)} %get-tuple-element.25.a_ref), channel_id=1, source_target_pairs={{0,3},{1,2},{2,1},{3,0},{4,7},{5,6},{6,5},{7,4},{8,11},{9,10},{10,... | collective-permute-start | bytes 49160 | tf_op jit(solution)/shard_map/ppermute | solution.py:281
  40.4 5.2 %collective-permute-start.4 = (f32[2,2048]{1,0:T(2,128)S(1)}, f32[2,2048]{1,0:T(2,128)S(1)}, u32[]{:S(2)}, u32[]{:S(2)}) collective-permute-start(f32[2,2048]{1,0:T(2,128)S(1)} %get-tuple-element.25.a_ref), channel_id=1, source_target_pairs={{0,2},{1,3},{2,0},{3,1},{4,6},{5,7},{6,4},{7,5},{8,10},{9,11},{10,... | collective-permute-start | bytes 49160 | tf_op jit(solution)/shard_map/ppermute | solution.py:281
  41.5 4.1 %collective-permute-start.3 = (f32[2,2048]{1,0:T(2,128)S(1)}, f32[2,2048]{1,0:T(2,128)S(1)}, u32[]{:S(2)}, u32[]{:S(2)}) collective-permute-start(f32[2,2048]{1,0:T(2,128)S(1)} %get-tuple-element.25.a_ref), channel_id=1, source_target_pairs={{0,1},{1,0},{2,3},{3,2},{4,5},{5,4},{6,7},{7,6},{8,9},{9,8},{10,11... | collective-permute-start | bytes 49160 | tf_op jit(solution)/shard_map/ppermute | solution.py:281
  46.3 15.7 %all-to-all-start.1 = ((bf16[64,2,512]{2,1,0:T(2,128)(2,1)}), bf16[64,2,512]{2,1,0:T(2,128)(2,1)S(1)}, u32[]{:S(2)}, u32[]{:S(2)}) async-start(bf16[64,2,512]{2,1,0:T(2,128)(2,1)} %last_sum.1), calls=%async_computation.1 | async-start | bytes 262144 | tf_op jit(solution)/shard_map/all_to_all | solution.py:388

commit v8 on v7

--- a/solution.py
+++ b/solution.py
@@ -376,7 +376,8 @@
         out_specs=(vmem,) * 2,
         compiler_params=pltpu.CompilerParams(vmem_limit_bytes=8 << 20),
         name="mlp",
-    )(inputs, w_gate_up, w_down, mine, *others)
+    )(inputs, w_gate_up, w_down, mine, others[0], others[2], others[1])
+    back = to_others([down] * 3, "mp")
     hidden = pl.pallas_call(
         last_kernel,
         out_shape=jax.ShapeDtypeStruct((n_seq, 2, cols), BF16),
@@ -384,7 +385,7 @@
         out_specs=vmem,
         compiler_params=pltpu.CompilerParams(vmem_limit_bytes=4 << 20),
         name="last_sum",
-    )(middle, down, *to_others([down] * 3, "mp"))
+    )(middle, down, back[0], back[2], back[1])
     hidden = lax.all_to_all(hidden, "seq", 0, 0)
     return (hidden.reshape(reqs, steps, cols), queries, new_keys, new_values)
 

time: 63 us -> 63.8 us (1.013)
  no operation moved by 1% of the time
where the time goes in v8:
time: 63.8 us; the launch traced here: 63.1 us
  waiting for transfers between devices  22.3 us (35%)
  starting transfers between devices  21.3 us (33%)
  Pallas kernels  18.1 us (28%)
  local copies, waits for them, and re-layouts  0.73 us (1%)
  between operations  0.71 us (1%)
    all_to_all x1, starting transfers between devices, per_device(): got = lax.all_to_all(part, 'seq', 0, 0)  9.32 us
    all_to_all x1, waiting for transfers between devices, per_device(): got = lax.all_to_all(part, 'seq', 0, 0)  8.99 us
    pallas_call x1, Pallas kernels, per_device(): pl.pallas_call(functools.partial(cached_kernel, group, reqs, steps, block...  8.39 us
    all_to_all x1, waiting for transfers between devices, per_device(): hidden = lax.all_to_all(hidden, 'seq', 0, 0)  7.71 us
    ppermute x6, starting transfers between devices, to_others(): lax.ppermute(values[k - 1], axis, [(i, i ^ k) for i in range(size)])  7.31 us
    ppermute x6, waiting for transfers between devices, to_others(): lax.ppermute(values[k - 1], axis, [(i, i ^ k) for i in range(size)])  5.58 us
    all_to_all x1, starting transfers between devices, per_device(): hidden = lax.all_to_all(hidden, 'seq', 0, 0)  4.65 us
    pallas_call x1, Pallas kernels, per_device(): pl.pallas_call(outputs_kernel, out_shape=(piece,) * 3, in_specs=[any_spac...  3.35 us
  transfers between devices with their start and end apart: 8, of which 6 were waited for; matrix products, arithmetic and copies ran while one was open for 0% of the time, Pallas kernels for 10%

profile of v8, /device:TPU:4, one launch (start us, length us, event | category | flops | bytes accessed | tf_op | source)
XLA Modules:
  0.0 63.1 jit_solution(4218162614453312721)
XLA Ops:
  0.6 8.4 %cached_attention.1 = (bf16[64,3,4,128]{3,2,1,0:T(4,128)(2,1)}, bf16[128,512]{1,0:T(8,128)(2,1)S(1)}, f32[8,128]{1,0:T(8,128)S(1)}, bf16[128,2048]{1,0:T(8,128)(...) custom-call(s32[32]{0:T(128)} %len_hbm.1, bf16[32,4,2048]{2,1,0:T(4,128)(2,1)} %x_ref.1, ...), custom_call_target="tpu_custom_call" | custom-call | tf_op jit(solution)/shard_map/cached_attention/pallas_call | solution.py:299
  9.0 9.3 %all-to-all-start = ((bf16[64,3,4,128]{3,2,1,0:T(4,128)(2,1)}), bf16[64,3,4,128]{3,2,1,0:T(4,128)(2,1)S(1)}, u32[]{:S(2)}, u32[]{:S(2)}) async-start(bf16[64,3,4,128]{3,2,1,0:T(4,128)(2,1)} %get-tuple-element.17), calls=%async_computation | async-start | bytes 393216 | tf_op jit(solution)/shard_map/all_to_all | solution.py:330
  18.4 2.9 %new_tokens.1 = (f32[3,8,128]{2,1,0:T(8,128)S(1)}, bf16[512,2048]{1,0:T(8,128)(2,1)S(1)}) custom-call(bf16[3,2048,512]{2,1,0:T(8,128)(2,1)} %w_hbm.5, bf16[512,2048]{1,0:T(8,128)(2,1)} %proj_hbm.1, f32[8,128]{1,0:T(8,128)S(1)} %get-tuple-element.18.q_own, bf16[128,2048]{1,0:T(8,128)(2,1)S(1)} %get-tuple-element.19.normed, ...), custom_call_target="tpu_custom_call" | custom-call | tf_op jit(solution)/shard_map/new_tokens/pallas_call | solution.py:332
  21.3 9.0 %all-to-all-done.got_ref = bf16[64,3,4,128]{3,2,1,0:T(4,128)(2,1)S(1)} async-done(((bf16[64,3,4,128]{3,2,1,0:T(4,128)(2,1)}), bf16[64,3,4,128]{3,2,1,0:T(4,128)(2,1)S(1)}, u32[]{:S(2)}, u32[]{:S(2)}) %all-to-all-start) | async-done | bytes 196640 | tf_op jit(solution)/shard_map/all_to_all | solution.py:330
  30.3 0.0 slice-start
  30.3 0.0 slice-start.1
  30.3 0.0 copy-start
  30.3 0.0 copy-start.1
  30.3 0.8 %merge_project.1.a_ref.after_hbm = f32[2,2048]{1,0:T(2,128)S(1)} custom-call(bf16[64,3,4,128]{3,2,1,0:T(4,128)(2,1)S(1)} %all-to-all-done.got_ref, f32[3,8,128]{2,1,0:T(8,128)S(1)} %get-tuple-element.22.fresh_ref, bf16[512,2048]{1,0:T(8,128)(2,1)S(1)} %get-tuple-element.23.w_ref), custom_call_target="tpu_custom_call" | custom-call | flops 10000000000 | bytes 62914560 | tf_op jit(solution)/shard_map/merge_project/pallas_call | solution.py:347
  31.1 0.8 %collective-permute-start.2 = (f32[2,2048]{1,0:T(2,128)S(1)}, f32[2,2048]{1,0:T(2,128)S(1)}, u32[]{:S(2)}, u32[]{:S(2)}) collective-permute-start(f32[2,2048]{1,0:T(2,128)S(1)} %merge_project.1.a_ref.after_hbm), channel_id=1, source_target_pairs={{0,2},{1,3},{2,0},{3,1},{4,6},{5,7},{6,4},{7,5},{8,10},{9,11},{10,... | collective-permute-start | bytes 49160 | tf_op jit(solution)/shard_map/ppermute | solution.py:281
  31.9 0.0 collective-permute-start.1
  31.9 2.8 %collective-permute-start = (f32[2,2048]{1,0:T(2,128)S(1)}, f32[2,2048]{1,0:T(2,128)S(1)}, u32[]{:S(2)}, u32[]{:S(2)}) collective-permute-start(f32[2,2048]{1,0:T(2,128)S(1)} %merge_project.1.a_ref.after_hbm), channel_id=1, source_target_pairs={{0,1},{1,0},{2,3},{3,2},{4,5},{5,4},{6,7},{7,6},{8,9},{9,8},{10,11... | collective-permute-start | bytes 49160 | tf_op jit(solution)/shard_map/ppermute | solution.py:281
  34.7 1.6 %collective-permute-done.2.d_ref = f32[2,2048]{1,0:T(2,128)S(1)} collective-permute-done((f32[2,2048]{1,0:T(2,128)S(1)}, f32[2,2048]{1,0:T(2,128)S(1)}, u32[]{:S(2)}, u32[]{:S(2)}) %collective-permute-start.2) | collective-permute-done | bytes 16416 | tf_op jit(solution)/shard_map/ppermute | solution.py:281
  36.3 0.4 collective-permute-done.1.c_ref
  36.7 0.0 collective-permute-done.b_ref
  36.7 0.0 slice-done
  36.7 0.0 slice-done.1
  36.7 0.0 copy-done
  36.7 0.0 copy-done.1
  36.7 1.9 %mlp.1 = (f32[2,2048]{1,0:T(2,128)S(1)}, f32[2,2048]{1,0:T(2,128)S(1)}) custom-call(bf16[32,4,2048]{2,1,0:T(4,128)(2,1)S(1)} %copy-done.1, bf16[2,2048,1024]{2,1,0:T(8,128)(2,1)S(1)} %bitcast.1, bf16[1024,2048]{1,0:T(8,128)(2,1)S(1)} %copy-done, f32[2,2048]{1,0:T(2,128)S(1)} %merge_project.1.a_ref.after_hbm, f32[2,2048]{1,0:T(2,128)S(1)} %collective-permute-done.b_ref, ...), custom_call_target="tpu_custom_call" | custom-call | tf_op jit(solution)/shard_map/mlp/pallas_call | solution.py:372
  38.6 2.6 %collective-permute-start.5 = (f32[2,2048]{1,0:T(2,128)S(1)}, f32[2,2048]{1,0:T(2,128)S(1)}, u32[]{:S(2)}, u32[]{:S(2)}) collective-permute-start(f32[2,2048]{1,0:T(2,128)S(1)} %get-tuple-element.25.a_ref), channel_id=1, source_target_pairs={{0,2},{1,3},{2,0},{3,1},{4,6},{5,7},{6,4},{7,5},{8,10},{9,11},{10,... | collective-permute-start | bytes 49160 | tf_op jit(solution)/shard_map/ppermute | solution.py:281
  41.3 0.3 collective-permute-start.4
  41.6 0.7 %collective-permute-start.3 = (f32[2,2048]{1,0:T(2,128)S(1)}, f32[2,2048]{1,0:T(2,128)S(1)}, u32[]{:S(2)}, u32[]{:S(2)}) collective-permute-start(f32[2,2048]{1,0:T(2,128)S(1)} %get-tuple-element.25.a_ref), channel_id=1, source_target_pairs={{0,1},{1,0},{2,3},{3,2},{4,5},{5,4},{6,7},{7,6},{8,9},{9,8},{10,11... | collective-permute-start | bytes 49160 | tf_op jit(solution)/shard_map/ppermute | solution.py:281
  42.3 1.6 %collective-permute-done.5.d_ref = f32[2,2048]{1,0:T(2,128)S(1)} collective-permute-done((f32[2,2048]{1,0:T(2,128)S(1)}, f32[2,2048]{1,0:T(2,128)S(1)}, u32[]{:S(2)}, u32[]{:S(2)}) %collective-permute-start.5) | collective-permute-done | bytes 16416 | tf_op jit(solution)/shard_map/ppermute | solution.py:281
  43.9 2.0 %collective-permute-done.4.c_ref = f32[2,2048]{1,0:T(2,128)S(1)} collective-permute-done((f32[2,2048]{1,0:T(2,128)S(1)}, f32[2,2048]{1,0:T(2,128)S(1)}, u32[]{:S(2)}, u32[]{:S(2)}) %collective-permute-start.4) | collective-permute-done | bytes 16416 | tf_op jit(solution)/shard_map/ppermute | solution.py:281
  45.9 0.0 collective-permute-done.3.b_ref
  45.9 0.7 %last_sum.1 = bf16[64,2,512]{2,1,0:T(2,128)(2,1)} custom-call(f32[2,2048]{1,0:T(2,128)S(1)} %get-tuple-element.24.middle_ref, f32[2,2048]{1,0:T(2,128)S(1)} %get-tuple-element.25.a_ref, f32[2,2048]{1,0:T(2,128)S(1)} %collective-permute-done.3.b_ref, f32[2,2048]{1,0:T(2,128)S(1)} %collective-permute-done.4.c_ref, f32[2,2048]{1,0:T(2,128)S(1)} %collective-permute-done.5.d_ref), custom_call_target="tpu_custom_call" | custom-call | tf_op jit(solution)/shard_map/last_sum/pallas_call | solution.py:381
  46.6 4.7 %all-to-all-start.1 = ((bf16[64,2,512]{2,1,0:T(2,128)(2,1)}), bf16[64,2,512]{2,1,0:T(2,128)(2,1)S(1)}, u32[]{:S(2)}, u32[]{:S(2)}) async-start(bf16[64,2,512]{2,1,0:T(2,128)(2,1)} %last_sum.1), calls=%async_computation.1 | async-start | bytes 262144 | tf_op jit(solution)/shard_map/all_to_all | solution.py:389
  51.3 3.4 %projections.1 = (bf16[32,4,512]{2,1,0:T(4,128)(2,1)}, bf16[32,4,512]{2,1,0:T(4,128)(2,1)}, bf16[32,4,512]{2,1,0:T(4,128)(2,1)}) custom-call(f32[2,2048]{1,0:T(2,128)S(1)} %merge_project.1.a_ref.after_hbm, bf16[3,2048,512]{2,1,0:T(8,128)(2,1)} %w_hbm.5, bf16[128,512]{1,0:T(8,128)(2,1)S(1)} %get-tuple-element.26.q_rows, ...), custom_call_target="tpu_custom_call" | custom-call | tf_op jit(solution)/shard_map/projections/pallas_call | solution.py:360
  54.7 7.7 %all-to-all-done.1 = bf16[64,2,512]{2,1,0:T(2,128)(2,1)S(1)} async-done(((bf16[64,2,512]{2,1,0:T(2,128)(2,1)}), bf16[64,2,512]{2,1,0:T(2,128)(2,1)S(1)}, u32[]{:S(2)}, u32[]{:S(2)}) %all-to-all-start.1) | async-done | bytes 131104 | tf_op jit(solution)/shard_map/all_to_all | solution.py:389
  62.4 0.7 %reshape.11 = bf16[32,4,512]{2,1,0:T(4,128)(2,1)} reshape(bf16[64,2,512]{2,1,0:T(2,128)(2,1)S(1)} %all-to-all-done.1) | data formatting | bytes 262144 | tf_op jit(solution)/shard_map/reshape | solution.py:390
  (1 shorter events, 0.0 us)
Async XLA Ops:
  9.0 21.2 %all-to-all-start = ((bf16[64,3,4,128]{3,2,1,0:T(4,128)(2,1)}), bf16[64,3,4,128]{3,2,1,0:T(4,128)(2,1)S(1)}, u32[]{:S(2)}, u32[]{:S(2)}) async-start(bf16[64,3,4,128]{3,2,1,0:T(4,128)(2,1)} %get-tuple-element.17), calls=%async_computation | async-start | bytes 393216 | tf_op jit(solution)/shard_map/all_to_all | solution.py:330
  30.3 6.4 %slice-start = ((s8[8388608]{0:T(1024)(128)(4,1)}), s8[4194304]{0:T(1024)(128)(4,1)S(1)}, s32[]{:S(2)}) async-start(s8[8388608]{0:T(1024)(128)(4,1)} %bitcast), calls=%async_computation.2 | async-start | bytes 8388608
  30.3 6.4 %slice-start.1 = ((s8[8388608]{0:T(1024)(128)(4,1)}), s8[4194304]{0:T(1024)(128)(4,1)S(1)}, s32[]{:S(2)}) async-start(s8[8388608]{0:T(1024)(128)(4,1)} %bitcast), calls=%async_computation.3 | async-start | bytes 8388608
  30.3 6.4 %copy-start = (bf16[1024,2048]{1,0:T(8,128)(2,1)S(1)}, bf16[1024,2048]{1,0:T(8,128)(2,1)}, u32[]{:S(2)}) copy-start(bf16[1024,2048]{1,0:T(8,128)(2,1)} %wd_ref.1) | copy-start | bytes 12582916
  30.3 6.4 %copy-start.1 = (bf16[32,4,2048]{2,1,0:T(4,128)(2,1)S(1)}, bf16[32,4,2048]{2,1,0:T(4,128)(2,1)}, u32[]{:S(2)}) copy-start(bf16[32,4,2048]{2,1,0:T(4,128)(2,1)} %x_ref.1) | copy-start | bytes 1572868
  31.1 5.3 %collective-permute-start.2 = (f32[2,2048]{1,0:T(2,128)S(1)}, f32[2,2048]{1,0:T(2,128)S(1)}, u32[]{:S(2)}, u32[]{:S(2)}) collective-permute-start(f32[2,2048]{1,0:T(2,128)S(1)} %merge_project.1.a_ref.after_hbm), channel_id=1, source_target_pairs={{0,2},{1,3},{2,0},{3,1},{4,6},{5,7},{6,4},{7,5},{8,10},{9,11},{10,... | collective-permute-start | bytes 49160 | tf_op jit(solution)/shard_map/ppermute | solution.py:281
  31.9 4.8 %collective-permute-start.1 = (f32[2,2048]{1,0:T(2,128)S(1)}, f32[2,2048]{1,0:T(2,128)S(1)}, u32[]{:S(2)}, u32[]{:S(2)}) collective-permute-start(f32[2,2048]{1,0:T(2,128)S(1)} %merge_project.1.a_ref.after_hbm), channel_id=1, source_target_pairs={{0,3},{1,2},{2,1},{3,0},{4,7},{5,6},{6,5},{7,4},{8,11},{9,10},{10,... | collective-permute-start | bytes 49160 | tf_op jit(solution)/shard_map/ppermute | solution.py:281
  31.9 4.8 %collective-permute-start = (f32[2,2048]{1,0:T(2,128)S(1)}, f32[2,2048]{1,0:T(2,128)S(1)}, u32[]{:S(2)}, u32[]{:S(2)}) collective-permute-start(f32[2,2048]{1,0:T(2,128)S(1)} %merge_project.1.a_ref.after_hbm), channel_id=1, source_target_pairs={{0,1},{1,0},{2,3},{3,2},{4,5},{5,4},{6,7},{7,6},{8,9},{9,8},{10,11... | collective-permute-start | bytes 49160 | tf_op jit(solution)/shard_map/ppermute | solution.py:281
  38.6 5.3 %collective-permute-start.5 = (f32[2,2048]{1,0:T(2,128)S(1)}, f32[2,2048]{1,0:T(2,128)S(1)}, u32[]{:S(2)}, u32[]{:S(2)}) collective-permute-start(f32[2,2048]{1,0:T(2,128)S(1)} %get-tuple-element.25.a_ref), channel_id=1, source_target_pairs={{0,2},{1,3},{2,0},{3,1},{4,6},{5,7},{6,4},{7,5},{8,10},{9,11},{10,... | collective-permute-start | bytes 49160 | tf_op jit(solution)/shard_map/ppermute | solution.py:281
  41.3 4.7 %collective-permute-start.4 = (f32[2,2048]{1,0:T(2,128)S(1)}, f32[2,2048]{1,0:T(2,128)S(1)}, u32[]{:S(2)}, u32[]{:S(2)}) collective-permute-start(f32[2,2048]{1,0:T(2,128)S(1)} %get-tuple-element.25.a_ref), channel_id=1, source_target_pairs={{0,3},{1,2},{2,1},{3,0},{4,7},{5,6},{6,5},{7,4},{8,11},{9,10},{10,... | collective-permute-start | bytes 49160 | tf_op jit(solution)/shard_map/ppermute | solution.py:281
  41.6 4.4 %collective-permute-start.3 = (f32[2,2048]{1,0:T(2,128)S(1)}, f32[2,2048]{1,0:T(2,128)S(1)}, u32[]{:S(2)}, u32[]{:S(2)}) collective-permute-start(f32[2,2048]{1,0:T(2,128)S(1)} %get-tuple-element.25.a_ref), channel_id=1, source_target_pairs={{0,1},{1,0},{2,3},{3,2},{4,5},{5,4},{6,7},{7,6},{8,9},{9,8},{10,11... | collective-permute-start | bytes 49160 | tf_op jit(solution)/shard_map/ppermute | solution.py:281
  46.6 15.7 %all-to-all-start.1 = ((bf16[64,2,512]{2,1,0:T(2,128)(2,1)}), bf16[64,2,512]{2,1,0:T(2,128)(2,1)S(1)}, u32[]{:S(2)}, u32[]{:S(2)}) async-start(bf16[64,2,512]{2,1,0:T(2,128)(2,1)} %last_sum.1), calls=%async_computation.1 | async-start | bytes 262144 | tf_op jit(solution)/shard_map/all_to_all | solution.py:389

commit v9 on v7

--- a/solution.py
+++ b/solution.py
@@ -166,11 +166,11 @@
 
 
 def fresh_kernel(
-    steps,
-    w_hbm, proj_hbm, q_own, normed, cosine, sine,
-    fresh_out, proj_out,
-    w_v, k16, v16, sem_w, sem_p,
+    w_hbm, proj_hbm, q_rows, q_own, normed, cosine, sine,
+    q_out, k_out, v_out, fresh_out, proj_out,
+    w_v, k_s, v_s, k16, v16, sem_w, sem_p,
 ):
+    reqs, steps, width = q_out.shape
     half = q_own.shape[0]
     heads = half // 2
     tall = 2 * half
@@ -180,15 +180,19 @@
         c.start()
     copy_p = pltpu.make_async_copy(proj_hbm, proj_out, sem_p)
     copy_p.start()
+    q_out[...] = q_rows[...].reshape(q_out.shape)
     block = pl.multiple_of((seq // 4) * 8, 8)
-    rows = normed[pl.ds(block, 8), :]
-    turns = (cosine[pl.ds(block, 8), :], sine[pl.ds(block, 8), :])
-    for j, store in enumerate((k16, v16)):
+    for j, (out, whole, store) in enumerate(((k_out, k_s, k16), (v_out, v_s, v16))):
         copies[j].wait()
-        part = jnp.dot(rows, w_v[j], preferred_element_type=F32)
+        part = jnp.dot(normed[...], w_v[j], preferred_element_type=F32)
         for h in range(heads):
-            v = part[:, h * DH : (h + 1) * DH]
-            store[pl.ds(h, 8, stride=heads), :] = rounded(turn(v, *turns) if j == 0 else v)
+            span = slice(h * DH, (h + 1) * DH)
+            v = part[:, span]
+            v = (turn(v, cosine[...], sine[...]) if j == 0 else v).astype(BF16)
+            out[:, :, span] = v.reshape(reqs, steps, DH)
+            whole[:, span] = v.astype(F32)
+        for h in range(heads):
+            store[pl.ds(h, 8, stride=heads), :] = whole[pl.ds(block, 8), h * DH : (h + 1) * DH]
     q = q_own[...]
     step = (seq % 2) * 2 + lax.broadcasted_iota(jnp.int32, (half, 1), 0) // heads
     base = pl.multiple_of(((seq // 2) % 2) * tall, tall)
@@ -232,25 +236,6 @@
         ctx_s[span, :] = o / whole
     ctx = jnp.concatenate([ctx_s[pl.ds(h, 2, stride=heads), :] for h in range(heads)], axis=1)
     out_ref[...] = jnp.dot(ctx.astype(BF16), w_ref[...], preferred_element_type=F32)
-
-
-def outputs_kernel(
-    after_hbm, w_hbm, q_rows, normed, cosine, sine,
-    q_out, k_out, v_out,
-    w_v, sem_w,
-):
-    reqs, steps, width = q_out.shape
-    copies = [pltpu.make_async_copy(w_hbm.at[1 + j], w_v.at[j], sem_w.at[j]) for j in range(2)]
-    for c in copies:
-        c.start()
-    q_out[...] = q_rows[...].reshape(q_out.shape)
-    for j, out in enumerate((k_out, v_out)):
-        copies[j].wait()
-        part = jnp.dot(normed[...], w_v[j], preferred_element_type=F32)
-        for h in range(width // DH):
-            v = part[:, h * DH : (h + 1) * DH]
-            v = turn(v, cosine[...], sine[...]) if j == 0 else v
-            out[:, :, h * DH : (h + 1) * DH] = v.reshape(reqs, steps, DH).astype(BF16)
 
 
 def mlp_kernel(x_ref, gu_ref, wd_ref, a_ref, b_ref, c_ref, d_ref, middle_out, down_out):
@@ -329,21 +314,28 @@
 
     got = lax.all_to_all(part, "seq", 0, 0)
 
-    fresh, w_proj = pl.pallas_call(
-        functools.partial(fresh_kernel, steps),
-        out_shape=(jax.ShapeDtypeStruct((3, tall // 2, DH), F32), jax.ShapeDtypeStruct(w_out.shape, BF16)),
-        in_specs=[any_space] * 2 + [vmem] * 4,
-        out_specs=(vmem,) * 2,
+    piece = jax.ShapeDtypeStruct((reqs, steps, width), BF16)
+    queries, new_keys, new_values, fresh, w_proj = pl.pallas_call(
+        fresh_kernel,
+        out_shape=(
+            piece, piece, piece,
+            jax.ShapeDtypeStruct((3, tall // 2, DH), F32),
+            jax.ShapeDtypeStruct(w_out.shape, BF16),
+        ),
+        in_specs=[any_space] * 2 + [vmem] * 5,
+        out_specs=(vmem,) * 5,
         scratch_shapes=[
             pltpu.VMEM((2, model, width), BF16),
+            pltpu.VMEM((rows, width), F32),
+            pltpu.VMEM((rows, width), F32),
             pltpu.VMEM((8 * heads, DH), F32),
             pltpu.VMEM((8 * heads, DH), F32),
             pltpu.SemaphoreType.DMA((2,)),
             pltpu.SemaphoreType.DMA,
         ],
-        compiler_params=pltpu.CompilerParams(vmem_limit_bytes=12 << 20),
+        compiler_params=pltpu.CompilerParams(vmem_limit_bytes=14 << 20),
         name="new_tokens",
-    )(in_hbm(w_qkv), in_hbm(w_out), q_own, normed, cosine, sine)
+    )(in_hbm(w_qkv), in_hbm(w_out), q_rows, q_own, normed, cosine, sine)
     mine = pl.pallas_call(
         merge_kernel,
         out_shape=jax.ShapeDtypeStruct((2, model), F32),
@@ -355,17 +347,6 @@
         name="merge_project",
     )(got, fresh, w_proj)
     others = to_others([mine] * 3, "mp")
-
-    piece = jax.ShapeDtypeStruct((reqs, steps, width), BF16)
-    queries, new_keys, new_values = pl.pallas_call(
-        outputs_kernel,
-        out_shape=(piece,) * 3,
-        in_specs=[any_space] * 2 + [vmem] * 4,
-        out_specs=(vmem,) * 3,
-        scratch_shapes=[pltpu.VMEM((2, model, width), BF16), pltpu.SemaphoreType.DMA((2,))],
-        compiler_params=pltpu.CompilerParams(vmem_limit_bytes=12 << 20),
-        name="projections",
-    )(mine, in_hbm(w_qkv), q_rows, normed, cosine, sine)
 
     cols = model // n_mp
     rows2 = jax.ShapeDtypeStruct((2, model), F32)

time: 63 us -> 62.1 us (0.986)
  blocking collectives: 0 us -> 15.5 us
  waiting for transfers between devices: 22.5 us -> 14.1 us
  starting transfers between devices: 20.7 us -> 16.1 us
  Pallas kernels: 18.1 us -> 14.8 us
    all_to_all x0 -> x1, blocking collectives: none -> 15.5 us  [per_device(): hidden = lax.all_to_all(hidden, 'seq', 0, 0)]
    all_to_all x1 -> x0, waiting for transfers between devices: 7.67 us -> none  [per_device(): hidden = lax.all_to_all(hidden, 'seq', 0, 0)]
    all_to_all x1 -> x0, starting transfers between devices: 4.65 us -> none  [per_device(): hidden = lax.all_to_all(hidden, 'seq', 0, 0)]
    pallas_call x2 -> x1, Pallas kernels: 6.24 us -> 3.63 us  [per_device(): pl.pallas_call(fresh_kernel, out_shape=(piece, piece, piece, jax.ShapeDty...]
    all_to_all x1, waiting for transfers between devices: 8.99 us -> 8.25 us  [per_device(): got = lax.all_to_all(part, 'seq', 0, 0)]
    pallas_call x1, Pallas kernels: 0.7 us -> 0.05 us  [per_device(): pl.pallas_call(last_kernel, out_shape=jax.ShapeDtypeStruct((n_seq, 2, col...]
  transfers between devices with their start and end apart: 8 -> 7, of which waited for: 6 -> 5; matrix products, arithmetic and copies ran while one was open for 0% -> 0% of each run, Pallas kernels for 10% -> 6%
where the time goes in v9:
time: 62.1 us; the launch traced here: 61.9 us
  starting transfers between devices  16.1 us (26%)
  blocking collectives  15.5 us (25%)
  Pallas kernels  14.8 us (24%)
  waiting for transfers between devices  14.1 us (23%)
  local copies, waits for them, and re-layouts  0.73 us (1%)
  between operations  0.71 us (1%)
    all_to_all x1, blocking collectives, per_device(): hidden = lax.all_to_all(hidden, 'seq', 0, 0)  15.5 us
    all_to_all x1, starting transfers between devices, per_device(): got = lax.all_to_all(part, 'seq', 0, 0)  9.32 us
    pallas_call x1, Pallas kernels, per_device(): pl.pallas_call(functools.partial(cached_kernel, group, reqs, steps, block...  8.4 us
    all_to_all x1, waiting for transfers between devices, per_device(): got = lax.all_to_all(part, 'seq', 0, 0)  8.25 us
    ppermute x6, starting transfers between devices, to_others(): lax.ppermute(values[k - 1], axis, [(i, i ^ k) for i in range(size)])  6.74 us
    ppermute x6, waiting for transfers between devices, to_others(): lax.ppermute(values[k - 1], axis, [(i, i ^ k) for i in range(size)])  5.86 us
    pallas_call x1, Pallas kernels, per_device(): pl.pallas_call(fresh_kernel, out_shape=(piece, piece, piece, jax.ShapeDty...  3.63 us
    pallas_call x1, Pallas kernels, per_device(): pl.pallas_call(mlp_kernel, out_shape=(rows2,) * 2, in_specs=[vmem] * 7, o...  1.94 us
  transfers between devices with their start and end apart: 7, of which 5 were waited for; matrix products, arithmetic and copies ran while one was open for 0% of the time, Pallas kernels for 6%

profile of v9, /device:TPU:4, one launch (start us, length us, event | category | flops | bytes accessed | tf_op | source)
XLA Modules:
  0.0 61.9 jit_solution(12548564060399919834)
XLA Ops:
  0.6 8.4 %cached_attention.1 = (bf16[64,3,4,128]{3,2,1,0:T(4,128)(2,1)}, bf16[128,512]{1,0:T(8,128)(2,1)S(1)}, f32[8,128]{1,0:T(8,128)S(1)}, bf16[128,2048]{1,0:T(8,128)(...) custom-call(s32[32]{0:T(128)} %len_hbm.1, bf16[32,4,2048]{2,1,0:T(4,128)(2,1)} %x_ref.1, ...), custom_call_target="tpu_custom_call" | custom-call | tf_op jit(solution)/shard_map/cached_attention/pallas_call | solution.py:284
  9.0 9.3 %all-to-all-start = ((bf16[64,3,4,128]{3,2,1,0:T(4,128)(2,1)}), bf16[64,3,4,128]{3,2,1,0:T(4,128)(2,1)S(1)}, u32[]{:S(2)}, u32[]{:S(2)}) async-start(bf16[64,3,4,128]{3,2,1,0:T(4,128)(2,1)} %get-tuple-element.17), calls=%async_computation | async-start | bytes 393216 | tf_op jit(solution)/shard_map/all_to_all | solution.py:315
  18.4 3.6 %new_tokens.1 = (bf16[32,4,512]{2,1,0:T(4,128)(2,1)}, bf16[32,4,512]{2,1,0:T(4,128)(2,1)}, bf16[32,4,512]{2,1,0:T(4,128)(2,1)}, f32[3,8,128]{2,1,0:T(8,128)S(1)}, bf16[512,2048]{1,0:T(8,128)(2,1)S(1)}) custom-call(bf16[3,2048,512]{2,1,0:T(8,128)(2,1)} %w_hbm.3, bf16[512,2048]{1,0:T(8,128)(2,1)} %proj_hbm.1, bf16[128,512]{1,0:T(8,128)(2,1)S(1)} %get-tuple-element.18.q_rows, ...), custom_call_target="tpu_custom_call" | custom-call | tf_op jit(solution)/shard_map/new_tokens/pallas_call | solution.py:318
  22.0 8.3 %all-to-all-done.got_ref = bf16[64,3,4,128]{3,2,1,0:T(4,128)(2,1)S(1)} async-done(((bf16[64,3,4,128]{3,2,1,0:T(4,128)(2,1)}), bf16[64,3,4,128]{3,2,1,0:T(4,128)(2,1)S(1)}, u32[]{:S(2)}, u32[]{:S(2)}) %all-to-all-start) | async-done | bytes 196640 | tf_op jit(solution)/shard_map/all_to_all | solution.py:315
  30.3 0.0 slice-start
  30.3 0.0 slice-start.1
  30.3 0.0 copy-start
  30.3 0.0 copy-start.1
  30.3 0.8 %merge_project.1.a_ref = f32[2,2048]{1,0:T(2,128)S(1)} custom-call(bf16[64,3,4,128]{3,2,1,0:T(4,128)(2,1)S(1)} %all-to-all-done.got_ref, f32[3,8,128]{2,1,0:T(8,128)S(1)} %get-tuple-element.23.fresh_ref, bf16[512,2048]{1,0:T(8,128)(2,1)S(1)} %get-tuple-element.24.w_ref), custom_call_target="tpu_custom_call" | custom-call | flops 10000000000 | bytes 62914560 | tf_op jit(solution)/shard_map/merge_project/pallas_call | solution.py:339
  31.1 0.0 collective-permute-start.2
  31.1 0.9 %collective-permute-start.1 = (f32[2,2048]{1,0:T(2,128)S(1)}, f32[2,2048]{1,0:T(2,128)S(1)}, u32[]{:S(2)}, u32[]{:S(2)}) collective-permute-start(f32[2,2048]{1,0:T(2,128)S(1)} %merge_project.1.a_ref), channel_id=1, source_target_pairs={{0,2},{1,3},{2,0},{3,1},{4,6},{5,7},{6,4},{7,5},{8,10},{9,11},{10,... | collective-permute-start | bytes 49160 | tf_op jit(solution)/shard_map/ppermute | solution.py:266
  32.0 2.4 %collective-permute-start = (f32[2,2048]{1,0:T(2,128)S(1)}, f32[2,2048]{1,0:T(2,128)S(1)}, u32[]{:S(2)}, u32[]{:S(2)}) collective-permute-start(f32[2,2048]{1,0:T(2,128)S(1)} %merge_project.1.a_ref), channel_id=1, source_target_pairs={{0,1},{1,0},{2,3},{3,2},{4,5},{5,4},{6,7},{7,6},{8,9},{9,8},{10,11... | collective-permute-start | bytes 49160 | tf_op jit(solution)/shard_map/ppermute | solution.py:266
  34.4 1.3 %collective-permute-done.2.d_ref = f32[2,2048]{1,0:T(2,128)S(1)} collective-permute-done((f32[2,2048]{1,0:T(2,128)S(1)}, f32[2,2048]{1,0:T(2,128)S(1)}, u32[]{:S(2)}, u32[]{:S(2)}) %collective-permute-start.2) | collective-permute-done | bytes 16416 | tf_op jit(solution)/shard_map/ppermute | solution.py:266
  35.7 0.7 %collective-permute-done.1.c_ref = f32[2,2048]{1,0:T(2,128)S(1)} collective-permute-done((f32[2,2048]{1,0:T(2,128)S(1)}, f32[2,2048]{1,0:T(2,128)S(1)}, u32[]{:S(2)}, u32[]{:S(2)}) %collective-permute-start.1) | collective-permute-done | bytes 16416 | tf_op jit(solution)/shard_map/ppermute | solution.py:266
  36.4 0.0 collective-permute-done.b_ref
  36.4 0.0 slice-done
  36.4 0.0 slice-done.1
  36.4 0.0 copy-done
  36.5 0.0 copy-done.1
  36.5 1.9 %mlp.1 = (f32[2,2048]{1,0:T(2,128)S(1)}, f32[2,2048]{1,0:T(2,128)S(1)}) custom-call(bf16[32,4,2048]{2,1,0:T(4,128)(2,1)S(1)} %copy-done.1, bf16[2,2048,1024]{2,1,0:T(8,128)(2,1)S(1)} %bitcast.1, bf16[1024,2048]{1,0:T(8,128)(2,1)S(1)} %copy-done, f32[2,2048]{1,0:T(2,128)S(1)} %merge_project.1.a_ref, f32[2,2048]{1,0:T(2,128)S(1)} %collective-permute-done.b_ref, ...), custom_call_target="tpu_custom_call" | custom-call | tf_op jit(solution)/shard_map/mlp/pallas_call | solution.py:353
  38.4 2.0 %collective-permute-start.5 = (f32[2,2048]{1,0:T(2,128)S(1)}, f32[2,2048]{1,0:T(2,128)S(1)}, u32[]{:S(2)}, u32[]{:S(2)}) collective-permute-start(f32[2,2048]{1,0:T(2,128)S(1)} %get-tuple-element.26.a_ref), channel_id=1, source_target_pairs={{0,3},{1,2},{2,1},{3,0},{4,7},{5,6},{6,5},{7,4},{8,11},{9,10},{10,... | collective-permute-start | bytes 49160 | tf_op jit(solution)/shard_map/ppermute | solution.py:266
  40.4 1.1 %collective-permute-start.4 = (f32[2,2048]{1,0:T(2,128)S(1)}, f32[2,2048]{1,0:T(2,128)S(1)}, u32[]{:S(2)}, u32[]{:S(2)}) collective-permute-start(f32[2,2048]{1,0:T(2,128)S(1)} %get-tuple-element.26.a_ref), channel_id=1, source_target_pairs={{0,2},{1,3},{2,0},{3,1},{4,6},{5,7},{6,4},{7,5},{8,10},{9,11},{10,... | collective-permute-start | bytes 49160 | tf_op jit(solution)/shard_map/ppermute | solution.py:266
  41.5 0.3 collective-permute-start.3
  41.8 1.3 %collective-permute-done.5.d_ref = f32[2,2048]{1,0:T(2,128)S(1)} collective-permute-done((f32[2,2048]{1,0:T(2,128)S(1)}, f32[2,2048]{1,0:T(2,128)S(1)}, u32[]{:S(2)}, u32[]{:S(2)}) %collective-permute-start.5) | collective-permute-done | bytes 16416 | tf_op jit(solution)/shard_map/ppermute | solution.py:266
  43.1 2.5 %collective-permute-done.4.c_ref = f32[2,2048]{1,0:T(2,128)S(1)} collective-permute-done((f32[2,2048]{1,0:T(2,128)S(1)}, f32[2,2048]{1,0:T(2,128)S(1)}, u32[]{:S(2)}, u32[]{:S(2)}) %collective-permute-start.4) | collective-permute-done | bytes 16416 | tf_op jit(solution)/shard_map/ppermute | solution.py:266
  45.6 0.0 collective-permute-done.3.b_ref
  45.7 15.5 %all_to_all.10 = bf16[64,2,512]{2,1,0:T(2,128)(2,1)S(1)} all-to-all(bf16[64,2,512]{2,1,0:T(2,128)(2,1)S(1)} %last_sum.1), channel_id=1, replica_groups=mesh['seq'=64,'mp'=4] {'seq'}, dimensions={0} | all-to-all | bytes 262144 | tf_op jit(solution)/shard_map/all_to_all | solution.py:369
  61.2 0.7 %reshape.11 = bf16[32,4,512]{2,1,0:T(4,128)(2,1)} reshape(bf16[64,2,512]{2,1,0:T(2,128)(2,1)S(1)} %all_to_all.10) | data formatting | bytes 262144 | tf_op jit(solution)/shard_map/reshape | solution.py:370
  (2 shorter events, 0.0 us)
Async XLA Ops:
  9.0 21.2 %all-to-all-start = ((bf16[64,3,4,128]{3,2,1,0:T(4,128)(2,1)}), bf16[64,3,4,128]{3,2,1,0:T(4,128)(2,1)S(1)}, u32[]{:S(2)}, u32[]{:S(2)}) async-start(bf16[64,3,4,128]{3,2,1,0:T(4,128)(2,1)} %get-tuple-element.17), calls=%async_computation | async-start | bytes 393216 | tf_op jit(solution)/shard_map/all_to_all | solution.py:315
  30.3 6.2 %slice-start = ((s8[8388608]{0:T(1024)(128)(4,1)}), s8[4194304]{0:T(1024)(128)(4,1)S(1)}, s32[]{:S(2)}) async-start(s8[8388608]{0:T(1024)(128)(4,1)} %bitcast), calls=%async_computation.2 | async-start | bytes 8388608
  30.3 6.2 %slice-start.1 = ((s8[8388608]{0:T(1024)(128)(4,1)}), s8[4194304]{0:T(1024)(128)(4,1)S(1)}, s32[]{:S(2)}) async-start(s8[8388608]{0:T(1024)(128)(4,1)} %bitcast), calls=%async_computation.3 | async-start | bytes 8388608
  30.3 6.2 %copy-start = (bf16[1024,2048]{1,0:T(8,128)(2,1)S(1)}, bf16[1024,2048]{1,0:T(8,128)(2,1)}, u32[]{:S(2)}) copy-start(bf16[1024,2048]{1,0:T(8,128)(2,1)} %wd_ref.1) | copy-start | bytes 12582916
  30.3 6.2 %copy-start.1 = (bf16[32,4,2048]{2,1,0:T(4,128)(2,1)S(1)}, bf16[32,4,2048]{2,1,0:T(4,128)(2,1)}, u32[]{:S(2)}) copy-start(bf16[32,4,2048]{2,1,0:T(4,128)(2,1)} %x_ref.1) | copy-start | bytes 1572868
  31.1 4.7 %collective-permute-start.2 = (f32[2,2048]{1,0:T(2,128)S(1)}, f32[2,2048]{1,0:T(2,128)S(1)}, u32[]{:S(2)}, u32[]{:S(2)}) collective-permute-start(f32[2,2048]{1,0:T(2,128)S(1)} %merge_project.1.a_ref), channel_id=1, source_target_pairs={{0,3},{1,2},{2,1},{3,0},{4,7},{5,6},{6,5},{7,4},{8,11},{9,10},{10,... | collective-permute-start | bytes 49160 | tf_op jit(solution)/shard_map/ppermute | solution.py:266
  31.1 5.4 %collective-permute-start.1 = (f32[2,2048]{1,0:T(2,128)S(1)}, f32[2,2048]{1,0:T(2,128)S(1)}, u32[]{:S(2)}, u32[]{:S(2)}) collective-permute-start(f32[2,2048]{1,0:T(2,128)S(1)} %merge_project.1.a_ref), channel_id=1, source_target_pairs={{0,2},{1,3},{2,0},{3,1},{4,6},{5,7},{6,4},{7,5},{8,10},{9,11},{10,... | collective-permute-start | bytes 49160 | tf_op jit(solution)/shard_map/ppermute | solution.py:266
  32.0 4.4 %collective-permute-start = (f32[2,2048]{1,0:T(2,128)S(1)}, f32[2,2048]{1,0:T(2,128)S(1)}, u32[]{:S(2)}, u32[]{:S(2)}) collective-permute-start(f32[2,2048]{1,0:T(2,128)S(1)} %merge_project.1.a_ref), channel_id=1, source_target_pairs={{0,1},{1,0},{2,3},{3,2},{4,5},{5,4},{6,7},{7,6},{8,9},{9,8},{10,11... | collective-permute-start | bytes 49160 | tf_op jit(solution)/shard_map/ppermute | solution.py:266
  38.4 4.7 %collective-permute-start.5 = (f32[2,2048]{1,0:T(2,128)S(1)}, f32[2,2048]{1,0:T(2,128)S(1)}, u32[]{:S(2)}, u32[]{:S(2)}) collective-permute-start(f32[2,2048]{1,0:T(2,128)S(1)} %get-tuple-element.26.a_ref), channel_id=1, source_target_pairs={{0,3},{1,2},{2,1},{3,0},{4,7},{5,6},{6,5},{7,4},{8,11},{9,10},{10,... | collective-permute-start | bytes 49160 | tf_op jit(solution)/shard_map/ppermute | solution.py:266
  40.4 5.2 %collective-permute-start.4 = (f32[2,2048]{1,0:T(2,128)S(1)}, f32[2,2048]{1,0:T(2,128)S(1)}, u32[]{:S(2)}, u32[]{:S(2)}) collective-permute-start(f32[2,2048]{1,0:T(2,128)S(1)} %get-tuple-element.26.a_ref), channel_id=1, source_target_pairs={{0,2},{1,3},{2,0},{3,1},{4,6},{5,7},{6,4},{7,5},{8,10},{9,11},{10,... | collective-permute-start | bytes 49160 | tf_op jit(solution)/shard_map/ppermute | solution.py:266
  41.5 4.1 %collective-permute-start.3 = (f32[2,2048]{1,0:T(2,128)S(1)}, f32[2,2048]{1,0:T(2,128)S(1)}, u32[]{:S(2)}, u32[]{:S(2)}) collective-permute-start(f32[2,2048]{1,0:T(2,128)S(1)} %get-tuple-element.26.a_ref), channel_id=1, source_target_pairs={{0,1},{1,0},{2,3},{3,2},{4,5},{5,4},{6,7},{7,6},{8,9},{9,8},{10,11... | collective-permute-start | bytes 49160 | tf_op jit(solution)/shard_map/ppermute | solution.py:266

commit v10 on v9

--- a/solution.py
+++ b/solution.py
@@ -357,7 +357,7 @@
         out_specs=(vmem,) * 2,
         compiler_params=pltpu.CompilerParams(vmem_limit_bytes=8 << 20),
         name="mlp",
-    )(inputs, w_gate_up, w_down, mine, *others)
+    )(inputs, w_gate_up, w_down, mine, *others[::-1])
     hidden = pl.pallas_call(
         last_kernel,
         out_shape=jax.ShapeDtypeStruct((n_seq, 2, cols), BF16),
@@ -365,7 +365,7 @@
         out_specs=vmem,
         compiler_params=pltpu.CompilerParams(vmem_limit_bytes=4 << 20),
         name="last_sum",
-    )(middle, down, *to_others([down] * 3, "mp"))
+    )(middle, down, *to_others([down] * 3, "mp")[::-1])
     hidden = lax.all_to_all(hidden, "seq", 0, 0)
     return (hidden.reshape(reqs, steps, cols), queries, new_keys, new_values)
 

time: 62.1 us -> 62.8 us (1.011)
  no operation moved by 1% of the time
where the time goes in v10:
time: 62.8 us; the launch traced here: 62.6 us
  starting transfers between devices  16.1 us (26%)
  blocking collectives  15.6 us (25%)
  Pallas kernels  14.8 us (24%)
  waiting for transfers between devices  14.6 us (23%)
  local copies, waits for them, and re-layouts  0.73 us (1%)
  between operations  0.7 us (1%)
    all_to_all x1, blocking collectives, per_device(): hidden = lax.all_to_all(hidden, 'seq', 0, 0)  15.6 us
    all_to_all x1, starting transfers between devices, per_device(): got = lax.all_to_all(part, 'seq', 0, 0)  9.32 us
    pallas_call x1, Pallas kernels, per_device(): pl.pallas_call(functools.partial(cached_kernel, group, reqs, steps, block...  8.4 us
    all_to_all x1, waiting for transfers between devices, per_device(): got = lax.all_to_all(part, 'seq', 0, 0)  8.25 us
    ppermute x6, starting transfers between devices, to_others(): lax.ppermute(values[k - 1], axis, [(i, i ^ k) for i in range(size)])  6.76 us
    ppermute x6, waiting for transfers between devices, to_others(): lax.ppermute(values[k - 1], axis, [(i, i ^ k) for i in range(size)])  6.38 us
    pallas_call x1, Pallas kernels, per_device(): pl.pallas_call(fresh_kernel, out_shape=(piece, piece, piece, jax.ShapeDty...  3.63 us
    pallas_call x1, Pallas kernels, per_device(): pl.pallas_call(mlp_kernel, out_shape=(rows2,) * 2, in_specs=[vmem] * 7, o...  1.94 us
  transfers between devices with their start and end apart: 7, of which 5 were waited for; matrix products, arithmetic and copies ran while one was open for 0% of the time, Pallas kernels for 6%

profile of v10, /device:TPU:4, one launch (start us, length us, event | category | flops | bytes accessed | tf_op | source)
XLA Modules:
  0.0 62.6 jit_solution(9136817043272452727)
XLA Ops:
  0.6 8.4 %cached_attention.1 = (bf16[64,3,4,128]{3,2,1,0:T(4,128)(2,1)}, bf16[128,512]{1,0:T(8,128)(2,1)S(1)}, f32[8,128]{1,0:T(8,128)S(1)}, bf16[128,2048]{1,0:T(8,128)(...) custom-call(s32[32]{0:T(128)} %len_hbm.1, bf16[32,4,2048]{2,1,0:T(4,128)(2,1)} %x_ref.1, ...), custom_call_target="tpu_custom_call" | custom-call | tf_op jit(solution)/shard_map/cached_attention/pallas_call | solution.py:284
  9.0 9.3 %all-to-all-start = ((bf16[64,3,4,128]{3,2,1,0:T(4,128)(2,1)}), bf16[64,3,4,128]{3,2,1,0:T(4,128)(2,1)S(1)}, u32[]{:S(2)}, u32[]{:S(2)}) async-start(bf16[64,3,4,128]{3,2,1,0:T(4,128)(2,1)} %get-tuple-element.17), calls=%async_computation | async-start | bytes 393216 | tf_op jit(solution)/shard_map/all_to_all | solution.py:315
  18.4 3.6 %new_tokens.1 = (bf16[32,4,512]{2,1,0:T(4,128)(2,1)}, bf16[32,4,512]{2,1,0:T(4,128)(2,1)}, bf16[32,4,512]{2,1,0:T(4,128)(2,1)}, f32[3,8,128]{2,1,0:T(8,128)S(1)}, bf16[512,2048]{1,0:T(8,128)(2,1)S(1)}) custom-call(bf16[3,2048,512]{2,1,0:T(8,128)(2,1)} %w_hbm.3, bf16[512,2048]{1,0:T(8,128)(2,1)} %proj_hbm.1, bf16[128,512]{1,0:T(8,128)(2,1)S(1)} %get-tuple-element.18.q_rows, ...), custom_call_target="tpu_custom_call" | custom-call | tf_op jit(solution)/shard_map/new_tokens/pallas_call | solution.py:318
  22.0 8.3 %all-to-all-done.got_ref = bf16[64,3,4,128]{3,2,1,0:T(4,128)(2,1)S(1)} async-done(((bf16[64,3,4,128]{3,2,1,0:T(4,128)(2,1)}), bf16[64,3,4,128]{3,2,1,0:T(4,128)(2,1)S(1)}, u32[]{:S(2)}, u32[]{:S(2)}) %all-to-all-start) | async-done | bytes 196640 | tf_op jit(solution)/shard_map/all_to_all | solution.py:315
  30.3 0.0 slice-start
  30.3 0.0 slice-start.1
  30.3 0.0 copy-start
  30.3 0.0 copy-start.1
  30.3 0.8 %merge_project.1.a_ref = f32[2,2048]{1,0:T(2,128)S(1)} custom-call(bf16[64,3,4,128]{3,2,1,0:T(4,128)(2,1)S(1)} %all-to-all-done.got_ref, f32[3,8,128]{2,1,0:T(8,128)S(1)} %get-tuple-element.23.fresh_ref, bf16[512,2048]{1,0:T(8,128)(2,1)S(1)} %get-tuple-element.24.w_ref), custom_call_target="tpu_custom_call" | custom-call | flops 10000000000 | bytes 62914560 | tf_op jit(solution)/shard_map/merge_project/pallas_call | solution.py:339
  31.1 0.0 collective-permute-start.2
  31.1 0.9 %collective-permute-start.1 = (f32[2,2048]{1,0:T(2,128)S(1)}, f32[2,2048]{1,0:T(2,128)S(1)}, u32[]{:S(2)}, u32[]{:S(2)}) collective-permute-start(f32[2,2048]{1,0:T(2,128)S(1)} %merge_project.1.a_ref), channel_id=1, source_target_pairs={{0,2},{1,3},{2,0},{3,1},{4,6},{5,7},{6,4},{7,5},{8,10},{9,11},{10,... | collective-permute-start | bytes 49160 | tf_op jit(solution)/shard_map/ppermute | solution.py:266
  32.0 2.5 %collective-permute-start = (f32[2,2048]{1,0:T(2,128)S(1)}, f32[2,2048]{1,0:T(2,128)S(1)}, u32[]{:S(2)}, u32[]{:S(2)}) collective-permute-start(f32[2,2048]{1,0:T(2,128)S(1)} %merge_project.1.a_ref), channel_id=1, source_target_pairs={{0,3},{1,2},{2,1},{3,0},{4,7},{5,6},{6,5},{7,4},{8,11},{9,10},{10,... | collective-permute-start | bytes 49160 | tf_op jit(solution)/shard_map/ppermute | solution.py:266
  34.5 0.0 collective-permute-done.2.d_ref
  34.5 2.0 %collective-permute-done.1.c_ref = f32[2,2048]{1,0:T(2,128)S(1)} collective-permute-done((f32[2,2048]{1,0:T(2,128)S(1)}, f32[2,2048]{1,0:T(2,128)S(1)}, u32[]{:S(2)}, u32[]{:S(2)}) %collective-permute-start.1) | collective-permute-done | bytes 16416 | tf_op jit(solution)/shard_map/ppermute | solution.py:266
  36.4 0.2 collective-permute-done.b_ref
  36.6 0.0 slice-done
  36.6 0.0 slice-done.1
  36.6 0.0 copy-done
  36.6 0.0 copy-done.1
  36.7 1.9 %mlp.1 = (f32[2,2048]{1,0:T(2,128)S(1)}, f32[2,2048]{1,0:T(2,128)S(1)}) custom-call(bf16[32,4,2048]{2,1,0:T(4,128)(2,1)S(1)} %copy-done.1, bf16[2,2048,1024]{2,1,0:T(8,128)(2,1)S(1)} %bitcast.1, bf16[1024,2048]{1,0:T(8,128)(2,1)S(1)} %copy-done, f32[2,2048]{1,0:T(2,128)S(1)} %merge_project.1.a_ref, f32[2,2048]{1,0:T(2,128)S(1)} %collective-permute-done.b_ref, ...), custom_call_target="tpu_custom_call" | custom-call | tf_op jit(solution)/shard_map/mlp/pallas_call | solution.py:353
  38.6 0.2 collective-permute-start.5
  38.8 2.7 %collective-permute-start.4 = (f32[2,2048]{1,0:T(2,128)S(1)}, f32[2,2048]{1,0:T(2,128)S(1)}, u32[]{:S(2)}, u32[]{:S(2)}) collective-permute-start(f32[2,2048]{1,0:T(2,128)S(1)} %get-tuple-element.26.a_ref), channel_id=1, source_target_pairs={{0,2},{1,3},{2,0},{3,1},{4,6},{5,7},{6,4},{7,5},{8,10},{9,11},{10,... | collective-permute-start | bytes 49160 | tf_op jit(solution)/shard_map/ppermute | solution.py:266
  41.5 0.5 collective-permute-start.3
  42.0 0.0 collective-permute-done.5.d_ref
  42.0 2.0 %collective-permute-done.4.c_ref = f32[2,2048]{1,0:T(2,128)S(1)} collective-permute-done((f32[2,2048]{1,0:T(2,128)S(1)}, f32[2,2048]{1,0:T(2,128)S(1)}, u32[]{:S(2)}, u32[]{:S(2)}) %collective-permute-start.4) | collective-permute-done | bytes 16416 | tf_op jit(solution)/shard_map/ppermute | solution.py:266
  44.0 2.2 %collective-permute-done.3.b_ref = f32[2,2048]{1,0:T(2,128)S(1)} collective-permute-done((f32[2,2048]{1,0:T(2,128)S(1)}, f32[2,2048]{1,0:T(2,128)S(1)}, u32[]{:S(2)}, u32[]{:S(2)}) %collective-permute-start.3) | collective-permute-done | bytes 16416 | tf_op jit(solution)/shard_map/ppermute | solution.py:266
  46.2 15.6 %all_to_all.10 = bf16[64,2,512]{2,1,0:T(2,128)(2,1)S(1)} all-to-all(bf16[64,2,512]{2,1,0:T(2,128)(2,1)S(1)} %last_sum.1), channel_id=1, replica_groups=mesh['seq'=64,'mp'=4] {'seq'}, dimensions={0} | all-to-all | bytes 262144 | tf_op jit(solution)/shard_map/all_to_all | solution.py:369
  61.9 0.7 %reshape.11 = bf16[32,4,512]{2,1,0:T(4,128)(2,1)} reshape(bf16[64,2,512]{2,1,0:T(2,128)(2,1)S(1)} %all_to_all.10) | data formatting | bytes 262144 | tf_op jit(solution)/shard_map/reshape | solution.py:370
  (2 shorter events, 0.0 us)
Async XLA Ops:
  9.0 21.2 %all-to-all-start = ((bf16[64,3,4,128]{3,2,1,0:T(4,128)(2,1)}), bf16[64,3,4,128]{3,2,1,0:T(4,128)(2,1)S(1)}, u32[]{:S(2)}, u32[]{:S(2)}) async-start(bf16[64,3,4,128]{3,2,1,0:T(4,128)(2,1)} %get-tuple-element.17), calls=%async_computation | async-start | bytes 393216 | tf_op jit(solution)/shard_map/all_to_all | solution.py:315
  30.3 6.4 %slice-start = ((s8[8388608]{0:T(1024)(128)(4,1)}), s8[4194304]{0:T(1024)(128)(4,1)S(1)}, s32[]{:S(2)}) async-start(s8[8388608]{0:T(1024)(128)(4,1)} %bitcast), calls=%async_computation.2 | async-start | bytes 8388608
  30.3 6.4 %slice-start.1 = ((s8[8388608]{0:T(1024)(128)(4,1)}), s8[4194304]{0:T(1024)(128)(4,1)S(1)}, s32[]{:S(2)}) async-start(s8[8388608]{0:T(1024)(128)(4,1)} %bitcast), calls=%async_computation.3 | async-start | bytes 8388608
  30.3 6.4 %copy-start = (bf16[1024,2048]{1,0:T(8,128)(2,1)S(1)}, bf16[1024,2048]{1,0:T(8,128)(2,1)}, u32[]{:S(2)}) copy-start(bf16[1024,2048]{1,0:T(8,128)(2,1)} %wd_ref.1) | copy-start | bytes 12582916
  30.3 6.4 %copy-start.1 = (bf16[32,4,2048]{2,1,0:T(4,128)(2,1)S(1)}, bf16[32,4,2048]{2,1,0:T(4,128)(2,1)}, u32[]{:S(2)}) copy-start(bf16[32,4,2048]{2,1,0:T(4,128)(2,1)} %x_ref.1) | copy-start | bytes 1572868
  31.1 3.4 %collective-permute-start.2 = (f32[2,2048]{1,0:T(2,128)S(1)}, f32[2,2048]{1,0:T(2,128)S(1)}, u32[]{:S(2)}, u32[]{:S(2)}) collective-permute-start(f32[2,2048]{1,0:T(2,128)S(1)} %merge_project.1.a_ref), channel_id=1, source_target_pairs={{0,1},{1,0},{2,3},{3,2},{4,5},{5,4},{6,7},{7,6},{8,9},{9,8},{10,11... | collective-permute-start | bytes 49160 | tf_op jit(solution)/shard_map/ppermute | solution.py:266
  31.1 5.3 %collective-permute-start.1 = (f32[2,2048]{1,0:T(2,128)S(1)}, f32[2,2048]{1,0:T(2,128)S(1)}, u32[]{:S(2)}, u32[]{:S(2)}) collective-permute-start(f32[2,2048]{1,0:T(2,128)S(1)} %merge_project.1.a_ref), channel_id=1, source_target_pairs={{0,2},{1,3},{2,0},{3,1},{4,6},{5,7},{6,4},{7,5},{8,10},{9,11},{10,... | collective-permute-start | bytes 49160 | tf_op jit(solution)/shard_map/ppermute | solution.py:266
  32.0 4.7 %collective-permute-start = (f32[2,2048]{1,0:T(2,128)S(1)}, f32[2,2048]{1,0:T(2,128)S(1)}, u32[]{:S(2)}, u32[]{:S(2)}) collective-permute-start(f32[2,2048]{1,0:T(2,128)S(1)} %merge_project.1.a_ref), channel_id=1, source_target_pairs={{0,3},{1,2},{2,1},{3,0},{4,7},{5,6},{6,5},{7,4},{8,11},{9,10},{10,... | collective-permute-start | bytes 49160 | tf_op jit(solution)/shard_map/ppermute | solution.py:266
  38.6 3.4 %collective-permute-start.5 = (f32[2,2048]{1,0:T(2,128)S(1)}, f32[2,2048]{1,0:T(2,128)S(1)}, u32[]{:S(2)}, u32[]{:S(2)}) collective-permute-start(f32[2,2048]{1,0:T(2,128)S(1)} %get-tuple-element.26.a_ref), channel_id=1, source_target_pairs={{0,1},{1,0},{2,3},{3,2},{4,5},{5,4},{6,7},{7,6},{8,9},{9,8},{10,11... | collective-permute-start | bytes 49160 | tf_op jit(solution)/shard_map/ppermute | solution.py:266
  38.8 5.3 %collective-permute-start.4 = (f32[2,2048]{1,0:T(2,128)S(1)}, f32[2,2048]{1,0:T(2,128)S(1)}, u32[]{:S(2)}, u32[]{:S(2)}) collective-permute-start(f32[2,2048]{1,0:T(2,128)S(1)} %get-tuple-element.26.a_ref), channel_id=1, source_target_pairs={{0,2},{1,3},{2,0},{3,1},{4,6},{5,7},{6,4},{7,5},{8,10},{9,11},{10,... | collective-permute-start | bytes 49160 | tf_op jit(solution)/shard_map/ppermute | solution.py:266
  41.5 4.7 %collective-permute-start.3 = (f32[2,2048]{1,0:T(2,128)S(1)}, f32[2,2048]{1,0:T(2,128)S(1)}, u32[]{:S(2)}, u32[]{:S(2)}) collective-permute-start(f32[2,2048]{1,0:T(2,128)S(1)} %get-tuple-element.26.a_ref), channel_id=1, source_target_pairs={{0,3},{1,2},{2,1},{3,0},{4,7},{5,6},{6,5},{7,4},{8,11},{9,10},{10,... | collective-permute-start | bytes 49160 | tf_op jit(solution)/shard_map/ppermute | solution.py:266

commit v11 on v10

--- a/solution.py
+++ b/solution.py
@@ -238,11 +238,11 @@
     out_ref[...] = jnp.dot(ctx.astype(BF16), w_ref[...], preferred_element_type=F32)
 
 
-def mlp_kernel(x_ref, gu_ref, wd_ref, a_ref, b_ref, c_ref, d_ref, middle_out, down_out):
+def mlp_kernel(x_ref, gu_ref, wd_ref, near_ref, far_ref, middle_out, down_out):
     seq = lax.axis_index("seq")
     x = x_ref[seq // 2].astype(F32)
     x = jnp.where(seq % 2 == 0, x[0:2], x[2:4])
-    middle = x + ((a_ref[...] + b_ref[...]) + (c_ref[...] + d_ref[...]))
+    middle = x + (near_ref[...] + far_ref[...])
     middle_out[...] = middle
     normed = norm_rows(middle).astype(BF16)
     gate = jnp.dot(normed, gu_ref[0], preferred_element_type=F32)
@@ -251,20 +251,18 @@
     down_out[...] = jnp.dot(active, wd_ref[...], preferred_element_type=F32)
 
 
-def last_kernel(middle_ref, a_ref, b_ref, c_ref, d_ref, out_ref):
+def last_kernel(middle_ref, near_ref, far_ref, out_ref):
     cols = out_ref.shape[2]
     span = pl.ds(pl.multiple_of(lax.axis_index("mp") * cols, cols), cols)
-    down = (a_ref[:, span] + b_ref[:, span]) + (c_ref[:, span] + d_ref[:, span])
+    down = near_ref[:, span] + far_ref[:, span]
     hidden = (middle_ref[:, span] + down).astype(BF16)
     out_ref[...] = jnp.broadcast_to(hidden[None], out_ref.shape)
 
 
-def to_others(values, axis):
+def halves(v, axis):
     size = lax.axis_size(axis)
-    got = [None] * (size - 1)
-    for k in range(size - 1, 0, -1):
-        got[k - 1] = lax.ppermute(values[k - 1], axis, [(i, i ^ k) for i in range(size)])
-    return got
+    near = v + lax.ppermute(v, axis, [(i, i ^ 1) for i in range(size)])
+    return near, lax.ppermute(near, axis, [(i, i ^ 2) for i in range(size)])
 
 
 def per_device(inputs, w_qkv, w_out, w_gate_up, w_down, cache_keys, cache_values, lengths):
@@ -346,26 +344,25 @@
         cost_estimate=pl.CostEstimate(flops=10**10, transcendentals=0, bytes_accessed=60 << 20),
         name="merge_project",
     )(got, fresh, w_proj)
-    others = to_others([mine] * 3, "mp")
 
     cols = model // n_mp
     rows2 = jax.ShapeDtypeStruct((2, model), F32)
     middle, down = pl.pallas_call(
         mlp_kernel,
         out_shape=(rows2,) * 2,
-        in_specs=[vmem] * 7,
+        in_specs=[vmem] * 5,
         out_specs=(vmem,) * 2,
         compiler_params=pltpu.CompilerParams(vmem_limit_bytes=8 << 20),
         name="mlp",
-    )(inputs, w_gate_up, w_down, mine, *others[::-1])
+    )(inputs, w_gate_up, w_down, *halves(mine, "mp"))
     hidden = pl.pallas_call(
         last_kernel,
         out_shape=jax.ShapeDtypeStruct((n_seq, 2, cols), BF16),
-        in_specs=[vmem] * 5,
+        in_specs=[vmem] * 3,
         out_specs=vmem,
         compiler_params=pltpu.CompilerParams(vmem_limit_bytes=4 << 20),
         name="last_sum",
-    )(middle, down, *to_others([down] * 3, "mp")[::-1])
+    )(middle, *halves(down, "mp"))
     hidden = lax.all_to_all(hidden, "seq", 0, 0)
     return (hidden.reshape(reqs, steps, cols), queries, new_keys, new_values)
 

time: 62.8 us -> 62.6 us (level)
  starting transfers between devices: 16.1 us -> 11.1 us
  waiting for transfers between devices: 14.6 us -> 19.5 us
    ppermute x6 -> x4, starting transfers between devices: 6.76 us -> 1.79 us  [the longest x2 1.77 us: halves(): return (near, lax.ppermute(near, axis, [(i, i ^ 2) for i in range(size)]))]
    ppermute x6 -> x4, waiting for transfers between devices: 6.38 us -> 11.2 us  [the longest x2 8.89 us: halves(): return (near, lax.ppermute(near, axis, [(i, i ^ 2) for i in range(size)]))]
  transfers between devices with their start and end apart: 7 -> 5, of which waited for: 5 -> 5; matrix products, arithmetic and copies ran while one was open for 0% -> 0% of each run, Pallas kernels for 6% -> 6%
where the time goes in v11:
time: 62.6 us; the launch traced here: 62.4 us
  waiting for transfers between devices  19.5 us (31%)
  blocking collectives  15.5 us (25%)
  Pallas kernels  14.8 us (24%)
  starting transfers between devices  11.1 us (18%)
  local copies, waits for them, and re-layouts  0.73 us (1%)
  between operations  0.7 us (1%)
    all_to_all x1, blocking collectives, per_device(): hidden = lax.all_to_all(hidden, 'seq', 0, 0)  15.5 us
    all_to_all x1, starting transfers between devices, per_device(): got = lax.all_to_all(part, 'seq', 0, 0)  9.32 us
    ppermute x2, waiting for transfers between devices, halves(): return (near, lax.ppermute(near, axis, [(i, i ^ 2) for i in range(size)]))  8.89 us
    pallas_call x1, Pallas kernels, per_device(): pl.pallas_call(functools.partial(cached_kernel, group, reqs, steps, block...  8.41 us
    all_to_all x1, waiting for transfers between devices, per_device(): got = lax.all_to_all(part, 'seq', 0, 0)  8.25 us
    pallas_call x1, Pallas kernels, per_device(): pl.pallas_call(fresh_kernel, out_shape=(piece, piece, piece, jax.ShapeDty...  3.63 us
    ppermute x2, waiting for transfers between devices, halves(): near = v + lax.ppermute(v, axis, [(i, i ^ 1) for i in range(size)])  2.36 us
    pallas_call x1, Pallas kernels, per_device(): pl.pallas_call(mlp_kernel, out_shape=(rows2,) * 2, in_specs=[vmem] * 5, o...  1.94 us
  transfers between devices with their start and end apart: 5, of which 5 were waited for; matrix products, arithmetic and copies ran while one was open for 0% of the time, Pallas kernels for 6%

profile of v11, /device:TPU:4, one launch (start us, length us, event | category | flops | bytes accessed | tf_op | source)
XLA Modules:
  0.0 62.4 jit_solution(11587508499957274208)
XLA Ops:
  0.6 8.4 %cached_attention.1 = (bf16[64,3,4,128]{3,2,1,0:T(4,128)(2,1)}, bf16[128,512]{1,0:T(8,128)(2,1)S(1)}, f32[8,128]{1,0:T(8,128)S(1)}, bf16[128,2048]{1,0:T(8,128)(...) custom-call(s32[32]{0:T(128)} %len_hbm.1, bf16[32,4,2048]{2,1,0:T(4,128)(2,1)} %x_ref.1, ...), custom_call_target="tpu_custom_call" | custom-call | tf_op jit(solution)/shard_map/cached_attention/pallas_call | solution.py:282
  9.0 9.3 %all-to-all-start = ((bf16[64,3,4,128]{3,2,1,0:T(4,128)(2,1)}), bf16[64,3,4,128]{3,2,1,0:T(4,128)(2,1)S(1)}, u32[]{:S(2)}, u32[]{:S(2)}) async-start(bf16[64,3,4,128]{3,2,1,0:T(4,128)(2,1)} %get-tuple-element.17), calls=%async_computation | async-start | bytes 393216 | tf_op jit(solution)/shard_map/all_to_all | solution.py:313
  18.4 3.6 %new_tokens.1 = (bf16[32,4,512]{2,1,0:T(4,128)(2,1)}, bf16[32,4,512]{2,1,0:T(4,128)(2,1)}, bf16[32,4,512]{2,1,0:T(4,128)(2,1)}, f32[3,8,128]{2,1,0:T(8,128)S(1)}, bf16[512,2048]{1,0:T(8,128)(2,1)S(1)}) custom-call(bf16[3,2048,512]{2,1,0:T(8,128)(2,1)} %w_hbm.3, bf16[512,2048]{1,0:T(8,128)(2,1)} %proj_hbm.1, bf16[128,512]{1,0:T(8,128)(2,1)S(1)} %get-tuple-element.18.q_rows, ...), custom_call_target="tpu_custom_call" | custom-call | tf_op jit(solution)/shard_map/new_tokens/pallas_call | solution.py:316
  22.0 8.3 %all-to-all-done.got_ref = bf16[64,3,4,128]{3,2,1,0:T(4,128)(2,1)S(1)} async-done(((bf16[64,3,4,128]{3,2,1,0:T(4,128)(2,1)}), bf16[64,3,4,128]{3,2,1,0:T(4,128)(2,1)S(1)}, u32[]{:S(2)}, u32[]{:S(2)}) %all-to-all-start) | async-done | bytes 196640 | tf_op jit(solution)/shard_map/all_to_all | solution.py:313
  30.3 0.0 slice-start
  30.3 0.0 slice-start.1
  30.3 0.0 copy-start
  30.3 0.0 copy-start.1
  30.3 0.8 %merge_project.1 = f32[2,2048]{1,0:T(2,128)S(1)} custom-call(bf16[64,3,4,128]{3,2,1,0:T(4,128)(2,1)S(1)} %all-to-all-done.got_ref, f32[3,8,128]{2,1,0:T(8,128)S(1)} %get-tuple-element.23.fresh_ref, bf16[512,2048]{1,0:T(8,128)(2,1)S(1)} %get-tuple-element.24.w_ref), custom_call_target="tpu_custom_call" | custom-call | flops 10000000000 | bytes 62914560 | tf_op jit(solution)/shard_map/merge_project/pallas_call | solution.py:337
  31.1 0.0 collective-permute-start
  31.1 1.2 %collective-permute-done = f32[2,2048]{1,0:T(2,128)S(1)} collective-permute-done((f32[2,2048]{1,0:T(2,128)S(1)}, f32[2,2048]{1,0:T(2,128)S(1)}, u32[]{:S(2)}, u32[]{:S(2)}) %collective-permute-start) | collective-permute-done | bytes 16416 | tf_op jit(solution)/shard_map/ppermute | solution.py:264
  32.3 0.9 %collective-permute-start.1 = (f32[2,2048]{1,0:T(2,128)S(1)}, f32[2,2048]{1,0:T(2,128)S(1)}, u32[]{:S(2)}, u32[]{:S(2)}) collective-permute-start(f32[2,2048]{1,0:T(2,128)S(1)} %add.6.near_ref), channel_id=1, source_target_pairs={{0,2},{1,3},{2,0},{3,1},{4,6},{5,7},{6,4},{7,5},{8,10},{9,11},{10,... | collective-permute-start | bytes 49160 | tf_op jit(solution)/shard_map/ppermute | solution.py:265
  33.2 4.4 %collective-permute-done.1.far_ref = f32[2,2048]{1,0:T(2,128)S(1)} collective-permute-done((f32[2,2048]{1,0:T(2,128)S(1)}, f32[2,2048]{1,0:T(2,128)S(1)}, u32[]{:S(2)}, u32[]{:S(2)}) %collective-permute-start.1) | collective-permute-done | bytes 16416 | tf_op jit(solution)/shard_map/ppermute | solution.py:265
  37.6 0.0 slice-done
  37.6 0.0 slice-done.1
  37.6 0.0 copy-done
  37.6 0.0 copy-done.1
  37.6 1.9 %mlp.1 = (f32[2,2048]{1,0:T(2,128)S(1)}, f32[2,2048]{1,0:T(2,128)S(1)}) custom-call(bf16[32,4,2048]{2,1,0:T(4,128)(2,1)S(1)} %copy-done.1, bf16[2,2048,1024]{2,1,0:T(8,128)(2,1)S(1)} %bitcast.1, bf16[1024,2048]{1,0:T(8,128)(2,1)S(1)} %copy-done, f32[2,2048]{1,0:T(2,128)S(1)} %add.6.near_ref, f32[2,2048]{1,0:T(2,128)S(1)} %collective-permute-done.1.far_ref), custom_call_target="tpu_custom_call" | custom-call | tf_op jit(solution)/shard_map/mlp/pallas_call | solution.py:350
  39.6 0.0 collective-permute-start.2
  39.6 1.2 %collective-permute-done.2 = f32[2,2048]{1,0:T(2,128)S(1)} collective-permute-done((f32[2,2048]{1,0:T(2,128)S(1)}, f32[2,2048]{1,0:T(2,128)S(1)}, u32[]{:S(2)}, u32[]{:S(2)}) %collective-permute-start.2) | collective-permute-done | bytes 16416 | tf_op jit(solution)/shard_map/ppermute | solution.py:264
  40.8 0.9 %collective-permute-start.3 = (f32[2,2048]{1,0:T(2,128)S(1)}, f32[2,2048]{1,0:T(2,128)S(1)}, u32[]{:S(2)}, u32[]{:S(2)}) collective-permute-start(f32[2,2048]{1,0:T(2,128)S(1)} %add.7.near_ref), channel_id=1, source_target_pairs={{0,2},{1,3},{2,0},{3,1},{4,6},{5,7},{6,4},{7,5},{8,10},{9,11},{10,... | collective-permute-start | bytes 49160 | tf_op jit(solution)/shard_map/ppermute | solution.py:265
  41.7 4.4 %collective-permute-done.3.far_ref = f32[2,2048]{1,0:T(2,128)S(1)} collective-permute-done((f32[2,2048]{1,0:T(2,128)S(1)}, f32[2,2048]{1,0:T(2,128)S(1)}, u32[]{:S(2)}, u32[]{:S(2)}) %collective-permute-start.3) | collective-permute-done | bytes 16416 | tf_op jit(solution)/shard_map/ppermute | solution.py:265
  46.2 15.5 %all_to_all.10 = bf16[64,2,512]{2,1,0:T(2,128)(2,1)S(1)} all-to-all(bf16[64,2,512]{2,1,0:T(2,128)(2,1)S(1)} %last_sum.1), channel_id=1, replica_groups=mesh['seq'=64,'mp'=4] {'seq'}, dimensions={0} | all-to-all | bytes 262144 | tf_op jit(solution)/shard_map/all_to_all | solution.py:366
  61.6 0.7 %reshape.11 = bf16[32,4,512]{2,1,0:T(4,128)(2,1)} reshape(bf16[64,2,512]{2,1,0:T(2,128)(2,1)S(1)} %all_to_all.10) | data formatting | bytes 262144 | tf_op jit(solution)/shard_map/reshape | solution.py:367
  (4 shorter events, 0.1 us)
Async XLA Ops:
  9.0 21.2 %all-to-all-start = ((bf16[64,3,4,128]{3,2,1,0:T(4,128)(2,1)}), bf16[64,3,4,128]{3,2,1,0:T(4,128)(2,1)S(1)}, u32[]{:S(2)}, u32[]{:S(2)}) async-start(bf16[64,3,4,128]{3,2,1,0:T(4,128)(2,1)} %get-tuple-element.17), calls=%async_computation | async-start | bytes 393216 | tf_op jit(solution)/shard_map/all_to_all | solution.py:313
  30.3 7.3 %slice-start = ((s8[8388608]{0:T(1024)(128)(4,1)}), s8[4194304]{0:T(1024)(128)(4,1)S(1)}, s32[]{:S(2)}) async-start(s8[8388608]{0:T(1024)(128)(4,1)} %bitcast), calls=%async_computation.2 | async-start | bytes 8388608
  30.3 7.3 %slice-start.1 = ((s8[8388608]{0:T(1024)(128)(4,1)}), s8[4194304]{0:T(1024)(128)(4,1)S(1)}, s32[]{:S(2)}) async-start(s8[8388608]{0:T(1024)(128)(4,1)} %bitcast), calls=%async_computation.3 | async-start | bytes 8388608
  30.3 7.3 %copy-start = (bf16[1024,2048]{1,0:T(8,128)(2,1)S(1)}, bf16[1024,2048]{1,0:T(8,128)(2,1)}, u32[]{:S(2)}) copy-start(bf16[1024,2048]{1,0:T(8,128)(2,1)} %wd_ref.1) | copy-start | bytes 12582916
  30.3 7.3 %copy-start.1 = (bf16[32,4,2048]{2,1,0:T(4,128)(2,1)S(1)}, bf16[32,4,2048]{2,1,0:T(4,128)(2,1)}, u32[]{:S(2)}) copy-start(bf16[32,4,2048]{2,1,0:T(4,128)(2,1)} %x_ref.1) | copy-start | bytes 1572868
  31.1 1.2 %collective-permute-start = (f32[2,2048]{1,0:T(2,128)S(1)}, f32[2,2048]{1,0:T(2,128)S(1)}, u32[]{:S(2)}, u32[]{:S(2)}) collective-permute-start(f32[2,2048]{1,0:T(2,128)S(1)} %merge_project.1), channel_id=1, source_target_pairs={{0,1},{1,0},{2,3},{3,2},{4,5},{5,4},{6,7},{7,6},{8,9},{9,8},{10,11... | collective-permute-start | bytes 49160 | tf_op jit(solution)/shard_map/ppermute | solution.py:264
  32.3 5.3 %collective-permute-start.1 = (f32[2,2048]{1,0:T(2,128)S(1)}, f32[2,2048]{1,0:T(2,128)S(1)}, u32[]{:S(2)}, u32[]{:S(2)}) collective-permute-start(f32[2,2048]{1,0:T(2,128)S(1)} %add.6.near_ref), channel_id=1, source_target_pairs={{0,2},{1,3},{2,0},{3,1},{4,6},{5,7},{6,4},{7,5},{8,10},{9,11},{10,... | collective-permute-start | bytes 49160 | tf_op jit(solution)/shard_map/ppermute | solution.py:265
  39.6 1.2 %collective-permute-start.2 = (f32[2,2048]{1,0:T(2,128)S(1)}, f32[2,2048]{1,0:T(2,128)S(1)}, u32[]{:S(2)}, u32[]{:S(2)}) collective-permute-start(f32[2,2048]{1,0:T(2,128)S(1)} %get-tuple-element.26), channel_id=1, source_target_pairs={{0,1},{1,0},{2,3},{3,2},{4,5},{5,4},{6,7},{7,6},{8,9},{9,8},{10,11... | collective-permute-start | bytes 49160 | tf_op jit(solution)/shard_map/ppermute | solution.py:264
  40.8 5.3 %collective-permute-start.3 = (f32[2,2048]{1,0:T(2,128)S(1)}, f32[2,2048]{1,0:T(2,128)S(1)}, u32[]{:S(2)}, u32[]{:S(2)}) collective-permute-start(f32[2,2048]{1,0:T(2,128)S(1)} %add.7.near_ref), channel_id=1, source_target_pairs={{0,2},{1,3},{2,0},{3,1},{4,6},{5,7},{6,4},{7,5},{8,10},{9,11},{10,... | collective-permute-start | bytes 49160 | tf_op jit(solution)/shard_map/ppermute | solution.py:265

commit v12 on v11

--- a/solution.py
+++ b/solution.py
@@ -63,8 +63,13 @@
     copy_l.start()
     copy_x = pltpu.make_async_copy(x_hbm, x_v, sem_x)
     copy_x.start()
-    copy_w = pltpu.make_async_copy(w_hbm.at[0], w_v, sem_w)
-    copy_w.start()
+    depth = w_v.shape[0] // 2
+    copies_w = [
+        pltpu.make_async_copy(w_hbm.at[0, pl.ds(i * depth, depth)], w_v.at[pl.ds(i * depth, depth)], sem_w.at[i])
+        for i in range(2)
+    ]
+    for c in copies_w:
+        c.start()
 
     copy_l.wait()
     count = jnp.int32(0)
@@ -112,8 +117,10 @@
         xs[pl.ds(r * steps, steps), :] = x_v[r].astype(F32)
     normed_out[...] = norm_rows(xs[...]).astype(BF16)
 
-    copy_w.wait()
-    part = jnp.dot(normed_out[...], w_v[...], preferred_element_type=F32)
+    copies_w[0].wait()
+    part = jnp.dot(normed_out[:, :depth], w_v[:depth], preferred_element_type=F32)
+    copies_w[1].wait()
+    part = part + jnp.dot(normed_out[:, depth:], w_v[depth:], preferred_element_type=F32)
     for h in range(heads):
         q = turn(part[:, h * DH : (h + 1) * DH], cos_out[...], sin_out[...]).astype(BF16)
         q_rows[:, h * DH : (h + 1) * DH] = q
@@ -302,7 +309,7 @@
             pltpu.VMEM((rows * heads, DH), F32),
             pltpu.SemaphoreType.DMA,
             pltpu.SemaphoreType.DMA,
-            pltpu.SemaphoreType.DMA,
+            pltpu.SemaphoreType.DMA((2,)),
             pltpu.SemaphoreType.DMA((reqs,)),
             pltpu.SemaphoreType.DMA((reqs,)),
         ],

time: 62.6 us -> 62.7 us (level)
  no operation moved by 1% of the time
where the time goes in v12:
time: 62.7 us; the launch traced here: 62.5 us
  waiting for transfers between devices  19.5 us (31%)
  blocking collectives  15.5 us (25%)
  Pallas kernels  15 us (24%)
  starting transfers between devices  11.1 us (18%)
  local copies, waits for them, and re-layouts  0.73 us (1%)
  between operations  0.7 us (1%)
    all_to_all x1, blocking collectives, per_device(): hidden = lax.all_to_all(hidden, 'seq', 0, 0)  15.5 us
    all_to_all x1, starting transfers between devices, per_device(): got = lax.all_to_all(part, 'seq', 0, 0)  9.32 us
    ppermute x2, waiting for transfers between devices, halves(): return (near, lax.ppermute(near, axis, [(i, i ^ 2) for i in range(size)]))  8.89 us
    pallas_call x1, Pallas kernels, per_device(): pl.pallas_call(functools.partial(cached_kernel, group, reqs, steps, block...  8.54 us
    all_to_all x1, waiting for transfers between devices, per_device(): got = lax.all_to_all(part, 'seq', 0, 0)  8.25 us
    pallas_call x1, Pallas kernels, per_device(): pl.pallas_call(fresh_kernel, out_shape=(piece, piece, piece, jax.ShapeDty...  3.63 us
    ppermute x2, waiting for transfers between devices, halves(): near = v + lax.ppermute(v, axis, [(i, i ^ 1) for i in range(size)])  2.36 us
    pallas_call x1, Pallas kernels, per_device(): pl.pallas_call(mlp_kernel, out_shape=(rows2,) * 2, in_specs=[vmem] * 5, o...  1.94 us
  transfers between devices with their start and end apart: 5, of which 5 were waited for; matrix products, arithmetic and copies ran while one was open for 0% of the time, Pallas kernels for 6%

profile of v12, /device:TPU:4, one launch (start us, length us, event | category | flops | bytes accessed | tf_op | source)
XLA Modules:
  0.0 62.5 jit_solution(4906768296947979914)
XLA Ops:
  0.6 8.5 %cached_attention.1 = (bf16[64,3,4,128]{3,2,1,0:T(4,128)(2,1)}, bf16[128,512]{1,0:T(8,128)(2,1)S(1)}, f32[8,128]{1,0:T(8,128)S(1)}, bf16[128,2048]{1,0:T(8,128)(...) custom-call(s32[32]{0:T(128)} %len_hbm.1, bf16[32,4,2048]{2,1,0:T(4,128)(2,1)} %x_ref.1, ...), custom_call_target="tpu_custom_call" | custom-call | tf_op jit(solution)/shard_map/cached_attention/pallas_call | solution.py:289
  9.2 9.3 %all-to-all-start = ((bf16[64,3,4,128]{3,2,1,0:T(4,128)(2,1)}), bf16[64,3,4,128]{3,2,1,0:T(4,128)(2,1)S(1)}, u32[]{:S(2)}, u32[]{:S(2)}) async-start(bf16[64,3,4,128]{3,2,1,0:T(4,128)(2,1)} %get-tuple-element.17), calls=%async_computation | async-start | bytes 393216 | tf_op jit(solution)/shard_map/all_to_all | solution.py:320
  18.5 3.6 %new_tokens.1 = (bf16[32,4,512]{2,1,0:T(4,128)(2,1)}, bf16[32,4,512]{2,1,0:T(4,128)(2,1)}, bf16[32,4,512]{2,1,0:T(4,128)(2,1)}, f32[3,8,128]{2,1,0:T(8,128)S(1)}, bf16[512,2048]{1,0:T(8,128)(2,1)S(1)}) custom-call(bf16[3,2048,512]{2,1,0:T(8,128)(2,1)} %w_hbm.3, bf16[512,2048]{1,0:T(8,128)(2,1)} %proj_hbm.1, bf16[128,512]{1,0:T(8,128)(2,1)S(1)} %get-tuple-element.18.q_rows, ...), custom_call_target="tpu_custom_call" | custom-call | tf_op jit(solution)/shard_map/new_tokens/pallas_call | solution.py:323
  22.2 8.3 %all-to-all-done.got_ref = bf16[64,3,4,128]{3,2,1,0:T(4,128)(2,1)S(1)} async-done(((bf16[64,3,4,128]{3,2,1,0:T(4,128)(2,1)}), bf16[64,3,4,128]{3,2,1,0:T(4,128)(2,1)S(1)}, u32[]{:S(2)}, u32[]{:S(2)}) %all-to-all-start) | async-done | bytes 196640 | tf_op jit(solution)/shard_map/all_to_all | solution.py:320
  30.4 0.0 slice-start
  30.4 0.0 slice-start.1
  30.4 0.0 copy-start
  30.4 0.0 copy-start.1
  30.4 0.8 %merge_project.1 = f32[2,2048]{1,0:T(2,128)S(1)} custom-call(bf16[64,3,4,128]{3,2,1,0:T(4,128)(2,1)S(1)} %all-to-all-done.got_ref, f32[3,8,128]{2,1,0:T(8,128)S(1)} %get-tuple-element.23.fresh_ref, bf16[512,2048]{1,0:T(8,128)(2,1)S(1)} %get-tuple-element.24.w_ref), custom_call_target="tpu_custom_call" | custom-call | flops 10000000000 | bytes 62914560 | tf_op jit(solution)/shard_map/merge_project/pallas_call | solution.py:344
  31.2 0.0 collective-permute-start
  31.2 1.2 %collective-permute-done = f32[2,2048]{1,0:T(2,128)S(1)} collective-permute-done((f32[2,2048]{1,0:T(2,128)S(1)}, f32[2,2048]{1,0:T(2,128)S(1)}, u32[]{:S(2)}, u32[]{:S(2)}) %collective-permute-start) | collective-permute-done | bytes 16416 | tf_op jit(solution)/shard_map/ppermute | solution.py:271
  32.4 0.9 %collective-permute-start.1 = (f32[2,2048]{1,0:T(2,128)S(1)}, f32[2,2048]{1,0:T(2,128)S(1)}, u32[]{:S(2)}, u32[]{:S(2)}) collective-permute-start(f32[2,2048]{1,0:T(2,128)S(1)} %add.6.near_ref), channel_id=1, source_target_pairs={{0,2},{1,3},{2,0},{3,1},{4,6},{5,7},{6,4},{7,5},{8,10},{9,11},{10,... | collective-permute-start | bytes 49160 | tf_op jit(solution)/shard_map/ppermute | solution.py:272
  33.3 4.4 %collective-permute-done.1.far_ref = f32[2,2048]{1,0:T(2,128)S(1)} collective-permute-done((f32[2,2048]{1,0:T(2,128)S(1)}, f32[2,2048]{1,0:T(2,128)S(1)}, u32[]{:S(2)}, u32[]{:S(2)}) %collective-permute-start.1) | collective-permute-done | bytes 16416 | tf_op jit(solution)/shard_map/ppermute | solution.py:272
  37.7 0.0 slice-done
  37.7 0.0 slice-done.1
  37.8 0.0 copy-done
  37.8 0.0 copy-done.1
  37.8 1.9 %mlp.1 = (f32[2,2048]{1,0:T(2,128)S(1)}, f32[2,2048]{1,0:T(2,128)S(1)}) custom-call(bf16[32,4,2048]{2,1,0:T(4,128)(2,1)S(1)} %copy-done.1, bf16[2,2048,1024]{2,1,0:T(8,128)(2,1)S(1)} %bitcast.1, bf16[1024,2048]{1,0:T(8,128)(2,1)S(1)} %copy-done, f32[2,2048]{1,0:T(2,128)S(1)} %add.6.near_ref, f32[2,2048]{1,0:T(2,128)S(1)} %collective-permute-done.1.far_ref), custom_call_target="tpu_custom_call" | custom-call | tf_op jit(solution)/shard_map/mlp/pallas_call | solution.py:357
  39.7 0.0 collective-permute-start.2
  39.7 1.2 %collective-permute-done.2 = f32[2,2048]{1,0:T(2,128)S(1)} collective-permute-done((f32[2,2048]{1,0:T(2,128)S(1)}, f32[2,2048]{1,0:T(2,128)S(1)}, u32[]{:S(2)}, u32[]{:S(2)}) %collective-permute-start.2) | collective-permute-done | bytes 16416 | tf_op jit(solution)/shard_map/ppermute | solution.py:271
  40.9 0.9 %collective-permute-start.3 = (f32[2,2048]{1,0:T(2,128)S(1)}, f32[2,2048]{1,0:T(2,128)S(1)}, u32[]{:S(2)}, u32[]{:S(2)}) collective-permute-start(f32[2,2048]{1,0:T(2,128)S(1)} %add.7.near_ref), channel_id=1, source_target_pairs={{0,2},{1,3},{2,0},{3,1},{4,6},{5,7},{6,4},{7,5},{8,10},{9,11},{10,... | collective-permute-start | bytes 49160 | tf_op jit(solution)/shard_map/ppermute | solution.py:272
  41.8 4.4 %collective-permute-done.3.far_ref = f32[2,2048]{1,0:T(2,128)S(1)} collective-permute-done((f32[2,2048]{1,0:T(2,128)S(1)}, f32[2,2048]{1,0:T(2,128)S(1)}, u32[]{:S(2)}, u32[]{:S(2)}) %collective-permute-start.3) | collective-permute-done | bytes 16416 | tf_op jit(solution)/shard_map/ppermute | solution.py:272
  46.3 15.5 %all_to_all.10 = bf16[64,2,512]{2,1,0:T(2,128)(2,1)S(1)} all-to-all(bf16[64,2,512]{2,1,0:T(2,128)(2,1)S(1)} %last_sum.1), channel_id=1, replica_groups=mesh['seq'=64,'mp'=4] {'seq'}, dimensions={0} | all-to-all | bytes 262144 | tf_op jit(solution)/shard_map/all_to_all | solution.py:373
  61.8 0.7 %reshape.11 = bf16[32,4,512]{2,1,0:T(4,128)(2,1)} reshape(bf16[64,2,512]{2,1,0:T(2,128)(2,1)S(1)} %all_to_all.10) | data formatting | bytes 262144 | tf_op jit(solution)/shard_map/reshape | solution.py:374
  (4 shorter events, 0.1 us)
Async XLA Ops:
  9.2 21.2 %all-to-all-start = ((bf16[64,3,4,128]{3,2,1,0:T(4,128)(2,1)}), bf16[64,3,4,128]{3,2,1,0:T(4,128)(2,1)S(1)}, u32[]{:S(2)}, u32[]{:S(2)}) async-start(bf16[64,3,4,128]{3,2,1,0:T(4,128)(2,1)} %get-tuple-element.17), calls=%async_computation | async-start | bytes 393216 | tf_op jit(solution)/shard_map/all_to_all | solution.py:320
  30.4 7.3 %slice-start = ((s8[8388608]{0:T(1024)(128)(4,1)}), s8[4194304]{0:T(1024)(128)(4,1)S(1)}, s32[]{:S(2)}) async-start(s8[8388608]{0:T(1024)(128)(4,1)} %bitcast), calls=%async_computation.2 | async-start | bytes 8388608
  30.4 7.3 %slice-start.1 = ((s8[8388608]{0:T(1024)(128)(4,1)}), s8[4194304]{0:T(1024)(128)(4,1)S(1)}, s32[]{:S(2)}) async-start(s8[8388608]{0:T(1024)(128)(4,1)} %bitcast), calls=%async_computation.3 | async-start | bytes 8388608
  30.4 7.3 %copy-start = (bf16[1024,2048]{1,0:T(8,128)(2,1)S(1)}, bf16[1024,2048]{1,0:T(8,128)(2,1)}, u32[]{:S(2)}) copy-start(bf16[1024,2048]{1,0:T(8,128)(2,1)} %wd_ref.1) | copy-start | bytes 12582916
  30.4 7.3 %copy-start.1 = (bf16[32,4,2048]{2,1,0:T(4,128)(2,1)S(1)}, bf16[32,4,2048]{2,1,0:T(4,128)(2,1)}, u32[]{:S(2)}) copy-start(bf16[32,4,2048]{2,1,0:T(4,128)(2,1)} %x_ref.1) | copy-start | bytes 1572868
  31.2 1.2 %collective-permute-start = (f32[2,2048]{1,0:T(2,128)S(1)}, f32[2,2048]{1,0:T(2,128)S(1)}, u32[]{:S(2)}, u32[]{:S(2)}) collective-permute-start(f32[2,2048]{1,0:T(2,128)S(1)} %merge_project.1), channel_id=1, source_target_pairs={{0,1},{1,0},{2,3},{3,2},{4,5},{5,4},{6,7},{7,6},{8,9},{9,8},{10,11... | collective-permute-start | bytes 49160 | tf_op jit(solution)/shard_map/ppermute | solution.py:271
  32.4 5.3 %collective-permute-start.1 = (f32[2,2048]{1,0:T(2,128)S(1)}, f32[2,2048]{1,0:T(2,128)S(1)}, u32[]{:S(2)}, u32[]{:S(2)}) collective-permute-start(f32[2,2048]{1,0:T(2,128)S(1)} %add.6.near_ref), channel_id=1, source_target_pairs={{0,2},{1,3},{2,0},{3,1},{4,6},{5,7},{6,4},{7,5},{8,10},{9,11},{10,... | collective-permute-start | bytes 49160 | tf_op jit(solution)/shard_map/ppermute | solution.py:272
  39.7 1.2 %collective-permute-start.2 = (f32[2,2048]{1,0:T(2,128)S(1)}, f32[2,2048]{1,0:T(2,128)S(1)}, u32[]{:S(2)}, u32[]{:S(2)}) collective-permute-start(f32[2,2048]{1,0:T(2,128)S(1)} %get-tuple-element.26), channel_id=1, source_target_pairs={{0,1},{1,0},{2,3},{3,2},{4,5},{5,4},{6,7},{7,6},{8,9},{9,8},{10,11... | collective-permute-start | bytes 49160 | tf_op jit(solution)/shard_map/ppermute | solution.py:271
  40.9 5.3 %collective-permute-start.3 = (f32[2,2048]{1,0:T(2,128)S(1)}, f32[2,2048]{1,0:T(2,128)S(1)}, u32[]{:S(2)}, u32[]{:S(2)}) collective-permute-start(f32[2,2048]{1,0:T(2,128)S(1)} %add.7.near_ref), channel_id=1, source_target_pairs={{0,2},{1,3},{2,0},{3,1},{4,6},{5,7},{6,4},{7,5},{8,10},{9,11},{10,... | collective-permute-start | bytes 49160 | tf_op jit(solution)/shard_map/ppermute | solution.py:272
